TPU v7x, 256 devices: a whole 4x4x8 slice. The times are simulated.
256 devices in a mesh: dp: 16 (over z_lo, x), seq: 16 (over z_hi, y, core).
Axes of the slice: x: 4, y: 4, z: 8 (z_hi: 2, z_lo: 4; z = z_hi * 4 + z_lo), core: 2. Of those that a mesh axis runs over, the one named last changes fastest.
Arguments:
- frames: bfloat16 [16, 4096, 1280], P('dp', 'seq'), may hold values from -6 to 6
- live: int32 [16, 4096], P('dp', 'seq'), may hold values from 0 to 1
- norm_gain: float32 [1280], replicated, may hold values from 0.25 to 1.75
- w_qkv: bfloat16 [1280, 1920], P('dp')
- w_out: bfloat16 [640, 1280], P('dp'), may hold values from -0.25 to 0.25
- cotangent: bfloat16 [16, 4096, 1280], P('dp', 'seq'), may hold values from -6 to 6
Outputs:
- grad_frames: bfloat16 [16, 4096, 1280], P('dp', 'seq')
- grad_qkv: float32 [1280, 1920], P('dp', 'seq')
- grad_out: float32 [640, 1280], P('dp', 'seq')
All inputs are finite; a program needn't handle non-finite values.
Results may differ from a plain program's by a relative error of at most 0.0095.
Values may be sent and summed in bfloat16 or wider, within the bound.
No kernel may reach another device: no remote copies, remote signals or barrier semaphores. Data moves between devices by JAX's collectives and lax.ppermute only.
A program may use at most 64 MiB of HBM per device.

v0:
```python
import math

import jax
import jax.numpy as jnp
from jax import lax
from jax.sharding import PartitionSpec as P

HEAD_DIM = 64
WIN = 512


EPS = 1e-05
NEG = -1e30


def from_behind(value, axis, steps):
    count = lax.axis_size(axis)
    leading, last = (max(0, -steps), min(count, count - steps))
    return lax.ppermute(value, axis, [(source, source + steps) for source in range(leading, last)])


def norm_rows(values_in):
    average = jnp.mean(values_in, axis=-1, keepdims=True)
    centred = values_in - average
    inverse = lax.rsqrt(jnp.mean(centred * centred, axis=-1, keepdims=True) + EPS)
    return (centred * inverse, inverse)


def against(left, right):
    return lax.dot_general(
        left, right, (((1,), (1,)), ((), ())), preferred_element_type=jnp.float32
    )


def leading(left, right):
    return lax.dot_general(
        left, right, (((0,), (0,)), ((), ())), preferred_element_type=jnp.float32
    )


def head_terms(query_head, key_head, value_head, grad_head, allowed, query_live, score_scale):
    scores = jnp.where(allowed, against(query_head, key_head) * score_scale, NEG)
    row_peak = jnp.max(scores, axis=-1, keepdims=True)
    exponent = jnp.exp(scores - row_peak)
    probabilities = exponent / jnp.sum(exponent, axis=-1, keepdims=True)
    probs_b = probabilities.astype(jnp.bfloat16)
    mixed = jnp.dot(probs_b, value_head, preferred_element_type=jnp.float32) * query_live[:, None]
    attended = mixed.astype(jnp.bfloat16)
    row_delta = jnp.sum(grad_head.astype(jnp.float32) * attended.astype(jnp.float32), axis=1)
    grad_probs = against(grad_head, value_head)
    grad_scores = (probabilities * (grad_probs - row_delta[:, None]) * score_scale).astype(
        jnp.bfloat16
    )
    grad_query = jnp.dot(grad_scores, key_head, preferred_element_type=jnp.float32)
    grad_key = leading(grad_scores, query_head)
    grad_value = leading(probs_b, grad_head)
    return (attended, grad_query, grad_key, grad_value)


def body(frames, live, norm_gain, w_qkv, w_out, cotangent):
    length = frames.shape[1]
    n_data = lax.axis_size("dp")
    n_seq = lax.axis_size("seq")
    full_qkv, full_out = (
        lax.all_gather(w_qkv, "dp", axis=0, tiled=True),
        lax.all_gather(w_out, "dp", axis=0, tiled=True),
    )
    inner = full_out.shape[0]
    heads = inner // HEAD_DIM
    hidden = frames[0].astype(jnp.float32)
    unit_rows, inverse = norm_rows(hidden)
    normed = (unit_rows * norm_gain).astype(jnp.bfloat16)
    projected = jnp.dot(normed, full_qkv, preferred_element_type=jnp.float32).astype(jnp.bfloat16)
    query = projected[:, :inner]
    key_values = projected[:, inner:]
    live_row = live[0]
    query_live = live_row.astype(jnp.float32)
    live_mark = live_row.astype(jnp.bfloat16)
    upstream = cotangent[0]
    grad_att = (against(upstream, full_out) * query_live[:, None]).astype(jnp.bfloat16)
    neighbours = -(-WIN // length)
    offsets = list(range(neighbours, 0, -1)) + list(range(-1, -neighbours - 1, -1))
    before_pairs, before_marks, after_pairs, after_marks = ([], [], [], [])
    for offset in offsets:
        distance = abs(offset)
        row_count = min(length, WIN - (distance - 1) * length)
        if offset > 0:
            send_pairs = key_values
            send_marks = live_mark
        else:
            send_pairs = key_values
            send_marks = live_mark
        got_pairs, got_marks = from_behind((send_pairs, send_marks), "seq", offset)
        if offset > 0:
            before_pairs.append(got_pairs)
            before_marks.append(got_marks)
        else:
            after_pairs.append(got_pairs)
            after_marks.append(got_marks)
    ext_pairs = jnp.concatenate(before_pairs + [key_values] + after_pairs, axis=0)
    ext_live = jnp.concatenate(before_marks + [live_mark] + after_marks, axis=0).astype(jnp.float32)
    total_span = length + 2 * WIN
    block_rows = min(length, 512)
    key_span = block_rows + 2 * WIN
    query_pos = jnp.arange(block_rows, dtype=jnp.int32)
    key_pos = jnp.arange(key_span, dtype=jnp.int32) - WIN
    in_window = jnp.abs(query_pos[:, None] - key_pos[None, :]) <= WIN
    allowances = [in_window & (ext_live[None, :] > 0.5)]
    score_scale = 1.0 / math.sqrt(HEAD_DIM)

    def split_heads(matrix):
        return matrix.reshape(matrix.shape[0], heads, HEAD_DIM).transpose(1, 0, 2)

    def merge_heads(matrix):
        return matrix.transpose(1, 0, 2).reshape(matrix.shape[1], inner)

    def one_head(inputs):
        query_head, key_head, value_head, grad_head = inputs
        out_blocks, query_blocks = ([], [])
        key_grads = jnp.zeros((total_span, HEAD_DIM), jnp.float32)
        value_grads = jnp.zeros((total_span, HEAD_DIM), jnp.float32)
        attended, grad_query, grad_key, grad_value = head_terms(
            query_head, key_head, value_head, grad_head, allowances[0], query_live, score_scale
        )
        out_blocks.append(attended)
        query_blocks.append(grad_query)
        key_grads = key_grads.at[0:key_span].add(grad_key)
        value_grads = value_grads.at[0:key_span].add(grad_value)
        return (
            jnp.concatenate(out_blocks, axis=0),
            jnp.concatenate(query_blocks, axis=0),
            key_grads,
            value_grads,
        )

    att_heads, query_heads, key_heads, value_heads = lax.map(
        one_head,
        (
            split_heads(query),
            split_heads(ext_pairs[:, :inner]),
            split_heads(ext_pairs[:, inner:]),
            split_heads(grad_att),
        ),
    )
    attention = merge_heads(att_heads)
    grad_query = merge_heads(query_heads)
    ext_grads = jnp.concatenate([merge_heads(key_heads), merge_heads(value_heads)], axis=1)
    own_grads = ext_grads[WIN : WIN + length]
    for offset in offsets:
        distance = abs(offset)
        row_count = min(length, WIN - (distance - 1) * length)
        if offset > 0:
            first_row = WIN - distance * length + length - row_count
        else:
            first_row = WIN + length + (distance - 1) * length
        arrived = from_behind(ext_grads[first_row : first_row + row_count], "seq", -offset)
        if offset > 0:
            own_grads = own_grads.at[length - row_count :].add(arrived)
        else:
            own_grads = own_grads.at[:row_count].add(arrived)
    grad_projected = jnp.concatenate([grad_query, own_grads], axis=1).astype(jnp.bfloat16)
    grad_unit = against(grad_projected, full_qkv) * norm_gain
    through = inverse * (
        grad_unit
        - jnp.mean(grad_unit, axis=-1, keepdims=True)
        - unit_rows * jnp.mean(grad_unit * unit_rows, axis=-1, keepdims=True)
    )
    grad_rows = (upstream.astype(jnp.float32) + through).astype(jnp.bfloat16)[None]
    factor = 1.0 / math.sqrt(n_data * n_seq * length)
    term_qkv = leading(normed, grad_projected)
    term_out = leading(attention, upstream)
    part_qkv, part_out = (
        lax.psum_scatter(term_qkv, "seq", scatter_dimension=1, tiled=True),
        lax.psum_scatter(term_out, "seq", scatter_dimension=1, tiled=True),
    )
    sum_qkv, sum_out = (
        lax.psum_scatter(part_qkv, "dp", scatter_dimension=0, tiled=True),
        lax.psum_scatter(part_out, "dp", scatter_dimension=0, tiled=True),
    )
    return (grad_rows, sum_qkv * factor, sum_out * factor)


def solution(mesh):
    return jax.shard_map(
        body,
        mesh=mesh,
        in_specs=(
            P("dp", "seq", None),
            P("dp", "seq"),
            P(),
            P("dp", None),
            P("dp", None),
            P("dp", "seq", None),
        ),
        out_specs=(P("dp", "seq", None), P("dp", "seq"), P("dp", "seq")),
        check_vma=False,
    )
```

profile of v0, /device:TPU:8, one launch (start us, length us, event | category | flops | bytes accessed | tf_op | source)
XLA Modules:
  0.0 898.2 jit_solution(4358646345607529689)
XLA Ops:
  9.4 3.5 collective-permute-start.4
  12.9 1.9 collective-permute-start.5
  14.8 3.6 collective-permute-start.6
  18.5 1.9 collective-permute-start.7
  22.0 79.7 %all-gather.3.cloned.1.call-done = bf16[1280,1920]{1,0:T(8,128)(2,1)} async-done(((bf16[80,1920]{1,0:T(8,128)(2,1)}), bf16[1280,1920]{1,0:T(8,128)(2,1)}) %all-gather.3.cloned.1.call-update) | async-done | bytes 4915216 | tf_op jit(solution)/shard_map/all_gather | solution.py:65
  101.7 4.0 convolution_convert_fusion
  107.6 3.3 collective-permute-start
  111.9 1.9 collective-permute-start.1
  113.9 70.7 %all-gather.5.cloned.1.call-done = bf16[640,1280]{1,0:T(8,128)(2,1)} async-done(((bf16[40,1280]{1,0:T(8,128)(2,1)}), bf16[640,1280]{1,0:T(8,128)(2,1)}) %all-gather.5.cloned.1.call-update) | async-done | bytes 1638416 | tf_op jit(solution)/shard_map/all_gather | solution.py:66
  184.5 3.1 fusion.61
  189.5 1.9 collective-permute-start.2
  191.4 1.9 collective-permute-start.3
  199.4 5.4 collective-permute-done.2
  206.0 9.9 %collective-permute-done.3 = bf16[256,1280]{1,0:T(8,128)(2,1)} collective-permute-done((bf16[256,1280]{1,0:T(8,128)(2,1)}, bf16[256,1280]{1,0:T(8,128)(2,1)}, u32[]{:S(2)}, u32[]{:S(2)}) %collective-permute-start.3) | collective-permute-done | bytes 655392 | tf_op jit(solution)/shard_map/ppermute | solution.py:19
  217.0 2.0 fusion.73
  219.0 3.6 copy.25
  222.6 3.5 copy.26
  226.1 109.6 %while.32 = (s32[]{:T(128)}, bf16[10,256,64]{1,2,0:T(8,128)(2,1)}, bf16[10,256,64]{1,2,0:T(8,128)(2,1)}, f32[10,1280,64]{1,2,0:T(8,128)S(1)}, f32[10,1280,64]{1,...) while((s32[]{:T(128)}, bf16[10,256,64]{1,2,0:T(8,128)(2,1)}, ...), condition=%wide.region_6.7_spmd.clone, body=%wide.region_2.6_spmd.clone.sunk | while | flops 258637056 | bytes 10183041 | solution.py:136
  230.0 2.0 bitcast_dynamic-update-slice_fusion.2
  239.1 1.9 fusion.107
  241.0 2.0 bitcast_dynamic-update-slice_fusion.2
  252.0 2.0 bitcast_dynamic-update-slice_fusion.2
  261.0 1.9 fusion.107
  262.9 2.0 bitcast_dynamic-update-slice_fusion.2
  273.9 2.0 bitcast_dynamic-update-slice_fusion.2
  284.8 2.0 bitcast_dynamic-update-slice_fusion.2
  295.8 2.0 bitcast_dynamic-update-slice_fusion.2
  306.7 2.0 bitcast_dynamic-update-slice_fusion.2
  315.8 1.9 fusion.107
  317.7 2.0 bitcast_dynamic-update-slice_fusion.2
  328.7 2.0 bitcast_dynamic-update-slice_fusion.2
  335.7 3.6 fusion.63
  339.4 2.2 fusion.59
  341.6 1.9 collective-permute-start.10
  343.6 8.6 collective-permute-start.11
  352.2 1.9 collective-permute-start.8
  354.2 3.1 collective-permute-start.9
  357.3 14.8 %collective-permute-done.10 = f32[256,1280]{0,1:T(8,128)S(1)} collective-permute-done((f32[256,1280]{0,1:T(8,128)S(1)}, f32[256,1280]{0,1:T(8,128)S(1)}, u32[]{:S(2)}, u32[]{:S(2)}) %collective-permute-start.10) | collective-permute-done | bytes 1310752 | tf_op jit(solution)/shard_map/ppermute | solution.py:19
  372.1 9.2 %collective-permute-done.11 = f32[256,1280]{0,1:T(8,128)S(1)} collective-permute-done((f32[256,1280]{0,1:T(8,128)S(1)}, f32[256,1280]{0,1:T(8,128)S(1)}, u32[]{:S(2)}, u32[]{:S(2)}) %collective-permute-start.11) | collective-permute-done | bytes 1310752 | tf_op jit(solution)/shard_map/ppermute | solution.py:19
  381.4 4.1 collective-permute-done.8
  385.5 14.1 %collective-permute-done.9 = f32[256,1280]{0,1:T(8,128)S(1)} collective-permute-done((f32[256,1280]{0,1:T(8,128)S(1)}, f32[256,1280]{0,1:T(8,128)S(1)}, u32[]{:S(2)}, u32[]{:S(2)}) %collective-permute-start.9) | collective-permute-done | bytes 1310752 | tf_op jit(solution)/shard_map/ppermute | solution.py:19
  400.8 5.3 fusion.66
  406.3 88.3 %reduce-scatter.9.cloned.1.call-done = f32[640,80]{0,1:T(8,128)} async-done(((f32[640,1280]{0,1:T(8,128)}), f32[640,80]{0,1:T(8,128)}) %reduce-scatter.9.cloned.1.call-update) | async-done | bytes 204816 | tf_op jit(solution)/shard_map/reduce_scatter | solution.py:174
  495.8 153.3 %reduce-scatter.7.cloned.1.call-done = f32[1280,120]{0,1:T(8,128)} async-done(((f32[1280,1920]{0,1:T(8,128)}), f32[1280,120]{0,1:T(8,128)}) %reduce-scatter.7.cloned.1.call-update) | async-done | bytes 614416 | tf_op jit(solution)/shard_map/reduce_scatter | solution.py:173
  649.2 2.2 copy.33
  651.4 4.2 fusion.71
  657.0 146.1 %all-reduce.3.cloned.1.call-done = f32[640,80]{0,1:T(8,128)} async-done(((f32[640,80]{0,1:T(8,128)}), f32[640,80]{0,1:T(8,128)}) %all-reduce.3.cloned.1.call-update) | async-done | bytes 204816
  804.8 85.0 %reduce-scatter.11.cloned.1.call-done = f32[80,120]{1,0:T(8,128)} async-done(((f32[1280,120]{1,0:T(8,128)}), f32[80,120]{1,0:T(8,128)}) %reduce-scatter.11.cloned.1.call-update) | async-done | bytes 38416
  (149 shorter events, 107.5 us)
Async XLA Ops:
  7.2 14.5 %copy-start.1 = (bf16[1,256,1280]{2,1,0:T(8,128)(2,1)S(1)}, bf16[1,256,1280]{2,1,0:T(8,128)(2,1)}, u32[]{:S(2)}) copy-start(bf16[1,256,1280]{2,1,0:T(8,128)(2,1)} %param.32) | copy-start | bytes 1966084
  7.2 94.5 %copy-start.11 = (f32[1280]{0:T(1024)S(1)}, f32[1280]{0:T(1024)}, u32[]{:S(2)}) copy-start(f32[1280]{0:T(1024)} %param.34) | copy-start | bytes 15364
  7.2 94.5 %all-gather.3.cloned.1.call-start = ((), (), s32[]{:S(2)}) async-start(), calls=%async_computation.3 | async-start | bytes 5222400 | tf_op jit(solution)/shard_map/all_gather | solution.py:65
  7.9 176.6 %all-gather.5.cloned.1.call-start = ((), (), s32[]{:S(2)}) async-start(), calls=%async_computation.4 | async-start | bytes 1740800 | tf_op jit(solution)/shard_map/all_gather | solution.py:66
  8.7 485.8 %reduce-scatter.9.cloned.1.call-start = ((), (), s32[]{:S(2)}) async-start(), calls=%async_computation.6 | async-start | bytes 3481600 | tf_op jit(solution)/shard_map/reduce_scatter | solution.py:174
  9.4 101.6 %collective-permute-start.4 = (bf16[256]{0:T(256)(128)(2,1)S(1)}, bf16[256]{0:T(256)(128)(2,1)S(1)}, u32[]{:S(2)}, u32[]{:S(2)}) collective-permute-start(bf16[256]{0:T(256)(128)(2,1)S(1)} %convert_reduce_fusion.1), channel_id=1, source_target_pairs={{0,2},{1,3},{2,4},{3,5},{4,6},{5,7},{6,8},{7,9},{8,10},{9,11},{10,... | collective-permute-start | bytes 1544 | tf_op jit(solution)/shard_map/ppermute | solution.py:19
  12.9 98.4 %collective-permute-start.5 = (bf16[256]{0:T(256)(128)(2,1)S(1)}, bf16[256]{0:T(256)(128)(2,1)S(1)}, u32[]{:S(2)}, u32[]{:S(2)}) collective-permute-start(bf16[256]{0:T(256)(128)(2,1)S(1)} %convert_reduce_fusion.1), channel_id=1, source_target_pairs={{0,1},{1,2},{2,3},{3,4},{4,5},{5,6},{6,7},{7,8},{8,9},{9,10},{10,1... | collective-permute-start | bytes 1544 | tf_op jit(solution)/shard_map/ppermute | solution.py:19
  14.8 96.9 %collective-permute-start.6 = (bf16[256]{0:T(256)(128)(2,1)S(1)}, bf16[256]{0:T(256)(128)(2,1)S(1)}, u32[]{:S(2)}, u32[]{:S(2)}) collective-permute-start(bf16[256]{0:T(256)(128)(2,1)S(1)} %convert_reduce_fusion.1), channel_id=1, source_target_pairs={{1,0},{2,1},{3,2},{4,3},{5,4},{6,5},{7,6},{8,7},{9,8},{10,9},{11,1... | collective-permute-start | bytes 1544 | tf_op jit(solution)/shard_map/ppermute | solution.py:19
  18.5 93.4 %collective-permute-start.7 = (bf16[256]{0:T(256)(128)(2,1)S(1)}, bf16[256]{0:T(256)(128)(2,1)S(1)}, u32[]{:S(2)}, u32[]{:S(2)}) collective-permute-start(bf16[256]{0:T(256)(128)(2,1)S(1)} %convert_reduce_fusion.1), channel_id=1, source_target_pairs={{2,0},{3,1},{4,2},{5,3},{6,4},{7,5},{8,6},{9,7},{10,8},{11,9},{12,... | collective-permute-start | bytes 1544 | tf_op jit(solution)/shard_map/ppermute | solution.py:19
  105.7 1.0 copy-start.4
  106.7 4.2 copy-start.12
  107.6 89.4 %collective-permute-start = (bf16[256,1280]{1,0:T(8,128)(2,1)}, bf16[256,1280]{1,0:T(8,128)(2,1)}, u32[]{:S(2)}, u32[]{:S(2)}) collective-permute-start(bf16[256,1280]{1,0:T(8,128)(2,1)} %slice.121), channel_id=1, source_target_pairs={{0,2},{1,3},{2,4},{3,5},{4,6},{5,7},{6,8},{7,9},{8,10},{9,11},{10,... | collective-permute-start | bytes 1966088 | tf_op jit(solution)/shard_map/ppermute | solution.py:19
  111.9 86.3 %collective-permute-start.1 = (bf16[256,1280]{1,0:T(8,128)(2,1)}, bf16[256,1280]{1,0:T(8,128)(2,1)}, u32[]{:S(2)}, u32[]{:S(2)}) collective-permute-start(bf16[256,1280]{1,0:T(8,128)(2,1)} %slice.121), channel_id=1, source_target_pairs={{0,1},{1,2},{2,3},{3,4},{4,5},{5,6},{6,7},{7,8},{8,9},{9,10},{10,1... | collective-permute-start | bytes 1966088 | tf_op jit(solution)/shard_map/ppermute | solution.py:19
  189.5 15.3 %collective-permute-start.2 = (bf16[256,1280]{1,0:T(8,128)(2,1)}, bf16[256,1280]{1,0:T(8,128)(2,1)}, u32[]{:S(2)}, u32[]{:S(2)}) collective-permute-start(bf16[256,1280]{1,0:T(8,128)(2,1)} %slice.121), channel_id=1, source_target_pairs={{1,0},{2,1},{3,2},{4,3},{5,4},{6,5},{7,6},{8,7},{9,8},{10,9},{11,1... | collective-permute-start | bytes 1966088 | tf_op jit(solution)/shard_map/ppermute | solution.py:19
  191.4 24.4 %collective-permute-start.3 = (bf16[256,1280]{1,0:T(8,128)(2,1)}, bf16[256,1280]{1,0:T(8,128)(2,1)}, u32[]{:S(2)}, u32[]{:S(2)}) collective-permute-start(bf16[256,1280]{1,0:T(8,128)(2,1)} %slice.121), channel_id=1, source_target_pairs={{2,0},{3,1},{4,2},{5,3},{6,4},{7,5},{8,6},{9,7},{10,8},{11,9},{12,... | collective-permute-start | bytes 1966088 | tf_op jit(solution)/shard_map/ppermute | solution.py:19
  197.0 2.4 copy-start.5
  339.4 309.8 %reduce-scatter.7.cloned.1.call-start = ((), (), s32[]{:S(2)}) async-start(), calls=%async_computation.5 | async-start | bytes 10444800 | tf_op jit(solution)/shard_map/reduce_scatter | solution.py:173
  339.4 60.1 %copy-start = (f32[10,1280,64]{1,2,0:T(8,128)S(1)}, f32[10,1280,64]{1,2,0:T(8,128)}, u32[]{:S(2)}) copy-start(f32[10,1280,64]{1,2,0:T(8,128)} %get-tuple-element.301) | copy-start | bytes 9830404
  341.6 30.5 %collective-permute-start.10 = (f32[256,1280]{0,1:T(8,128)S(1)}, f32[256,1280]{0,1:T(8,128)S(1)}, u32[]{:S(2)}, u32[]{:S(2)}) collective-permute-start(f32[256,1280]{0,1:T(8,128)S(1)} %get-tuple-element.397), channel_id=1, source_target_pairs={{0,1},{1,2},{2,3},{3,4},{4,5},{5,6},{6,7},{7,8},{8,9},{9,10},{10,1... | collective-permute-start | bytes 3932168 | tf_op jit(solution)/shard_map/ppermute | solution.py:19
  343.6 37.8 %collective-permute-start.11 = (f32[256,1280]{0,1:T(8,128)S(1)}, f32[256,1280]{0,1:T(8,128)S(1)}, u32[]{:S(2)}, u32[]{:S(2)}) collective-permute-start(f32[256,1280]{0,1:T(8,128)S(1)} %get-tuple-element.396), channel_id=1, source_target_pairs={{0,2},{1,3},{2,4},{3,5},{4,6},{5,7},{6,8},{7,9},{8,10},{9,11},{10,... | collective-permute-start | bytes 3932168 | tf_op jit(solution)/shard_map/ppermute | solution.py:19
  352.2 33.3 %collective-permute-start.8 = (f32[256,1280]{0,1:T(8,128)S(1)}, f32[256,1280]{0,1:T(8,128)S(1)}, u32[]{:S(2)}, u32[]{:S(2)}) collective-permute-start(f32[256,1280]{0,1:T(8,128)S(1)} %get-tuple-element.394), channel_id=1, source_target_pairs={{2,0},{3,1},{4,2},{5,3},{6,4},{7,5},{8,6},{9,7},{10,8},{11,9},{12,... | collective-permute-start | bytes 3932168 | tf_op jit(solution)/shard_map/ppermute | solution.py:19
  354.1 46.7 %copy-start.2 = (bf16[1,256,1280]{2,1,0:T(8,128)(2,1)S(1)}, bf16[1,256,1280]{2,1,0:T(8,128)(2,1)}, u32[]{:S(2)}) copy-start(bf16[1,256,1280]{2,1,0:T(8,128)(2,1)} %param.32) | copy-start | bytes 1966084
  354.1 46.7 %copy-start.9 = (bf16[10,256,64]{1,2,0:T(8,128)(2,1)S(1)}, bf16[10,256,64]{1,2,0:T(8,128)(2,1)}, u32[]{:S(2)}) copy-start(bf16[10,256,64]{1,2,0:T(8,128)(2,1)} %get-tuple-element.299) | copy-start | bytes 983044
  354.2 45.4 %collective-permute-start.9 = (f32[256,1280]{0,1:T(8,128)S(1)}, f32[256,1280]{0,1:T(8,128)S(1)}, u32[]{:S(2)}, u32[]{:S(2)}) collective-permute-start(f32[256,1280]{0,1:T(8,128)S(1)} %get-tuple-element.395), channel_id=1, source_target_pairs={{1,0},{2,1},{3,2},{4,3},{5,4},{6,5},{7,6},{8,7},{9,8},{10,9},{11,1... | collective-permute-start | bytes 3932168 | tf_op jit(solution)/shard_map/ppermute | solution.py:19
  400.0 0.8 copy-start.6
  406.1 88.4 %copy-start.13 = (u32[256]{0:T(256)S(1)}, u32[256]{0:T(256)}, u32[]{:S(2)}) copy-start(u32[256]{0:T(256)} %constant.302) | copy-start | bytes 3076
  406.2 245.2 %copy-start.3 = (bf16[1,256,1280]{2,1,0:T(8,128)(2,1)S(1)}, bf16[1,256,1280]{2,1,0:T(8,128)(2,1)}, u32[]{:S(2)}) copy-start(bf16[1,256,1280]{2,1,0:T(8,128)(2,1)} %param.32) | copy-start | bytes 1966084
  406.2 245.2 %copy-start.7 = (bf16[256,1280]{0,1:T(8,128)(2,1)S(1)}, bf16[256,1280]{0,1:T(8,128)(2,1)}, u32[]{:S(2)}) copy-start(bf16[256,1280]{0,1:T(8,128)(2,1)} %copy-done.6) | copy-start | bytes 1966084
  406.2 245.2 %copy-start.10 = (bf16[10,256,64]{1,2,0:T(8,128)(2,1)S(1)}, bf16[10,256,64]{1,2,0:T(8,128)(2,1)}, u32[]{:S(2)}) copy-start(bf16[10,256,64]{1,2,0:T(8,128)(2,1)} %get-tuple-element.299) | copy-start | bytes 983044
  406.2 396.9 %all-reduce.3.cloned.1.call-start = ((), (), s32[]{:S(2)}) async-start(), calls=%async_computation.8 | async-start | bytes 409600
  494.5 395.2 %reduce-scatter.11.cloned.1.call-start = ((), (), s32[]{:S(2)}) async-start(), calls=%async_computation.7 | async-start | bytes 696320
  651.4 4.3 copy-start.8
Sparse Core Ops, SparseCore 0:
  9.8 91.8 all-gather.2
  103.5 81.0 all-gather.4
  339.5 155.0 reduce-scatter.8
  499.1 149.9 reduce-scatter.6
  651.6 151.4 all-reduce.2
  805.5 84.2 reduce-scatter.10
where the time goes:
time: 902 us; the launch traced here: 898 us
  waiting for transfers between devices  682 us (76%)
  matrix products  118 us (13%)
  starting transfers between devices  35.9 us (4%)
  local copies, waits for them, and re-layouts  27.9 us (3%)
  other arithmetic  18.6 us (2%)
  between operations  15.2 us (2%)
    unnamed x8, waiting for transfers between devices  233 us
    reduce_scatter x1, waiting for transfers between devices, body(): lax.psum_scatter(term_qkv, 'seq', scatter_dimension=1, tiled=True)  153 us
    reduce_scatter x1, waiting for transfers between devices, body(): lax.psum_scatter(term_out, 'seq', scatter_dimension=1, tiled=True)  88.3 us
    all_gather x1, waiting for transfers between devices, body(): lax.all_gather(w_qkv, 'dp', axis=0, tiled=True)  79.7 us
    all_gather x1, waiting for transfers between devices, body(): lax.all_gather(w_out, 'dp', axis=0, tiled=True)  70.7 us
    ppermute x12, waiting for transfers between devices, from_behind(): lax.ppermute(value, axis, [(source, source + steps) for source in range(l...  57.6 us
    dot_general x22, matrix products, against(): lax.dot_general(left, right, (((1,), (1,)), ((), ())), preferred_element_...  38 us
    dot_general x22, matrix products, leading(): lax.dot_general(left, right, (((0,), (0,)), ((), ())), preferred_element_...  38 us
  transfers between devices with their start and end apart: 18, of which 12 were waited for; matrix products, arithmetic and copies ran while one was open for 4% of the time, Pallas kernels for 0%

commit v1 on v0

v1 whole, which is shorter than its diff:
```python
import functools
import math

import jax
import jax.numpy as jnp
from jax import lax
from jax.experimental import pallas as pl
from jax.experimental.pallas import tpu as pltpu
from jax.sharding import Mesh, PartitionSpec as P

HEAD_DIM = 64
WIN = 512
EPS = 1e-05
NEG = -1e30

ZL, X, ZH, Y, C = 4, 4, 2, 4, 2
CHIPS_Z = ZL * ZH
BF = jnp.bfloat16
F32 = jnp.float32


def dot(left, right, cl, cr):
    return lax.dot_general(left, right, (((cl,), (cr,)), ((), ())), preferred_element_type=F32)


def swap_core(value):
    return lax.ppermute(value, "c", [(0, 1), (1, 0)])


def along_seq(value, step):
    count = ZH * Y
    pairs = [(i, i + step) for i in range(count) if 0 <= i + step < count]
    return lax.ppermute(value, ("zh", "y"), pairs)


def spread_z(value, step):
    pairs = []
    for y in range(Y):
        for half in range(ZH):
            z = y + ZL * half
            to = (z + step) % CHIPS_Z
            src = ((z % ZL) * ZH + z // ZL) * Y + y
            dst = ((to % ZL) * ZH + to // ZL) * Y + y
            pairs.append((src, dst))
    return lax.ppermute(value, ("zl", "zh", "y"), pairs)


def both(core, own, other, axis):
    first = jnp.where(core == 0, own, other)
    second = jnp.where(core == 0, other, own)
    return jnp.concatenate([first, second], axis=axis)


def norm_rows(values_in):
    average = jnp.mean(values_in, axis=-1, keepdims=True)
    centred = values_in - average
    inverse = lax.rsqrt(jnp.mean(centred * centred, axis=-1, keepdims=True) + EPS)
    return (centred * inverse, inverse)


def attention_kernel(q_ref, g_ref, own_ref, prev_ref, next_ref, bias_ref, live_ref,
                     att_ref, dq_ref, down_ref, dprev_ref, dnext_ref):
    rows = 256
    chunks_k, chunks_v = ([], [])
    for ref in (prev_ref, own_ref, next_ref):
        for half in range(2):
            cols = slice(half * rows, (half + 1) * rows)
            chunks_k.append(ref[0, :, cols])
            chunks_v.append(ref[1, :, cols])
    grads_k, grads_v = ([None] * 6, [None] * 6)
    scale = 1.0 / math.sqrt(HEAD_DIM)
    for block in range(2):
        cols = slice(block * rows, (block + 1) * rows)
        keys_t = jnp.concatenate(chunks_k[block:block + 5], axis=1)
        values_t = jnp.concatenate(chunks_v[block:block + 5], axis=1)
        query = (q_ref[:, cols].astype(F32) * scale).astype(BF)
        grad = g_ref[:, cols]
        scores = dot(keys_t.T, query, 1, 0) + bias_ref[block]
        peak = jnp.max(scores, axis=0, keepdims=True)
        exponent = jnp.exp(scores - peak)
        inverse = 1.0 / jnp.sum(exponent, axis=0, keepdims=True)
        probs = exponent * inverse
        probs_b = probs.astype(BF)
        attended = (dot(values_t, probs_b, 1, 0) * live_ref[:, cols]).astype(BF)
        att_ref[:, cols] = attended
        delta = jnp.sum(grad.astype(F32) * attended.astype(F32), axis=0, keepdims=True)
        grad_probs = dot(values_t.T, grad, 1, 0)
        grad_scores = (probs * (grad_probs - delta)).astype(BF)
        dq_ref[:, cols] = (dot(keys_t, grad_scores, 1, 0) * scale).astype(BF)
        grad_k = dot(query, grad_scores, 1, 1)
        grad_v = dot(grad, probs_b, 1, 1)
        for i in range(5):
            part = slice(i * rows, (i + 1) * rows)
            at = block + i
            grads_k[at] = grad_k[:, part] if grads_k[at] is None else grads_k[at] + grad_k[:, part]
            grads_v[at] = grad_v[:, part] if grads_v[at] is None else grads_v[at] + grad_v[:, part]
    for index, ref in enumerate((dprev_ref, down_ref, dnext_ref)):
        for half in range(2):
            cols = slice(half * rows, (half + 1) * rows)
            ref[0, :, cols] = grads_k[2 * index + half].astype(ref.dtype)
            ref[1, :, cols] = grads_v[2 * index + half].astype(ref.dtype)


def attention(query, grad, own, before, after, bias, live):
    inner, rows = query.shape
    heads = inner // HEAD_DIM
    one = pl.BlockSpec((HEAD_DIM, rows), lambda h: (h, 0))
    two = pl.BlockSpec((2, HEAD_DIM, rows), lambda h: (0, h, 0))
    pair = (2, inner, rows)
    return pl.pallas_call(
        attention_kernel,
        grid=(heads,),
        in_specs=[one, one, two, two, two,
                  pl.BlockSpec(bias.shape, lambda h: (0, 0, 0)),
                  pl.BlockSpec(live.shape, lambda h: (0, 0))],
        out_specs=[one, one, two, two, two],
        out_shape=[
            jax.ShapeDtypeStruct((inner, rows), BF),
            jax.ShapeDtypeStruct((inner, rows), BF),
            jax.ShapeDtypeStruct(pair, F32),
            jax.ShapeDtypeStruct(pair, BF),
            jax.ShapeDtypeStruct(pair, BF),
        ],
        name="attention",
    )(query, grad, own, before, after, bias, live)


def weight_kernel(rows_ref, grads_ref, out_ref):
    block = rows_ref.shape[2]
    left = rows_ref[...].reshape(ZL * block, rows_ref.shape[3])
    product = dot(left, grads_ref[...], 1, 1).astype(BF)
    for zl in range(ZL):
        for zh in range(ZH):
            for y in range(Y):
                lanes = (zh * Y + y) * 128
                out_ref[0, y, zl, zh] = product[zl * block:(zl + 1) * block, lanes:lanes + 128]


def weight_terms(rows_t, grads):
    block = rows_t.shape[0] // (ZL * X)
    count = rows_t.shape[1]
    return pl.pallas_call(
        weight_kernel,
        grid=(X,),
        in_specs=[
            pl.BlockSpec((ZL, 1, block, count), lambda x: (0, x, 0, 0)),
            pl.BlockSpec(grads.shape, lambda x: (0, 0)),
        ],
        out_specs=pl.BlockSpec((1, Y, ZL, ZH, block, 128), lambda x: (x, 0, 0, 0, 0, 0)),
        out_shape=jax.ShapeDtypeStruct((X, Y, ZL, ZH, block, 128), BF),
        name="weight_terms",
    )(rows_t.reshape(ZL, X, block, count), grads)


def to_owners_xy(blocks):
    flat = blocks.reshape((X * Y, ZL * ZH) + blocks.shape[4:])
    got = lax.all_to_all(flat, ("x", "y"), 0, 0, tiled=True)
    return jnp.sum(got.astype(F32), axis=0).astype(BF)


def body(frames, live, norm_gain, w_qkv, w_out, cotangent):
    core = lax.axis_index("c")
    is_home = lax.axis_index("zl") == lax.axis_index("y")
    length = frames.shape[1]
    model = frames.shape[2]
    half = w_qkv.shape[1] // 6
    shard = w_qkv.shape[0]
    shards = ZL * X

    mine = lax.dynamic_index_in_dim(w_qkv.reshape(shard, 3, 2, half), core, 2, keepdims=False)
    out_cols = lax.dynamic_index_in_dim(w_out.reshape(shard // 2, 2, 2 * half), core, 1, keepdims=False)
    out_cols = jnp.concatenate([out_cols[:, :half], out_cols[:, half:]], axis=0)
    payload = jnp.concatenate([mine[:, 1], mine[:, 2], mine[:, 0], out_cols], axis=1)
    moved = [spread_z(payload, step) for step in (1, -1, 2)]
    piece = jnp.where(is_home, payload, moved[0] + moved[1] + moved[2])

    def gather_xy(rows):
        spread = jnp.broadcast_to(rows[None], (shards,) + rows.shape)
        return lax.all_to_all(spread, ("y", "x"), 0, 0, tiled=True)

    upstream = cotangent[0]
    upstream_2 = both(core, upstream, swap_core(upstream), 0)
    live_own = live[0].astype(F32)[None]
    live_2 = both(core, live_own, swap_core(live_own), 1)
    live_before, live_after = along_seq(live_2, 1), along_seq(live_2, -1)
    hidden = frames[0].astype(F32)
    unit_rows, inverse = norm_rows(hidden)
    normed = (unit_rows * norm_gain).astype(BF)
    normed_2 = both(core, normed, swap_core(normed), 0)
    normed_t = normed_2.T

    span = length + 2 * WIN
    key_pos = jnp.arange(span, dtype=jnp.int32) - WIN
    query_pos = jnp.arange(length, dtype=jnp.int32)
    in_window = jnp.abs(query_pos[None, :] - key_pos[:, None]) <= WIN
    live_all = jnp.concatenate([live_before, live_2, live_after], axis=1)[0]
    bias = jnp.stack([
        jnp.where(in_window & (live_all[i * length:i * length + span, None] > 0.5), 0.0, NEG)
        for i in range(2)
    ])

    w_kv = gather_xy(piece[:, :2 * half]).reshape(model, 2 * half)
    pairs = dot(w_kv, normed_2, 0, 1).astype(BF)
    before, after = along_seq(pairs, 1), along_seq(pairs, -1)

    w_qo = gather_xy(piece[:, 2 * half:])
    w_q = w_qo[:, :, :half].reshape(model, half)
    out_part = w_qo[:, :, half:].reshape(shards, 2, shard // 2, half)
    out_part = out_part.transpose(0, 2, 1, 3).reshape(2, half, 2 * half)
    out_mine = lax.dynamic_index_in_dim(out_part, core, 0, keepdims=False)
    out_send = lax.dynamic_index_in_dim(out_part, 1 - core, 0, keepdims=False)
    w_o = both(core, out_mine, swap_core(out_send), 1)
    query = dot(w_q, normed_2, 0, 1).astype(BF)
    grad_att = (dot(w_o, upstream_2, 1, 1) * live_2).astype(BF)

    pair_shape = (2, half, 2 * length)
    attended, grad_query, grad_own, grad_before, grad_after = attention(
        query, grad_att, pairs.reshape(pair_shape), before.reshape(pair_shape),
        after.reshape(pair_shape), bias, live_2,
    )
    from_after = along_seq(grad_before, -1)
    from_before = along_seq(grad_after, 1)

    attended_all = both(core, attended, swap_core(attended), 0)
    blocks = ZH * Y
    cot_mine = lax.dynamic_index_in_dim(
        upstream_2.reshape(2 * length, blocks, 2, model // (2 * blocks)), core, 2, keepdims=False)
    cot_mine = jnp.pad(cot_mine, ((0, 0), (0, 0), (0, 128 - cot_mine.shape[2]))).reshape(2 * length, blocks * 128)
    term_out = dot(attended_all, cot_mine, 1, 0).astype(BF)
    term_out = term_out.reshape(ZL, X, -1, ZH, Y, 128).transpose(1, 4, 0, 3, 2, 5)
    sum_out = to_owners_xy(term_out)

    grad_pairs = (grad_own + from_after.astype(F32) + from_before.astype(F32)).astype(BF)
    grads = jnp.concatenate([grad_query[None], grad_pairs], axis=0)
    grads_other = swap_core(grads)
    grads_all = both(core, grads[:, None], grads_other[:, None], 1)
    grads_mine = lax.dynamic_index_in_dim(
        grads_all.reshape(blocks, 2, -1, 2 * length), core, 1, keepdims=False)
    grads_mine = jnp.pad(grads_mine, ((0, 0), (0, 128 - grads_mine.shape[1]), (0, 0)))
    term_qkv = weight_terms(normed_t, grads_mine.reshape(blocks * 128, 2 * length))

    part = dot(grad_pairs.reshape(2 * half, 2 * length), w_kv, 0, 1) + dot(grad_query, w_q, 0, 1)
    part = part.reshape(2, length, model)
    part_send = lax.dynamic_index_in_dim(part, 1 - core, 0, keepdims=False).astype(BF)
    part_mine = lax.dynamic_index_in_dim(part, core, 0, keepdims=False)
    grad_unit = (part_mine + swap_core(part_send).astype(F32)) * norm_gain

    sum_qkv = to_owners_xy(term_qkv)
    sums = jnp.concatenate([sum_qkv, sum_out], axis=1)
    sums = lax.all_to_all(sums, ("zl", "zh"), 0, 0, tiled=True)
    factor = 1.0 / math.sqrt(shards * blocks * 2 * length)
    total = jnp.sum(sums.astype(F32), axis=0) * factor

    through = inverse * (
        grad_unit
        - jnp.mean(grad_unit, axis=-1, keepdims=True)
        - unit_rows * jnp.mean(grad_unit * unit_rows, axis=-1, keepdims=True)
    )
    grad_rows = (upstream.astype(F32) + through).astype(BF)[None]
    cols = w_qkv.shape[1] // (2 * blocks)
    return (grad_rows, total[:shard, :cols], total[shard:, :model // (2 * blocks)])


def solution(mesh):
    split = Mesh(mesh.devices.reshape(ZL, X, ZH, Y, C), ("zl", "x", "zh", "y", "c"))
    dp, seq = ("zl", "x"), ("zh", "y", "c")
    return jax.shard_map(
        body,
        mesh=split,
        in_specs=(P(dp, seq, None), P(dp, seq), P(), P(dp, None), P(dp, None), P(dp, seq, None)),
        out_specs=(P(dp, seq, None), P(dp, seq), P(dp, seq)),
        check_vma=False,
    )
```

time: 902 us -> 273 us (0.30)
  waiting for transfers between devices: 682 us -> 79.9 us
  matrix products: 118 us -> 11 us
  starting transfers between devices: 35.9 us -> 89.6 us
  Pallas kernels: 0 us -> 26.1 us
  between operations: 15.2 us -> 1.12 us
    reduce_scatter x2 -> x0, waiting for transfers between devices: 242 us -> none  [the longest x1 153 us: body(): lax.psum_scatter(term_qkv, 'seq', scatter_dimension=1, tiled=True)]
    unnamed x8 -> x0, waiting for transfers between devices: 233 us -> none
    all_gather x2 -> x0, waiting for transfers between devices: 150 us -> none  [the longest x1 79.7 us: body(): lax.all_gather(w_qkv, 'dp', axis=0, tiled=True)]
    dot_general x65 -> x6, matrix products: 118 us -> 11 us  [dot(): lax.dot_general(left, right, (((cl,), (cr,)), ((), ())), preferred_elemen...]
    all_to_all x0 -> x5, starting transfers between devices: none -> 68.4 us  [the longest x2 27.2 us: to_owners_xy(): got = lax.all_to_all(flat, ('x', 'y'), 0, 0, tiled=True)]
    all_to_all x0 -> x5, waiting for transfers between devices: none -> 47.3 us  [the longest x2 31.4 us: to_owners_xy(): got = lax.all_to_all(flat, ('x', 'y'), 0, 0, tiled=True)]
    pallas_call x0 -> x2, Pallas kernels: none -> 26.1 us  [the longest x1 21 us: attention(): pl.pallas_call(attention_kernel, grid=(heads,), in_specs=[one, one, two,...]
    ppermute x12 -> x16, waiting for transfers between devices: 57.6 us -> 32.6 us  [the longest x6 22.9 us: along_seq(): return lax.ppermute(value, ('zh', 'y'), pairs)]
  transfers between devices with their start and end apart: 18 -> 21, of which waited for: 12 -> 12; matrix products, arithmetic and copies ran while one was open for 4% -> 22% of each run, Pallas kernels for 0% -> 2%
where the time goes in v1:
time: 273 us; the launch traced here: 270 us
  starting transfers between devices  89.6 us (33%)
  waiting for transfers between devices  79.9 us (29%)
  local copies, waits for them, and re-layouts  34.7 us (13%)
  other arithmetic  27.3 us (10%)
  Pallas kernels  26.1 us (10%)
  matrix products  11 us (4%)
    all_to_all x2, waiting for transfers between devices, to_owners_xy(): got = lax.all_to_all(flat, ('x', 'y'), 0, 0, tiled=True)  31.4 us
    all_to_all x2, starting transfers between devices, to_owners_xy(): got = lax.all_to_all(flat, ('x', 'y'), 0, 0, tiled=True)  27.2 us
    all_to_all x1, starting transfers between devices, body(): sums = lax.all_to_all(sums, ('zl', 'zh'), 0, 0, tiled=True)  23.9 us
    ppermute x6, waiting for transfers between devices, along_seq(): return lax.ppermute(value, ('zh', 'y'), pairs)  22.9 us
    pallas_call x1, Pallas kernels, attention(): pl.pallas_call(attention_kernel, grid=(heads,), in_specs=[one, one, two,...  21 us
    ppermute x6, starting transfers between devices, along_seq(): return lax.ppermute(value, ('zh', 'y'), pairs)  17.9 us
    all_to_all x2, starting transfers between devices, gather_xy(): return lax.all_to_all(spread, ('y', 'x'), 0, 0, tiled=True)  17.2 us
    all_to_all x2, waiting for transfers between devices, gather_xy(): return lax.all_to_all(spread, ('y', 'x'), 0, 0, tiled=True)  12.3 us
  transfers between devices with their start and end apart: 21, of which 12 were waited for; matrix products, arithmetic and copies ran while one was open for 22% of the time, Pallas kernels for 2%

profile of v1, /device:TPU:8, one launch (start us, length us, event | category | flops | bytes accessed | tf_op | source)
XLA Modules:
  0.0 269.7 jit_solution(9350308762289995579)
XLA Ops:
  1.8 1.4 reshape.224
  7.3 9.7 %collective-permute-done.1 = bf16[80,1280]{1,0:T(8,128)(2,1)S(1)} collective-permute-done((bf16[80,1280]{1,0:T(8,128)(2,1)S(1)}, bf16[80,1280]{1,0:T(8,128)(2,1)S(1)}, u32[]{:S(2)}, u32[]{:S(2)}) %collective-permute-start.1) | collective-permute-done | bytes 204832 | tf_op jit(solution)/shard_map/ppermute | solution.py:45
  18.4 10.8 %all-to-all-start = ((bf16[16,80,640]{2,1,0:T(8,128)(2,1)}), bf16[16,80,640]{2,1,0:T(8,128)(2,1)S(1)}, u32[]{:S(2)}, u32[]{:S(2)}) async-start(bf16[16,80,640]{2,1,0:T(8,128)(2,1)} %broadcast_in_dim.18), calls=%async_computation | async-start | bytes 3276800 | tf_op jit(solution)/shard_map/all_to_all | solution.py:179
  32.2 2.0 collective-permute-start.10
  34.2 3.8 %collective-permute-start.9 = (f32[1,512]{1,0:T(1,128)S(1)}, f32[1,512]{1,0:T(1,128)S(1)}, u32[]{:S(2)}, u32[]{:S(2)}) collective-permute-start(f32[1,512]{1,0:T(1,128)S(1)} %pad_maximum_fusion.8.live_ref), channel_id=1, source_target_pairs={{0,2},{2,4},{4,6},{6,8},{8,10},{10,12},{12,14},{1,3},{3,5},{5,7},{... | collective-permute-start | bytes 6152 | tf_op jit(solution)/shard_map/ppermute | solution.py:33
  38.1 1.6 collective-permute-done.10
  39.6 5.0 %collective-permute-done.9 = f32[1,512]{1,0:T(1,128)S(1)} collective-permute-done((f32[1,512]{1,0:T(1,128)S(1)}, f32[1,512]{1,0:T(1,128)S(1)}, u32[]{:S(2)}, u32[]{:S(2)}) %collective-permute-start.9) | collective-permute-done | bytes 2080 | tf_op jit(solution)/shard_map/ppermute | solution.py:33
  44.7 2.6 and_select_fusion.1
  47.3 4.1 %all-to-all-done = bf16[16,80,640]{2,1,0:T(8,128)(2,1)S(1)} async-done(((bf16[16,80,640]{2,1,0:T(8,128)(2,1)}), bf16[16,80,640]{2,1,0:T(8,128)(2,1)S(1)}, u32[]{:S(2)}, u32[]{:S(2)}) %all-to-all-start) | async-done | bytes 1638432 | tf_op jit(solution)/shard_map/all_to_all | solution.py:179
  52.7 6.5 %all-to-all-start.1 = ((bf16[16,80,640]{2,1,0:T(8,128)(2,1)}), bf16[16,80,640]{2,1,0:T(8,128)(2,1)}, u32[]{:S(2)}, u32[]{:S(2)}) async-start(bf16[16,80,640]{2,1,0:T(8,128)(2,1)} %broadcast_in_dim.19), calls=%async_computation.1 | async-start | bytes 3276800 | tf_op jit(solution)/shard_map/all_to_all | solution.py:179
  59.2 3.4 %pad_maximum_fusion.bias_ref = f32[2,1280,256]{2,1,0:T(8,128)} fusion(f32[1,1280,256]{2,1,0:T(8,128)} %get-tuple-element.46, f32[1,1280,256]{2,1,0:T(8,128)} %get-tuple-element.45), kind=kLoop, calls=%fused_computation.1 | loop fusion | flops 655360 | bytes 5242880 | tf_op jit(solution)/shard_map/stack | solution.py:197
  62.5 2.3 broadcast_select_fusion.1
  64.9 2.5 broadcast_select_fusion.3
  67.4 1.4 fusion.25
  69.6 1.6 reshape.228
  71.2 1.8 dynamic-slice_bitcast_fusion.2
  73.0 8.3 %all-to-all-done.1 = bf16[16,80,640]{2,1,0:T(8,128)(2,1)} async-done(((bf16[16,80,640]{2,1,0:T(8,128)(2,1)}), bf16[16,80,640]{2,1,0:T(8,128)(2,1)}, u32[]{:S(2)}, u32[]{:S(2)}) %all-to-all-start.1) | async-done | bytes 1638432 | tf_op jit(solution)/shard_map/all_to_all | solution.py:179
  81.3 2.7 %convolution_convert_fusion.1 = bf16[640,512]{1,0:T(8,128)(2,1)S(1)} fusion(bf16[1280,640]{1,0:T(8,128)(2,1)} %bitcast.12, bf16[256,1280]{0,1:T(8,128)(2,1)} %get-tuple-element.33, bf16[256,1280]{0,1:T(8,128)(2,1)S(1)} %copy-done.5), kind=kOutput, calls=%fused_computation.6 | convolution fusion | flops 841809920 | bytes 3604480 | tf_op jit(solution)/shard_map/dot_general | solution.py:23
  84.1 4.1 %collective-permute-start.8 = (bf16[640,512]{1,0:T(8,128)(2,1)S(1)}, bf16[640,512]{1,0:T(8,128)(2,1)S(1)}, u32[]{:S(2)}, u32[]{:S(2)}) collective-permute-start(bf16[640,512]{1,0:T(8,128)(2,1)S(1)} %convolution_convert_fusion.1), channel_id=1, source_target_pairs={{2,0},{4,2},{6,4},{8,6},{10,8},{12,10},{14,12},{3,1},{5,3},{7,5},{... | collective-permute-start | bytes 1966088 | tf_op jit(solution)/shard_map/ppermute | solution.py:33
  88.2 2.1 collective-permute-start.7
  90.3 1.4 convolution_convert_fusion.2.q_ref
  94.3 5.5 %collective-permute-done.8 = bf16[640,512]{1,0:T(8,128)(2,1)S(1)} collective-permute-done((bf16[640,512]{1,0:T(8,128)(2,1)S(1)}, bf16[640,512]{1,0:T(8,128)(2,1)S(1)}, u32[]{:S(2)}, u32[]{:S(2)}) %collective-permute-start.8) | collective-permute-done | bytes 655392 | tf_op jit(solution)/shard_map/ppermute | solution.py:33
  99.9 2.9 %collective-permute-done.7 = bf16[640,512]{1,0:T(8,128)(2,1)S(1)} collective-permute-done((bf16[640,512]{1,0:T(8,128)(2,1)S(1)}, bf16[640,512]{1,0:T(8,128)(2,1)S(1)}, u32[]{:S(2)}, u32[]{:S(2)}) %collective-permute-start.7) | collective-permute-done | bytes 655392 | tf_op jit(solution)/shard_map/ppermute | solution.py:33
  103.7 21.0 %attention.1 = (bf16[320,512]{1,0:T(8,128)(2,1)}, bf16[320,512]{1,0:T(8,128)(2,1)}, f32[2,320,512]{2,1,0:T(8,128)}, bf16[2,320,512]{2,1,0:T(8,128)(2,1)}, bf16[2,320,512]{2,1,0:T(8,128)(2,1)}) custom-call(bf16[320,512]{1,0:T(8,128)(2,1)} %convolution_convert_fusion.2.q_ref, bf16[320,512]{1,0:T(8,128)(2,1)} %fusion.14.g_ref, bf16[2,320,512]{2,1,0:T(8,128)(2,1)} %bitcast.123, ...), custom_call_target="tpu_custom_call" | custom-call | tf_op jit(solution)/shard_map/attention/pallas_call | solution.py:110
  124.7 1.9 collective-permute-start.11
  126.6 3.9 %collective-permute-start.12 = (bf16[2,320,512]{2,1,0:T(8,128)(2,1)}, bf16[2,320,512]{2,1,0:T(8,128)(2,1)S(1)}, u32[]{:S(2)}, u32[]{:S(2)}) collective-permute-start(bf16[2,320,512]{2,1,0:T(8,128)(2,1)} %get-tuple-element.10), channel_id=1, source_target_pairs={{0,2},{2,4},{4,6},{6,8},{8,10},{10,12},{12,14},{1,3},{3,5},{5,7},{... | collective-permute-start | bytes 1966088 | tf_op jit(solution)/shard_map/ppermute | solution.py:33
  132.7 5.9 %collective-permute-done.11 = bf16[2,320,512]{2,1,0:T(8,128)(2,1)S(1)} collective-permute-done((bf16[2,320,512]{2,1,0:T(8,128)(2,1)}, bf16[2,320,512]{2,1,0:T(8,128)(2,1)S(1)}, u32[]{:S(2)}, u32[]{:S(2)}) %collective-permute-start.11) | collective-permute-done | bytes 655392 | tf_op jit(solution)/shard_map/ppermute | solution.py:33
  138.7 1.9 collective-permute-done.12
  142.7 2.0 convolution_convert_fusion
  144.7 3.8 %reshape.241 = bf16[4,4,40,2,4,128]{5,4,3,2,1,0:T(4,128)(2,1)} reshape(bf16[640,1024]{1,0:T(8,128)(2,1)} %convolution_convert_fusion) | data formatting | bytes 2621440 | tf_op jit(solution)/shard_map/reshape | solution.py:230
  148.4 2.6 copy.33
  151.1 21.4 %all-to-all-start.3 = ((bf16[16,8,40,128]{3,2,1,0:T(8,128)(2,1)}), bf16[16,8,40,128]{3,2,1,0:T(8,128)(2,1)}, u32[]{:S(2)}, u32[]{:S(2)}) async-start(bf16[16,8,40,128]{3,2,1,0:T(8,128)(2,1)} %bitcast.111), calls=%async_computation.3 | async-start | bytes 2621440 | tf_op jit(solution)/shard_map/all_to_all | solution.py:157
  172.5 2.3 pad_maximum_fusion.2
  177.7 5.1 %weight_terms.1 = bf16[4,4,4,2,80,128]{5,4,3,2,1,0:T(8,128)(2,1)} custom-call(bf16[4,4,80,512]{3,2,1,0:T(8,128)(2,1)} %bitcast.112, bf16[1024,512]{1,0:T(8,128)(2,1)} %bitcast.114), custom_call_target="tpu_custom_call" | custom-call | tf_op jit(solution)/shard_map/weight_terms/pallas_call | solution.py:142
  182.8 10.1 %all-to-all-done.3 = bf16[16,8,40,128]{3,2,1,0:T(8,128)(2,1)} async-done(((bf16[16,8,40,128]{3,2,1,0:T(8,128)(2,1)}), bf16[16,8,40,128]{3,2,1,0:T(8,128)(2,1)}, u32[]{:S(2)}, u32[]{:S(2)}) %all-to-all-start.3) | async-done | bytes 1310752 | tf_op jit(solution)/shard_map/all_to_all | solution.py:157
  193.0 5.8 %all-to-all-start.2 = ((bf16[16,8,80,128]{3,2,1,0:T(8,128)(2,1)}), bf16[16,8,80,128]{3,2,1,0:T(8,128)(2,1)}, u32[]{:S(2)}, u32[]{:S(2)}) async-start(bf16[16,8,80,128]{3,2,1,0:T(8,128)(2,1)} %bitcast.107), calls=%async_computation.2 | async-start | bytes 5242880 | tf_op jit(solution)/shard_map/all_to_all | solution.py:157
  199.6 2.7 convolution_add_fusion
  202.3 1.5 copy-done
  205.0 2.5 constant_dynamic-slice_fusion.1
  207.5 1.7 copy.30
  209.2 1.5 fusion.24
  210.7 1.5 reduce_sum.74
  212.2 21.3 %all-to-all-done.2 = bf16[16,8,80,128]{3,2,1,0:T(8,128)(2,1)} async-done(((bf16[16,8,80,128]{3,2,1,0:T(8,128)(2,1)}), bf16[16,8,80,128]{3,2,1,0:T(8,128)(2,1)}, u32[]{:S(2)}, u32[]{:S(2)}) %all-to-all-start.2) | async-done | bytes 2621472 | tf_op jit(solution)/shard_map/all_to_all | solution.py:157
  233.5 2.1 reduce_sum.73
  236.3 23.9 %all-to-all-start.4 = ((bf16[8,120,128]{2,1,0:T(8,128)(2,1)}), bf16[8,120,128]{2,1,0:T(8,128)(2,1)S(1)}, u32[]{:S(2)}, u32[]{:S(2)}) async-start(bf16[8,120,128]{2,1,0:T(8,128)(2,1)} %pad_maximum_fusion.5), calls=%async_computation.4 | async-start | bytes 491520 | tf_op jit(solution)/shard_map/all_to_all | solution.py:250
  260.3 2.5 fusion.18
  262.7 2.2 copy.34
  264.9 3.5 %all-to-all-done.4 = bf16[8,120,128]{2,1,0:T(8,128)(2,1)S(1)} async-done(((bf16[8,120,128]{2,1,0:T(8,128)(2,1)}), bf16[8,120,128]{2,1,0:T(8,128)(2,1)S(1)}, u32[]{:S(2)}, u32[]{:S(2)}) %all-to-all-start.4) | async-done | bytes 245792 | tf_op jit(solution)/shard_map/all_to_all | solution.py:250
  (103 shorter events, 26.3 us)
Async XLA Ops:
  1.8 4.7 %copy-start.17 = (s32[1,256]{1,0:T(1,128)S(1)}, s32[1,256]{1,0:T(1,128)}, u32[]{:S(2)}) copy-start(s32[1,256]{1,0:T(1,128)} %param.7) | copy-start | bytes 3076
  1.8 4.8 %copy-start.13 = (bf16[1,256,1280]{2,1,0:T(8,128)(2,1)S(1)}, bf16[1,256,1280]{2,1,0:T(8,128)(2,1)}, u32[]{:S(2)}) copy-start(bf16[1,256,1280]{2,1,0:T(8,128)(2,1)} %param.6) | copy-start | bytes 1966084
  3.8 3.5 %collective-permute-start.2 = (bf16[80,1280]{1,0:T(8,128)(2,1)S(1)}, bf16[80,1280]{1,0:T(8,128)(2,1)S(1)}, u32[]{:S(2)}, u32[]{:S(2)}) collective-permute-start(bf16[80,1280]{1,0:T(8,128)(2,1)S(1)} %concatenate.35), channel_id=1, source_target_pairs={{0,128},{8,136},{66,194},{74,202},{132,12},{140,4},{198,78},{206,7... | collective-permute-start | bytes 614408 | tf_op jit(solution)/shard_map/ppermute | solution.py:45
  4.5 12.5 %collective-permute-start.1 = (bf16[80,1280]{1,0:T(8,128)(2,1)S(1)}, bf16[80,1280]{1,0:T(8,128)(2,1)S(1)}, u32[]{:S(2)}, u32[]{:S(2)}) collective-permute-start(bf16[80,1280]{1,0:T(8,128)(2,1)S(1)} %concatenate.35), channel_id=1, source_target_pairs={{0,200},{8,192},{66,2},{74,10},{132,68},{140,76},{198,134},{206,14... | collective-permute-start | bytes 614408 | tf_op jit(solution)/shard_map/ppermute | solution.py:45
  5.8 11.2 %collective-permute-start = (bf16[80,1280]{1,0:T(8,128)(2,1)S(1)}, bf16[80,1280]{1,0:T(8,128)(2,1)S(1)}, u32[]{:S(2)}, u32[]{:S(2)}) collective-permute-start(bf16[80,1280]{1,0:T(8,128)(2,1)S(1)} %concatenate.35), channel_id=1, source_target_pairs={{0,64},{8,72},{66,130},{74,138},{132,196},{140,204},{198,14},{206,... | collective-permute-start | bytes 614408 | tf_op jit(solution)/shard_map/ppermute | solution.py:45
  6.5 25.7 %collective-permute-start.6 = (f32[1,256]{1,0:T(1,128)S(1)}, f32[1,256]{1,0:T(1,128)S(1)}, u32[]{:S(2)}, u32[]{:S(2)}) collective-permute-start(f32[1,256]{1,0:T(1,128)S(1)} %convert_element_type.65), channel_id=1, source_target_pairs={{0,1},{1,0},{2,3},{3,2},{4,5},{5,4},{6,7},{7,6},{8,9},{9,8},{10,11... | collective-permute-start | bytes 3080 | tf_op jit(solution)/shard_map/ppermute | solution.py:27
  18.4 10.8 %copy-start.15 = (f32[1280]{0:T(1024)S(1)}, f32[1280]{0:T(1024)}, u32[]{:S(2)}) copy-start(f32[1280]{0:T(1024)} %param.8) | copy-start | bytes 15364
  18.4 33.0 %all-to-all-start = ((bf16[16,80,640]{2,1,0:T(8,128)(2,1)}), bf16[16,80,640]{2,1,0:T(8,128)(2,1)S(1)}, u32[]{:S(2)}, u32[]{:S(2)}) async-start(bf16[16,80,640]{2,1,0:T(8,128)(2,1)} %broadcast_in_dim.18), calls=%async_computation | async-start | bytes 3276800 | tf_op jit(solution)/shard_map/all_to_all | solution.py:179
  30.2 34.6 %collective-permute-start.3 = (bf16[256,1280]{0,1:T(8,128)(2,1)}, bf16[256,1280]{0,1:T(8,128)(2,1)}, u32[]{:S(2)}, u32[]{:S(2)}) collective-permute-start(bf16[256,1280]{0,1:T(8,128)(2,1)} %fusion.6), channel_id=1, source_target_pairs={{0,1},{1,0},{2,3},{3,2},{4,5},{5,4},{6,7},{7,6},{8,9},{9,8},{10,11... | collective-permute-start | bytes 1966088 | tf_op jit(solution)/shard_map/ppermute | solution.py:27
  31.6 31.0 %collective-permute-start.5 = (bf16[256,1280]{0,1:T(8,128)(2,1)S(1)}, bf16[256,1280]{0,1:T(8,128)(2,1)}, u32[]{:S(2)}, u32[]{:S(2)}) collective-permute-start(bf16[256,1280]{0,1:T(8,128)(2,1)S(1)} %bitcast.110), channel_id=1, source_target_pairs={{0,1},{1,0},{2,3},{3,2},{4,5},{5,4},{6,7},{7,6},{8,9},{9,8},{10,11... | collective-permute-start | bytes 1966088 | tf_op jit(solution)/shard_map/ppermute | solution.py:27
  32.2 59.6 %copy-start.16 = (f32[1,512]{1,0:T(1,128)}, f32[1,512]{1,0:T(1,128)S(1)}, u32[]{:S(2)}) copy-start(f32[1,512]{1,0:T(1,128)S(1)} %pad_maximum_fusion.8.live_ref) | copy-start | bytes 6148
  32.2 7.4 %collective-permute-start.10 = (f32[1,512]{1,0:T(1,128)S(1)}, f32[1,512]{1,0:T(1,128)S(1)}, u32[]{:S(2)}, u32[]{:S(2)}) collective-permute-start(f32[1,512]{1,0:T(1,128)S(1)} %pad_maximum_fusion.8.live_ref), channel_id=1, source_target_pairs={{2,0},{4,2},{6,4},{8,6},{10,8},{12,10},{14,12},{3,1},{5,3},{7,5},{... | collective-permute-start | bytes 6152 | tf_op jit(solution)/shard_map/ppermute | solution.py:33
  34.2 10.4 %collective-permute-start.9 = (f32[1,512]{1,0:T(1,128)S(1)}, f32[1,512]{1,0:T(1,128)S(1)}, u32[]{:S(2)}, u32[]{:S(2)}) collective-permute-start(f32[1,512]{1,0:T(1,128)S(1)} %pad_maximum_fusion.8.live_ref), channel_id=1, source_target_pairs={{0,2},{2,4},{4,6},{6,8},{8,10},{10,12},{12,14},{1,3},{3,5},{5,7},{... | collective-permute-start | bytes 6152 | tf_op jit(solution)/shard_map/ppermute | solution.py:33
  52.7 28.6 %all-to-all-start.1 = ((bf16[16,80,640]{2,1,0:T(8,128)(2,1)}), bf16[16,80,640]{2,1,0:T(8,128)(2,1)}, u32[]{:S(2)}, u32[]{:S(2)}) async-start(bf16[16,80,640]{2,1,0:T(8,128)(2,1)} %broadcast_in_dim.19), calls=%async_computation.1 | async-start | bytes 3276800 | tf_op jit(solution)/shard_map/all_to_all | solution.py:179
  69.6 11.7 %copy-start.5 = (bf16[256,1280]{0,1:T(8,128)(2,1)S(1)}, bf16[256,1280]{0,1:T(8,128)(2,1)}, u32[]{:S(2)}) copy-start(bf16[256,1280]{0,1:T(8,128)(2,1)} %get-tuple-element.32) | copy-start | bytes 1966084
  73.0 18.7 %collective-permute-start.4 = (bf16[320,640]{1,0:T(8,128)(2,1)}, bf16[320,640]{1,0:T(8,128)(2,1)S(1)}, u32[]{:S(2)}, u32[]{:S(2)}) collective-permute-start(bf16[320,640]{1,0:T(8,128)(2,1)} %dynamic-slice_bitcast_fusion.2), channel_id=1, source_target_pairs={{0,1},{1,0},{2,3},{3,2},{4,5},{5,4},{6,7},{7,6},{8,9},{9,8},{10,11... | collective-permute-start | bytes 1228808 | tf_op jit(solution)/shard_map/ppermute | solution.py:27
  81.3 9.0 %copy-start.1 = (bf16[16,80,320]{2,1,0:T(8,128)(2,1)S(1)}, bf16[16,80,320]{2,1,0:T(8,128)(2,1)}, u32[]{:S(2)}) copy-start(bf16[16,80,320]{2,1,0:T(8,128)(2,1)} %get-tuple-element.29) | copy-start | bytes 2457604
  81.3 9.0 %copy-start.6 = (bf16[256,1280]{0,1:T(8,128)(2,1)S(1)}, bf16[256,1280]{0,1:T(8,128)(2,1)}, u32[]{:S(2)}) copy-start(bf16[256,1280]{0,1:T(8,128)(2,1)} %get-tuple-element.33) | copy-start | bytes 1966084
  84.1 7.7 %copy-start.10 = (bf16[640,512]{1,0:T(8,128)(2,1)}, bf16[640,512]{1,0:T(8,128)(2,1)S(1)}, u32[]{:S(2)}) copy-start(bf16[640,512]{1,0:T(8,128)(2,1)S(1)} %convolution_convert_fusion.1) | copy-start | bytes 1966084
  84.1 15.8 %collective-permute-start.8 = (bf16[640,512]{1,0:T(8,128)(2,1)S(1)}, bf16[640,512]{1,0:T(8,128)(2,1)S(1)}, u32[]{:S(2)}, u32[]{:S(2)}) collective-permute-start(bf16[640,512]{1,0:T(8,128)(2,1)S(1)} %convolution_convert_fusion.1), channel_id=1, source_target_pairs={{2,0},{4,2},{6,4},{8,6},{10,8},{12,10},{14,12},{3,1},{5,3},{7,5},{... | collective-permute-start | bytes 1966088 | tf_op jit(solution)/shard_map/ppermute | solution.py:33
  88.2 14.6 %collective-permute-start.7 = (bf16[640,512]{1,0:T(8,128)(2,1)S(1)}, bf16[640,512]{1,0:T(8,128)(2,1)S(1)}, u32[]{:S(2)}, u32[]{:S(2)}) collective-permute-start(bf16[640,512]{1,0:T(8,128)(2,1)S(1)} %convolution_convert_fusion.1), channel_id=1, source_target_pairs={{0,2},{2,4},{4,6},{6,8},{8,10},{10,12},{12,14},{1,3},{3,5},{5,7},{... | collective-permute-start | bytes 1966088 | tf_op jit(solution)/shard_map/ppermute | solution.py:33
  90.3 1.4 copy-start.3
  91.7 1.1 copy-start.7
  91.7 1.3 copy-start.8
  99.9 2.9 %copy-start.11 = (bf16[640,512]{1,0:T(8,128)(2,1)}, bf16[640,512]{1,0:T(8,128)(2,1)S(1)}, u32[]{:S(2)}) copy-start(bf16[640,512]{1,0:T(8,128)(2,1)S(1)} %collective-permute-done.8) | copy-start | bytes 1966084
  102.8 0.9 copy-start.12
  124.7 14.0 %collective-permute-start.11 = (bf16[2,320,512]{2,1,0:T(8,128)(2,1)}, bf16[2,320,512]{2,1,0:T(8,128)(2,1)S(1)}, u32[]{:S(2)}, u32[]{:S(2)}) collective-permute-start(bf16[2,320,512]{2,1,0:T(8,128)(2,1)} %get-tuple-element.9), channel_id=1, source_target_pairs={{2,0},{4,2},{6,4},{8,6},{10,8},{12,10},{14,12},{3,1},{5,3},{7,5},{... | collective-permute-start | bytes 1966088 | tf_op jit(solution)/shard_map/ppermute | solution.py:33
  126.6 14.0 %collective-permute-start.12 = (bf16[2,320,512]{2,1,0:T(8,128)(2,1)}, bf16[2,320,512]{2,1,0:T(8,128)(2,1)S(1)}, u32[]{:S(2)}, u32[]{:S(2)}) collective-permute-start(bf16[2,320,512]{2,1,0:T(8,128)(2,1)} %get-tuple-element.10), channel_id=1, source_target_pairs={{0,2},{2,4},{4,6},{6,8},{8,10},{10,12},{12,14},{1,3},{3,5},{5,7},{... | collective-permute-start | bytes 1966088 | tf_op jit(solution)/shard_map/ppermute | solution.py:33
  131.8 1.0 copy-start.14
  131.8 8.8 %copy-start.9 = (f32[2,320,512]{2,1,0:T(8,128)S(1)}, f32[2,320,512]{2,1,0:T(8,128)}, u32[]{:S(2)}) copy-start(f32[2,320,512]{2,1,0:T(8,128)} %get-tuple-element.8) | copy-start | bytes 3932164
  132.7 9.9 %collective-permute-start.15 = (bf16[320,512]{1,0:T(8,128)(2,1)S(1)}, bf16[320,512]{1,0:T(8,128)(2,1)S(1)}, u32[]{:S(2)}, u32[]{:S(2)}) collective-permute-start(bf16[320,512]{1,0:T(8,128)(2,1)S(1)} %copy-done.14), channel_id=1, source_target_pairs={{0,1},{1,0},{2,3},{3,2},{4,5},{5,4},{6,7},{7,6},{8,9},{9,8},{10,11... | collective-permute-start | bytes 983048 | tf_op jit(solution)/shard_map/ppermute | solution.py:27
  140.6 1.0 copy-start.4
  142.6 32.2 %collective-permute-start.14 = (bf16[3,320,512]{2,1,0:T(8,128)(2,1)}, bf16[3,320,512]{2,1,0:T(8,128)(2,1)}, u32[]{:S(2)}, u32[]{:S(2)}) collective-permute-start(bf16[3,320,512]{2,1,0:T(8,128)(2,1)} %pad_maximum_fusion.4), channel_id=1, source_target_pairs={{0,1},{1,0},{2,3},{3,2},{4,5},{5,4},{6,7},{7,6},{8,9},{9,8},{10,11... | collective-permute-start | bytes 2949128 | tf_op jit(solution)/shard_map/ppermute | solution.py:27
  151.1 41.9 %all-to-all-start.3 = ((bf16[16,8,40,128]{3,2,1,0:T(8,128)(2,1)}), bf16[16,8,40,128]{3,2,1,0:T(8,128)(2,1)}, u32[]{:S(2)}, u32[]{:S(2)}) async-start(bf16[16,8,40,128]{3,2,1,0:T(8,128)(2,1)} %bitcast.111), calls=%async_computation.3 | async-start | bytes 2621440 | tf_op jit(solution)/shard_map/all_to_all | solution.py:157
  193.0 5.8 %copy-start.2 = (bf16[16,80,320]{2,1,0:T(8,128)(2,1)S(1)}, bf16[16,80,320]{2,1,0:T(8,128)(2,1)}, u32[]{:S(2)}) copy-start(bf16[16,80,320]{2,1,0:T(8,128)(2,1)} %get-tuple-element.29) | copy-start | bytes 2457604
  193.0 40.5 %all-to-all-start.2 = ((bf16[16,8,80,128]{3,2,1,0:T(8,128)(2,1)}), bf16[16,8,80,128]{3,2,1,0:T(8,128)(2,1)}, u32[]{:S(2)}, u32[]{:S(2)}) async-start(bf16[16,8,80,128]{3,2,1,0:T(8,128)(2,1)} %bitcast.107), calls=%async_computation.2 | async-start | bytes 5242880 | tf_op jit(solution)/shard_map/all_to_all | solution.py:157
  202.3 1.5 copy-start
  205.0 4.2 %collective-permute-start.13 = (bf16[256,1280]{0,1:T(8,128)(2,1)}, bf16[256,1280]{0,1:T(8,128)(2,1)}, u32[]{:S(2)}, u32[]{:S(2)}) collective-permute-start(bf16[256,1280]{0,1:T(8,128)(2,1)} %bitcast.94), channel_id=1, source_target_pairs={{0,1},{1,0},{2,3},{3,2},{4,5},{5,4},{6,7},{7,6},{8,9},{9,8},{10,11... | collective-permute-start | bytes 1966088 | tf_op jit(solution)/shard_map/ppermute | solution.py:27
  236.3 32.1 %all-to-all-start.4 = ((bf16[8,120,128]{2,1,0:T(8,128)(2,1)}), bf16[8,120,128]{2,1,0:T(8,128)(2,1)S(1)}, u32[]{:S(2)}, u32[]{:S(2)}) async-start(bf16[8,120,128]{2,1,0:T(8,128)(2,1)} %pad_maximum_fusion.5), calls=%async_computation.4 | async-start | bytes 491520 | tf_op jit(solution)/shard_map/all_to_all | solution.py:250

commit v2 on v1

v2 whole, which is shorter than its diff:
```python
import math

import jax
import jax.numpy as jnp
from jax import lax
from jax.experimental import pallas as pl
from jax.experimental.pallas import tpu as pltpu
from jax.sharding import Mesh, PartitionSpec as P

HEAD_DIM = 64
WIN = 512
EPS = 1e-05
NEG = -1e30

ZL, X, ZH, Y, C = 4, 4, 2, 4, 2
CHIPS_Z = ZL * ZH
BF = jnp.bfloat16
F32 = jnp.float32


def dot(left, right, cl, cr):
    return lax.dot_general(left, right, (((cl,), (cr,)), ((), ())), preferred_element_type=F32)


def swap_core(value):
    return lax.ppermute(value, "c", [(0, 1), (1, 0)])


def along_y(value, step):
    pairs = [(i, i + step) for i in range(Y) if 0 <= i + step < Y]
    return lax.ppermute(value, "y", pairs)


def across_y(value):
    return lax.ppermute(value, ("zh", "y"), [(Y - 1, 0), (Y, 2 * Y - 1)])


def across_z(value):
    return lax.ppermute(value, ("zh", "y"), [(0, Y), (2 * Y - 1, Y - 1)])


def across(value):
    return lax.ppermute(value, ("zh", "y"), [(Y - 1, Y), (Y, Y - 1)])


def spread_z(value, step):
    pairs = []
    for y in range(Y):
        for half in range(ZH):
            z = y + ZL * half
            to = (z + step) % CHIPS_Z
            src = ((z % ZL) * ZH + z // ZL) * Y + y
            dst = ((to % ZL) * ZH + to // ZL) * Y + y
            pairs.append((src, dst))
    return lax.ppermute(value, ("zl", "zh", "y"), pairs)


def both(core, own, other, axis):
    first = jnp.where(core == 0, own, other)
    second = jnp.where(core == 0, other, own)
    return jnp.concatenate([first, second], axis=axis)


def norm_rows(values_in):
    average = jnp.mean(values_in, axis=-1, keepdims=True)
    centred = values_in - average
    inverse = lax.rsqrt(jnp.mean(centred * centred, axis=-1, keepdims=True) + EPS)
    return (centred * inverse, inverse)


def attention_kernel(flag_ref, q_ref, g_ref, own_ref, prev_ref, next_ref, across_ref, bias_ref, live_ref,
                     att_ref, dq_ref, down_ref, dprev_ref, dnext_ref, dacross_ref):
    rows = 256
    last = flag_ref[1].astype(F32)
    first = flag_ref[2].astype(F32)
    chunks_k, chunks_v = ([], [])
    for ref, share in ((prev_ref, first), (own_ref, None), (next_ref, last)):
        for half in range(2):
            cols = slice(half * rows, (half + 1) * rows)
            for kind, chunks in ((0, chunks_k), (1, chunks_v)):
                chunk = ref[kind, :, cols]
                if share is not None:
                    chunk = (chunk.astype(F32) + across_ref[kind, :, cols].astype(F32) * share).astype(BF)
                chunks.append(chunk)
    grads_k, grads_v = ([None] * 6, [None] * 6)
    scale = 1.0 / math.sqrt(HEAD_DIM)
    for block in range(2):
        cols = slice(block * rows, (block + 1) * rows)
        keys_t = jnp.concatenate(chunks_k[block:block + 5], axis=1)
        values_t = jnp.concatenate(chunks_v[block:block + 5], axis=1)
        query = (q_ref[:, cols].astype(F32) * scale).astype(BF)
        grad = g_ref[:, cols]
        scores = dot(keys_t.T, query, 1, 0) + bias_ref[block]
        peak = jnp.max(scores, axis=0, keepdims=True)
        exponent = jnp.exp(scores - peak)
        inverse = 1.0 / jnp.sum(exponent, axis=0, keepdims=True)
        probs = exponent * inverse
        probs_b = probs.astype(BF)
        attended = (dot(values_t, probs_b, 1, 0) * live_ref[:, cols]).astype(BF)
        att_ref[:, cols] = attended
        delta = jnp.sum(grad.astype(F32) * attended.astype(F32), axis=0, keepdims=True)
        grad_probs = dot(values_t.T, grad, 1, 0)
        grad_scores = (probs * (grad_probs - delta)).astype(BF)
        dq_ref[:, cols] = (dot(keys_t, grad_scores, 1, 0) * scale).astype(BF)
        grad_k = dot(query, grad_scores, 1, 1)
        grad_v = dot(grad, probs_b, 1, 1)
        for i in range(5):
            part = slice(i * rows, (i + 1) * rows)
            at = block + i
            grads_k[at] = grad_k[:, part] if grads_k[at] is None else grads_k[at] + grad_k[:, part]
            grads_v[at] = grad_v[:, part] if grads_v[at] is None else grads_v[at] + grad_v[:, part]
    for kind, grads in ((0, grads_k), (1, grads_v)):
        for half in range(2):
            cols = slice(half * rows, (half + 1) * rows)
            dprev_ref[kind, :, cols] = grads[half].astype(BF)
            down_ref[kind, :, cols] = grads[2 + half]
            dnext_ref[kind, :, cols] = grads[4 + half].astype(BF)
            dacross_ref[kind, :, cols] = (grads[half] * first + grads[4 + half] * last).astype(BF)


SCALARS = pl.BlockSpec(memory_space=pltpu.SMEM)


def attention(flags, query, grad, own, before, after, beyond, bias, live):
    inner, rows = query.shape
    heads = inner // HEAD_DIM
    one = pl.BlockSpec((HEAD_DIM, rows), lambda h: (h, 0))
    two = pl.BlockSpec((2, HEAD_DIM, rows), lambda h: (0, h, 0))
    pair = (2, inner, rows)
    return pl.pallas_call(
        attention_kernel,
        grid=(heads,),
        in_specs=[SCALARS, one, one, two, two, two, two,
                  pl.BlockSpec(bias.shape, lambda h: (0, 0, 0)),
                  pl.BlockSpec(live.shape, lambda h: (0, 0))],
        out_specs=[one, one, two, two, two, two],
        out_shape=[
            jax.ShapeDtypeStruct((inner, rows), BF),
            jax.ShapeDtypeStruct((inner, rows), BF),
            jax.ShapeDtypeStruct(pair, F32),
            jax.ShapeDtypeStruct(pair, BF),
            jax.ShapeDtypeStruct(pair, BF),
            jax.ShapeDtypeStruct(pair, BF),
        ],
        name="attention",
    )(flags, query, grad, own, before, after, beyond, bias, live)


def turn_kernel(in_ref, out_ref):
    out_ref[...] = in_ref[...].T


def turn(value):
    rows, cols = value.shape
    step = 256
    return pl.pallas_call(
        turn_kernel,
        grid=(cols // step,),
        in_specs=[pl.BlockSpec((rows, step), lambda i: (0, i))],
        out_specs=pl.BlockSpec((step, rows), lambda i: (i, 0)),
        out_shape=jax.ShapeDtypeStruct((cols, rows), value.dtype),
        name="turn",
    )(value)


def out_grad_kernel(flag_ref, own_ref, other_ref, cot_ref, live_ref, out_ref):
    core = flag_ref[0]
    shards, rows, cols = own_ref.shape
    block = rows // 2
    total = None
    for ref, which in ((own_ref, core), (other_ref, 1 - core)):
        weights = ref[...].reshape(shards * rows, cols)
        cot = cot_ref[:, pl.ds(pl.multiple_of(which * 2 * cols, 128), 2 * cols)]
        for half in range(2):
            product = dot(weights, cot[:, half * cols:(half + 1) * cols], 1, 1)
            parts = [product[i * rows + half * block:i * rows + (half + 1) * block] for i in range(shards)]
            total = parts if total is None else [t + p for t, p in zip(total, parts)]
    out_ref[...] = (jnp.concatenate(total, axis=0) * live_ref[...]).astype(BF)


def out_grads(flags, own, other, cot, live):
    full = pl.BlockSpec(memory_space=pltpu.VMEM)
    return pl.pallas_call(
        out_grad_kernel,
        in_specs=[SCALARS, full, full, full, full],
        out_specs=full,
        out_shape=jax.ShapeDtypeStruct((own.shape[0] * own.shape[1] // 2, cot.shape[0]), BF),
        name="out_grads",
    )(flags, own, other, cot, live)


TAIL = 32


def out_kernel(flag_ref, own_ref, other_ref, cot_ref, out_ref, sum_ref):
    core = flag_ref[0]
    half = own_ref.shape[0]
    block = half // (ZL * X // 2)
    sum_ref[pl.ds(pl.multiple_of(core * half, 64), half)] = dot(own_ref[...], cot_ref[...], 1, 0)
    sum_ref[pl.ds(pl.multiple_of((1 - core) * half, 64), half)] = dot(other_ref[...], cot_ref[...], 1, 0)
    for x in range(X):
        for y in range(Y):
            tails = []
            for zl in range(ZL):
                rows = slice((zl * X + x) * block, (zl * X + x + 1) * block)
                out_ref[x, y, zl * block:(zl + 1) * block] = sum_ref[rows, y * 128:(y + 1) * 128]
                begin = Y * 128 + y * TAIL
                tails.append(sum_ref[rows, begin:begin + TAIL])
            out_ref[x, y, ZL * block:] = jnp.concatenate(tails, axis=1)


def out_terms(flags, own, other, cot):
    block = own.shape[0] // (ZL * X // 2)
    full = pl.BlockSpec(memory_space=pltpu.VMEM)
    return pl.pallas_call(
        out_kernel,
        in_specs=[SCALARS, full, full, full],
        out_specs=full,
        out_shape=jax.ShapeDtypeStruct((X, Y, (ZL + 1) * block, 128), F32),
        scratch_shapes=[pltpu.VMEM((2 * own.shape[0], cot.shape[1]), F32)],
        name="out_terms",
    )(flags, own, other, cot)


def weight_kernel(flag_ref, rows_ref, far_rows_ref, own_ref, other_ref, extra_ref, out_ref, near_ref, far_ref, sum_ref):
    block = rows_ref.shape[2]
    count = rows_ref.shape[3]
    half = own_ref.shape[1]
    cols = 3 * 2 * half // (ZH * Y * C)

    def assemble(core):
        for at in range(ZH * Y):
            near, far = ([], [])
            begin = (2 * at + core) * cols
            end = begin + cols
            while begin < end:
                kind, which, row = begin // (2 * half), begin // half % 2, begin % half
                size = min(end - begin, half - row)
                ref = own_ref if which == core else other_ref
                near.append(ref[kind].astype(F32)[row:row + size])
                if kind == 0:
                    far.append(jnp.zeros((size, count), F32))
                else:
                    far.append(ref[kind + 2].astype(F32)[row:row + size])
                begin += size
            pad = jnp.zeros((128 - cols, count), F32)
            near_ref[at * 128:(at + 1) * 128] = jnp.concatenate(near + [pad], axis=0).astype(BF)
            far_ref[at * 128:(at + 1) * 128] = jnp.concatenate(far + [pad], axis=0).astype(BF)

    start = pl.program_id(0) == 0

    @pl.when(start & (flag_ref[0] == 0))
    def _():
        assemble(0)

    @pl.when(start & (flag_ref[0] == 1))
    def _():
        assemble(1)

    sum_ref[...] = dot(rows_ref[...].reshape(ZL * block, count), near_ref[...], 1, 1)

    @pl.when(flag_ref[1] + flag_ref[2] > 0)
    def _():
        sum_ref[...] += dot(far_rows_ref[...].reshape(ZL * block, count), far_ref[...], 1, 1)

    for zl in range(ZL):
        for zh in range(ZH):
            for y in range(Y):
                lanes = (zh * Y + y) * 128
                at = (zl * ZH + zh) * block
                out_ref[0, y, at:at + block] = sum_ref[zl * block:(zl + 1) * block, lanes:lanes + 128].astype(BF)
    out_ref[0, :, ZL * ZH * block:] = extra_ref[0].astype(BF)


def weight_terms(flags, rows_t, far_rows_t, own, other, extra):
    block = rows_t.shape[0] // (ZL * X)
    count = rows_t.shape[1]
    left = pl.BlockSpec((ZL, 1, block, count), lambda x: (0, x, 0, 0))
    right = pl.BlockSpec(own.shape, lambda x: (0, 0, 0))
    lanes = ZH * Y * 128
    height = ZL * ZH * block + extra.shape[2]
    return pl.pallas_call(
        weight_kernel,
        grid=(X,),
        in_specs=[SCALARS, left, left, right, right,
                  pl.BlockSpec((1,) + extra.shape[1:], lambda x: (x, 0, 0, 0))],
        out_specs=pl.BlockSpec((1, Y, height, 128), lambda x: (x, 0, 0, 0)),
        out_shape=jax.ShapeDtypeStruct((X, Y, height, 128), BF),
        scratch_shapes=[
            pltpu.VMEM((lanes, count), BF),
            pltpu.VMEM((lanes, count), BF),
            pltpu.VMEM((ZL * block, lanes), F32),
        ],
        name="weight_terms",
    )(flags, rows_t.reshape(ZL, X, block, count), far_rows_t.reshape(ZL, X, block, count), own, other, extra)


def body(frames, live, norm_gain, w_qkv, w_out, cotangent):
    core = lax.axis_index("c")
    chip = lax.axis_index("zh") * Y + lax.axis_index("y")
    flags = jnp.stack([core, chip == Y - 1, chip == Y]).astype(jnp.int32)
    is_home = lax.axis_index("zl") == lax.axis_index("y")
    length = frames.shape[1]
    model = frames.shape[2]
    half = w_qkv.shape[1] // 6
    shard = w_qkv.shape[0]
    shards = ZL * X

    mine = lax.dynamic_index_in_dim(w_qkv.reshape(shard, 3, 2, half), core, 2, keepdims=False)
    out_cols = lax.dynamic_index_in_dim(w_out.reshape(shard // 2, 2, 2 * half), core, 1, keepdims=False)
    out_cols = jnp.concatenate([out_cols[:, :half], out_cols[:, half:]], axis=0)
    payload = jnp.concatenate([mine[:, 1], mine[:, 2], out_cols, mine[:, 0]], axis=1)
    moved = []
    for step in (1, -1, 2):
        moved.append(spread_z(payload, step))
    piece = jnp.where(is_home, payload, moved[0] + moved[1] + moved[2])

    live_own = live[0].astype(F32)[None]
    marks = jnp.pad(live_own.astype(BF), ((0, 15), (0, model - length)))
    far = across_y(jnp.concatenate([frames[0], marks], axis=0))
    far = across_z(far)
    live_2 = both(core, live_own, swap_core(live_own), 1)
    unit_rows, inverse = norm_rows(frames[0].astype(F32))
    normed = (unit_rows * norm_gain).astype(BF)
    upstream = cotangent[0]
    upstream_other = swap_core(upstream)
    upstream_2 = both(core, upstream, upstream_other, 0)
    normed_other = swap_core(normed)
    normed_2 = both(core, normed, normed_other, 0)
    normed_t = turn(normed_2)
    blocks = ZH * Y
    width = model // (2 * blocks)
    cot_mine = lax.dynamic_index_in_dim(
        upstream_2.reshape(2 * length, ZH, Y, 2, width), core, 3, keepdims=False)
    cot_mine = cot_mine.transpose(0, 2, 1, 3).reshape(2 * length, Y, ZH * width)
    cot_mine = jnp.concatenate([
        cot_mine[:, :, :128].reshape(2 * length, Y * 128),
        cot_mine[:, :, 128:].reshape(2 * length, Y * TAIL)], axis=1)

    spread = jnp.broadcast_to(piece[None], (shards,) + piece.shape)
    weights = lax.all_to_all(spread, ("y", "x"), 0, 0, tiled=True)
    w_kv = weights[:, :, :2 * half].reshape(model, 2 * half)
    pairs = dot(w_kv, normed_2, 0, 1).astype(BF)
    before = along_y(pairs, 1)
    after = along_y(pairs, -1)
    w_o = weights[:, :, 2 * half:3 * half]
    count = shards // 2
    w_o_mine = lax.dynamic_slice_in_dim(w_o, core * count, count, 0)
    w_o_other = swap_core(lax.dynamic_slice_in_dim(w_o, (1 - core) * count, count, 0))
    grad_att = out_grads(flags, w_o_mine, w_o_other, upstream_2, live_2)
    w_q = weights[:, :, 3 * half:].reshape(model, half)
    query = dot(w_q, normed_2, 0, 1).astype(BF)

    far, _ = lax.optimization_barrier((far, pairs))
    far_live = far[length:length + 1, :length].astype(F32)
    far_live = both(core, far_live, swap_core(far_live), 1)
    far = (norm_rows(far[:length].astype(F32))[0] * norm_gain).astype(BF)
    far_2 = both(core, far, swap_core(far), 0)
    beyond = dot(w_kv, far_2, 0, 1).astype(BF)

    live_before = along_y(live_2, 1) + far_live * flags[2].astype(F32)
    live_after = along_y(live_2, -1) + far_live * flags[1].astype(F32)
    span = length + 2 * WIN
    key_pos = jnp.arange(span, dtype=jnp.int32) - WIN
    query_pos = jnp.arange(length, dtype=jnp.int32)
    in_window = jnp.abs(query_pos[None, :] - key_pos[:, None]) <= WIN
    live_all = jnp.concatenate([live_before, live_2, live_after], axis=1)[0]
    bias = jnp.stack([
        jnp.where(in_window & (live_all[i * length:i * length + span, None] > 0.5), 0.0, NEG)
        for i in range(2)
    ])

    pair_shape = (2, half, 2 * length)
    attended, grad_query, grad_own, grad_before, grad_after, grad_far = attention(
        flags, query, grad_att, pairs.reshape(pair_shape), before.reshape(pair_shape),
        after.reshape(pair_shape), beyond.reshape(pair_shape), bias, live_2,
    )
    from_after = along_y(grad_before, -1)
    from_before = along_y(grad_after, 1)
    from_far = across(grad_far)

    attended_other = swap_core(attended)
    term_out = out_terms(flags, attended, attended_other, cot_mine)
    far_2, _ = lax.optimization_barrier((far_2, grad_own))
    far_t = turn(far_2)
    grad_own, term_out, far_t = lax.optimization_barrier((grad_own, term_out, far_t))

    grad_pairs = (grad_own + from_after.astype(F32) + from_before.astype(F32)).astype(BF)
    grads = jnp.concatenate([grad_query[None], grad_pairs, grad_far], axis=0)
    grads_other = swap_core(grads)
    terms = weight_terms(flags, normed_t, far_t, grads, grads_other, term_out)
    grad_pairs, terms = lax.optimization_barrier((grad_pairs, terms))
    got = lax.all_to_all(terms.reshape((X * Y,) + terms.shape[2:]), ("x", "y"), 0, 0, tiled=True)

    grad_pairs = (grad_pairs.astype(F32) + from_far.astype(F32)).astype(BF).reshape(2 * half, 2 * length)
    part = dot(grad_pairs, w_kv, 0, 1) + dot(grad_query, w_q, 0, 1)
    part = part.reshape(2, length, model)
    part_send = lax.dynamic_index_in_dim(part, 1 - core, 0, keepdims=False).astype(BF)
    part_mine = lax.dynamic_index_in_dim(part, core, 0, keepdims=False)
    grad_unit = (part_mine + swap_core(part_send).astype(F32)) * norm_gain

    sums = jnp.sum(got.astype(F32), axis=0).astype(BF)
    owners = ZL * ZH
    block = shard // 2
    sum_qkv = sums[:owners * shard].reshape(owners, shard, 128)
    sum_out = sums[owners * shard:]
    tails = sum_out[ZL * block:].reshape(block, ZL, TAIL).transpose(1, 0, 2)
    sum_out = jnp.concatenate([sum_out[:ZL * block].reshape(ZL, block, 128), tails], axis=2)
    sum_out = sum_out.reshape(ZL, block, ZH, width).transpose(0, 2, 1, 3).reshape(owners, block, width)
    sum_out = jnp.pad(sum_out, ((0, 0), (0, 0), (0, 128 - width)))
    sums = jnp.concatenate([sum_qkv, sum_out], axis=1)
    sums = lax.all_to_all(sums, ("zl", "zh"), 0, 0, tiled=True)
    factor = 1.0 / math.sqrt(shards * blocks * 2 * length)
    total = jnp.sum(sums.astype(F32), axis=0) * factor

    through = inverse * (
        grad_unit
        - jnp.mean(grad_unit, axis=-1, keepdims=True)
        - unit_rows * jnp.mean(grad_unit * unit_rows, axis=-1, keepdims=True)
    )
    grad_rows = (upstream.astype(F32) + through).astype(BF)[None]
    cols = w_qkv.shape[1] // (2 * blocks)
    return (grad_rows, total[:shard, :cols], total[shard:, :model // (2 * blocks)])


def solution(mesh):
    split = Mesh(mesh.devices.reshape(ZL, X, ZH, Y, C), ("zl", "x", "zh", "y", "c"))
    dp, seq = ("zl", "x"), ("zh", "y", "c")
    return jax.shard_map(
        body,
        mesh=split,
        in_specs=(P(dp, seq, None), P(dp, seq), P(), P(dp, None), P(dp, None), P(dp, seq, None)),
        out_specs=(P(dp, seq, None), P(dp, seq), P(dp, seq)),
        check_vma=False,
    )
```

time: 273 us -> 289 us (1.059)
  the two profiles are of different devices: /device:TPU:8 before, /device:TPU:63 now
where the time goes in v2:
time: 289 us; the launch traced here: 288 us
  waiting for transfers between devices  132 us (46%)
  starting transfers between devices  60 us (21%)
  Pallas kernels  45.7 us (16%)
  other arithmetic  25.4 us (9%)
  local copies, waits for them, and re-layouts  15.9 us (6%)
  matrix products  7.51 us (3%)
    ppermute x1, waiting for transfers between devices, across(): return lax.ppermute(value, ('zh', 'y'), [(Y - 1, Y), (Y, Y - 1)])  38.6 us
    ppermute x1, waiting for transfers between devices, across_y(): return lax.ppermute(value, ('zh', 'y'), [(Y - 1, 0), (Y, 2 * Y - 1)])  36.2 us
    ppermute x1, waiting for transfers between devices, across_z(): return lax.ppermute(value, ('zh', 'y'), [(0, Y), (2 * Y - 1, Y - 1)])  31 us
    pallas_call x1, Pallas kernels, attention(): pl.pallas_call(attention_kernel, grid=(heads,), in_specs=[SCALARS, one, o...  21.3 us
    ppermute x6, starting transfers between devices, along_y(): return lax.ppermute(value, 'y', pairs)  14.9 us
    all_to_all x1, starting transfers between devices, body(): sums = lax.all_to_all(sums, ('zl', 'zh'), 0, 0, tiled=True)  13.6 us
    ppermute x3, waiting for transfers between devices, spread_z(): return lax.ppermute(value, ('zl', 'zh', 'y'), pairs)  12.4 us
    ppermute x9, starting transfers between devices, swap_core(): return lax.ppermute(value, 'c', [(0, 1), (1, 0)])  8.76 us
  transfers between devices with their start and end apart: 24, of which 8 were waited for; matrix products, arithmetic and copies ran while one was open for 11% of the time, Pallas kernels for 6%

profile of v2, /device:TPU:63, one launch (start us, length us, event | category | flops | bytes accessed | tf_op | source)
XLA Modules:
  0.0 288.2 jit_solution(16159470753292629130)
XLA Ops:
  1.8 1.4 reshape.296
  5.2 1.3 collective-permute-start.2
  7.0 12.4 %collective-permute-done.2 = bf16[80,1280]{1,0:T(8,128)(2,1)S(1)} collective-permute-done((bf16[80,1280]{1,0:T(8,128)(2,1)S(1)}, bf16[80,1280]{1,0:T(8,128)(2,1)S(1)}, u32[]{:S(2)}, u32[]{:S(2)}) %collective-permute-start.2) | collective-permute-done | bytes 204832 | tf_op jit(solution)/shard_map/ppermute | solution.py:55
  19.4 2.0 broadcast_in_dim.14
  21.4 6.5 %all-to-all-start = ((bf16[16,80,1280]{2,1,0:T(8,128)(2,1)}), bf16[16,80,1280]{2,1,0:T(8,128)(2,1)}, u32[]{:S(2)}, u32[]{:S(2)}) async-start(bf16[16,80,1280]{2,1,0:T(8,128)(2,1)} %broadcast_in_dim.14), calls=%async_computation | async-start | bytes 6553600 | tf_op jit(solution)/shard_map/all_to_all | solution.py:341
  28.2 1.9 collective-permute-start.3
  30.1 3.0 %collective-permute-start.9 = (bf16[272,1280]{1,0:T(8,128)(2,1)S(1)}, bf16[272,1280]{1,0:T(8,128)(2,1)}, u32[]{:S(2)}, u32[]{:S(2)}) collective-permute-start(bf16[272,1280]{1,0:T(8,128)(2,1)S(1)} %fusion.19), channel_id=1, source_target_pairs={{6,0},{8,14},{7,1},{9,15},{22,16},{24,30},{23,17},{25,31},{38,32},... | collective-permute-start | bytes 2088968 | tf_op jit(solution)/shard_map/ppermute | solution.py:35
  34.6 1.3 collective-permute-start.12
  35.9 4.0 %collective-permute-start.14 = (f32[1,512]{1,0:T(1,128)S(1)}, f32[1,512]{1,0:T(1,128)S(1)}, u32[]{:S(2)}, u32[]{:S(2)}) collective-permute-start(f32[1,512]{1,0:T(1,128)S(1)} %pad_maximum_fusion.9.live_ref), channel_id=1, source_target_pairs={{2,0},{4,2},{6,4},{3,1},{5,3},{7,5},{10,8},{12,10},{14,12},{11,9},... | collective-permute-start | bytes 6152 | tf_op jit(solution)/shard_map/ppermute | solution.py:31
  39.9 1.5 broadcast_select_fusion.5
  41.4 36.2 %collective-permute-done.9 = bf16[272,1280]{1,0:T(8,128)(2,1)} collective-permute-done((bf16[272,1280]{1,0:T(8,128)(2,1)S(1)}, bf16[272,1280]{1,0:T(8,128)(2,1)}, u32[]{:S(2)}, u32[]{:S(2)}) %collective-permute-start.9) | collective-permute-done | bytes 696352 | tf_op jit(solution)/shard_map/ppermute | solution.py:35
  77.6 1.3 collective-permute-start.10
  78.9 1.2 broadcast_select_fusion.3
  80.1 1.2 pad_maximum_fusion.3.cot_ref
  81.3 1.7 slice.97
  83.1 1.9 convolution_convert_fusion.1
  85.0 31.0 %collective-permute-done.10 = bf16[272,1280]{1,0:T(8,128)(2,1)S(1)} collective-permute-done((bf16[272,1280]{1,0:T(8,128)(2,1)}, bf16[272,1280]{1,0:T(8,128)(2,1)S(1)}, u32[]{:S(2)}, u32[]{:S(2)}) %collective-permute-start.10) | collective-permute-done | bytes 696352 | tf_op jit(solution)/shard_map/ppermute | solution.py:39
  116.2 1.3 collective-permute-start.7
  117.5 4.9 %collective-permute-start.8 = (bf16[640,512]{1,0:T(8,128)(2,1)}, bf16[640,512]{1,0:T(8,128)(2,1)}, u32[]{:S(2)}, u32[]{:S(2)}) collective-permute-start(bf16[640,512]{1,0:T(8,128)(2,1)} %convolution_convert_fusion.1), channel_id=1, source_target_pairs={{2,0},{4,2},{6,4},{3,1},{5,3},{7,5},{10,8},{12,10},{14,12},{11,9},... | collective-permute-start | bytes 1966088 | tf_op jit(solution)/shard_map/ppermute | solution.py:31
  124.9 2.0 fusion.26
  126.9 1.5 convolution_convert_fusion.2.q_ref
  130.7 1.8 pad_maximum_fusion.bias_ref
  133.3 4.0 %out_grads.1.g_ref = bf16[320,512]{1,0:T(8,128)(2,1)} custom-call(s32[3]{0:T(128)} %pad_add_fusion.flag_ref, bf16[8,80,320]{2,1,0:T(8,128)(2,1)} %get-tuple-element.42.own_ref, bf16[8,80,320]{2,1,0:T(8,128)(2,1)} %copy-done.21, bf16[512,1280]{1,0:T(8,128)(2,1)} %pad_maximum_fusion.3.cot_ref, f32[1,512]{1,0:T(1,128)} %copy-done.27), custom_call_target="tpu_custom_call" | custom-call | tf_op jit(solution)/shard_map/out_grads/pallas_call | solution.py:183
  137.2 1.5 broadcast_select_fusion.1
  138.8 1.9 convolution_convert_fusion
  140.8 21.3 %attention.1 = (bf16[320,512]{1,0:T(8,128)(2,1)}, bf16[320,512]{1,0:T(8,128)(2,1)}, f32[2,320,512]{2,1,0:T(8,128)}, bf16[2,320,512]{2,1,0:T(8,128)(2,1)}, bf16[2...) custom-call(s32[3]{0:T(128)} %pad_add_fusion.flag_ref, bf16[320,512]{1,0:T(8,128)(2,1)} %convolution_convert_fusion.2.q_ref, ...), custom_call_target="tpu_custom_call" | custom-call | tf_op jit(solution)/shard_map/attention/pallas_call | solution.py:130
  162.1 2.1 collective-permute-start.16
  164.2 1.3 collective-permute-start.17
  168.3 1.1 pad_maximum_fusion.4.in_ref
  169.5 4.2 %turn.2 = bf16[1280,512]{1,0:T(8,128)(2,1)} custom-call(bf16[512,1280]{1,0:T(8,128)(2,1)} %pad_maximum_fusion.4.in_ref), custom_call_target="tpu_custom_call" | custom-call | tf_op jit(solution)/shard_map/turn/pallas_call | solution.py:156
  174.5 3.5 %out_terms.1.extra_ref = f32[4,4,200,128]{3,2,1,0:T(8,128)} custom-call(s32[3]{0:T(128)} %pad_add_fusion.flag_ref, bf16[320,512]{1,0:T(8,128)(2,1)} %get-tuple-element.18.own_ref, bf16[320,512]{1,0:T(8,128)(2,1)} %copy-done.23, bf16[512,640]{1,0:T(8,128)(2,1)} %pad_maximum_fusion.5.cot_ref), custom_call_target="tpu_custom_call" | custom-call | tf_op jit(solution)/shard_map/out_terms/pallas_call | solution.py:215
  178.0 4.6 %collective-permute-done.17 = bf16[2,320,512]{2,1,0:T(8,128)(2,1)} collective-permute-done((bf16[2,320,512]{2,1,0:T(8,128)(2,1)}, bf16[2,320,512]{2,1,0:T(8,128)(2,1)}, u32[]{:S(2)}, u32[]{:S(2)}) %collective-permute-start.17) | collective-permute-done | bytes 655392 | tf_op jit(solution)/shard_map/ppermute | solution.py:31
  182.6 1.6 add_convert_fusion.1
  185.9 1.2 pad_maximum_fusion.2.in_ref
  187.1 4.2 %turn.3 = bf16[1280,512]{1,0:T(8,128)(2,1)} custom-call(bf16[512,1280]{1,0:T(8,128)(2,1)} %pad_maximum_fusion.2.in_ref), custom_call_target="tpu_custom_call" | custom-call | tf_op jit(solution)/shard_map/turn/pallas_call | solution.py:156
  191.3 8.5 %weight_terms.1 = bf16[4,4,840,128]{3,2,1,0:T(8,128)(2,1)} custom-call(s32[3]{0:T(128)} %pad_add_fusion.flag_ref, bf16[4,4,80,512]{3,2,1,0:T(8,128)(2,1)} %bitcast.82, bf16[4,4,80,512]{3,2,1,0:T(8,128)(2,1)} %bitcast.81, bf16[5,320,512]{2,1,0:T(8,128)(2,1)} %copy-done.4, bf16[5,320,512]{2,1,0:T(8,128)(2,1)} %collective-permute-done.18.other_ref, ...), custom_call_target="tpu_custom_call" | custom-call | tf_op jit(solution)/shard_map/weight_terms/pallas_call | solution.py:282
  199.8 7.4 %all-to-all-start.1 = ((bf16[16,840,128]{2,1,0:T(8,128)(2,1)}), bf16[16,840,128]{2,1,0:T(8,128)(2,1)}, u32[]{:S(2)}, u32[]{:S(2)}) async-start(bf16[16,840,128]{2,1,0:T(8,128)(2,1)} %bitcast.74), calls=%async_computation.1 | async-start | bytes 6881280 | tf_op jit(solution)/shard_map/all_to_all | solution.py:393
  207.2 1.9 collective-permute-start.19
  210.1 38.6 %collective-permute-done.19 = bf16[2,320,512]{2,1,0:T(8,128)(2,1)} collective-permute-done((bf16[2,320,512]{2,1,0:T(8,128)(2,1)S(1)}, bf16[2,320,512]{2,1,0:T(8,128)(2,1)}, u32[]{:S(2)}, u32[]{:S(2)}) %collective-permute-start.19) | collective-permute-done | bytes 655392 | tf_op jit(solution)/shard_map/ppermute | solution.py:43
  248.7 1.3 add_convert_fusion
  250.0 1.2 convolution_add_fusion
  251.3 3.4 %collective-permute-start.20 = (bf16[256,1280]{1,0:T(8,128)(2,1)S(1)}, bf16[256,1280]{1,0:T(8,128)(2,1)S(1)}, u32[]{:S(2)}, u32[]{:S(2)}) collective-permute-start(bf16[256,1280]{1,0:T(8,128)(2,1)S(1)} %fusion.20), channel_id=1, source_target_pairs={{0,1},{1,0},{2,3},{3,2},{4,5},{5,4},{6,7},{7,6},{8,9},{9,8},{10,11... | collective-permute-start | bytes 1966088 | tf_op jit(solution)/shard_map/ppermute | solution.py:26
  254.7 1.7 collective-permute-done.20
  257.8 2.5 reduce_sum.81
  261.2 1.6 fusion.23
  262.9 13.6 %all-to-all-start.2 = ((bf16[8,120,128]{2,1,0:T(8,128)(2,1)}), bf16[8,120,128]{2,1,0:T(8,128)(2,1)S(1)}, u32[]{:S(2)}, u32[]{:S(2)}) async-start(bf16[8,120,128]{2,1,0:T(8,128)(2,1)} %fusion.23), calls=%async_computation.2 | async-start | bytes 491520 | tf_op jit(solution)/shard_map/all_to_all | solution.py:412
  276.4 2.8 fusion.21
  279.2 7.7 %all-to-all-done.2 = bf16[8,120,128]{2,1,0:T(8,128)(2,1)S(1)} async-done(((bf16[8,120,128]{2,1,0:T(8,128)(2,1)}), bf16[8,120,128]{2,1,0:T(8,128)(2,1)S(1)}, u32[]{:S(2)}, u32[]{:S(2)}) %all-to-all-start.2) | async-done | bytes 245792 | tf_op jit(solution)/shard_map/all_to_all | solution.py:412
  (140 shorter events, 20.9 us)
Async XLA Ops:
  1.8 4.7 %copy-start = (bf16[1,256,1280]{2,1,0:T(8,128)(2,1)S(1)}, bf16[1,256,1280]{2,1,0:T(8,128)(2,1)}, u32[]{:S(2)}) copy-start(bf16[1,256,1280]{2,1,0:T(8,128)(2,1)} %param.6) | copy-start | bytes 1966084
  3.8 3.2 %collective-permute-start = (bf16[80,1280]{1,0:T(8,128)(2,1)S(1)}, bf16[80,1280]{1,0:T(8,128)(2,1)S(1)}, u32[]{:S(2)}, u32[]{:S(2)}) collective-permute-start(bf16[80,1280]{1,0:T(8,128)(2,1)S(1)} %concatenate.60), channel_id=1, source_target_pairs={{0,64},{8,72},{66,130},{74,138},{132,196},{140,204},{198,14},{206,... | collective-permute-start | bytes 614408 | tf_op jit(solution)/shard_map/ppermute | solution.py:55
  4.5 2.5 collective-permute-start.1
  5.2 14.2 %collective-permute-start.2 = (bf16[80,1280]{1,0:T(8,128)(2,1)S(1)}, bf16[80,1280]{1,0:T(8,128)(2,1)S(1)}, u32[]{:S(2)}, u32[]{:S(2)}) collective-permute-start(bf16[80,1280]{1,0:T(8,128)(2,1)S(1)} %concatenate.60), channel_id=1, source_target_pairs={{0,128},{8,136},{66,194},{74,202},{132,12},{140,4},{198,78},{206,7... | collective-permute-start | bytes 614408 | tf_op jit(solution)/shard_map/ppermute | solution.py:55
  6.7 249.7 %copy-start.25 = (f32[256]{0:T(256)}, f32[256]{0:T(256)S(1)}, u32[]{:S(2)}) copy-start(f32[256]{0:T(256)S(1)} %broadcast_multiply_fusion.4) | copy-start | bytes 3076
  21.4 6.5 %copy-start.24 = (f32[1280]{0:T(1024)S(1)}, f32[1280]{0:T(1024)}, u32[]{:S(2)}) copy-start(f32[1280]{0:T(1024)} %param.8) | copy-start | bytes 15364
  21.4 59.9 %all-to-all-start = ((bf16[16,80,1280]{2,1,0:T(8,128)(2,1)}), bf16[16,80,1280]{2,1,0:T(8,128)(2,1)}, u32[]{:S(2)}, u32[]{:S(2)}) async-start(bf16[16,80,1280]{2,1,0:T(8,128)(2,1)} %broadcast_in_dim.14), calls=%async_computation | async-start | bytes 6553600 | tf_op jit(solution)/shard_map/all_to_all | solution.py:341
  27.9 2.2 copy-start.28
  27.9 228.5 %copy-start.26 = (f32[256]{0:T(256)}, f32[256]{0:T(256)S(1)}, u32[]{:S(2)}) copy-start(f32[256]{0:T(256)S(1)} %add_rsqrt_fusion.1) | copy-start | bytes 3076
  27.9 5.8 %copy-start.7 = (bf16[1,256,1280]{2,1,0:T(8,128)(2,1)S(1)}, bf16[1,256,1280]{2,1,0:T(8,128)(2,1)}, u32[]{:S(2)}) copy-start(bf16[1,256,1280]{2,1,0:T(8,128)(2,1)} %param.11) | copy-start | bytes 1966084
  28.2 11.7 %collective-permute-start.3 = (bf16[256,1280]{1,0:T(8,128)(2,1)S(1)}, bf16[256,1280]{1,0:T(8,128)(2,1)S(1)}, u32[]{:S(2)}, u32[]{:S(2)}) collective-permute-start(bf16[256,1280]{1,0:T(8,128)(2,1)S(1)} %fusion.11), channel_id=1, source_target_pairs={{0,1},{1,0},{2,3},{3,2},{4,5},{5,4},{6,7},{7,6},{8,9},{9,8},{10,11... | collective-permute-start | bytes 1966088 | tf_op jit(solution)/shard_map/ppermute | solution.py:26
  30.1 47.5 %collective-permute-start.9 = (bf16[272,1280]{1,0:T(8,128)(2,1)S(1)}, bf16[272,1280]{1,0:T(8,128)(2,1)}, u32[]{:S(2)}, u32[]{:S(2)}) collective-permute-start(bf16[272,1280]{1,0:T(8,128)(2,1)S(1)} %fusion.19), channel_id=1, source_target_pairs={{6,0},{8,14},{7,1},{9,15},{22,16},{24,30},{23,17},{25,31},{38,32},... | collective-permute-start | bytes 2088968 | tf_op jit(solution)/shard_map/ppermute | solution.py:35
  33.2 1.4 collective-permute-start.6
  33.7 45.2 %collective-permute-start.5 = (bf16[256,1280]{1,0:T(8,128)(2,1)S(1)}, bf16[256,1280]{1,0:T(8,128)(2,1)}, u32[]{:S(2)}, u32[]{:S(2)}) collective-permute-start(bf16[256,1280]{1,0:T(8,128)(2,1)S(1)} %bitcast.87), channel_id=1, source_target_pairs={{0,1},{1,0},{2,3},{3,2},{4,5},{5,4},{6,7},{7,6},{8,9},{9,8},{10,11... | collective-permute-start | bytes 1966088 | tf_op jit(solution)/shard_map/ppermute | solution.py:26
  34.6 6.8 %copy-start.27 = (f32[1,512]{1,0:T(1,128)}, f32[1,512]{1,0:T(1,128)S(1)}, u32[]{:S(2)}) copy-start(f32[1,512]{1,0:T(1,128)S(1)} %pad_maximum_fusion.9.live_ref) | copy-start | bytes 6148
  34.6 94.9 %collective-permute-start.12 = (f32[1,512]{1,0:T(1,128)S(1)}, f32[1,512]{1,0:T(1,128)S(1)}, u32[]{:S(2)}, u32[]{:S(2)}) collective-permute-start(f32[1,512]{1,0:T(1,128)S(1)} %pad_maximum_fusion.9.live_ref), channel_id=1, source_target_pairs={{0,2},{2,4},{4,6},{1,3},{3,5},{5,7},{8,10},{10,12},{12,14},{9,11},... | collective-permute-start | bytes 6152 | tf_op jit(solution)/shard_map/ppermute | solution.py:31
  35.9 94.2 %collective-permute-start.14 = (f32[1,512]{1,0:T(1,128)S(1)}, f32[1,512]{1,0:T(1,128)S(1)}, u32[]{:S(2)}, u32[]{:S(2)}) collective-permute-start(f32[1,512]{1,0:T(1,128)S(1)} %pad_maximum_fusion.9.live_ref), channel_id=1, source_target_pairs={{2,0},{4,2},{6,4},{3,1},{5,3},{7,5},{10,8},{12,10},{14,12},{11,9},... | collective-permute-start | bytes 6152 | tf_op jit(solution)/shard_map/ppermute | solution.py:31
  77.6 38.4 %collective-permute-start.10 = (bf16[272,1280]{1,0:T(8,128)(2,1)}, bf16[272,1280]{1,0:T(8,128)(2,1)S(1)}, u32[]{:S(2)}, u32[]{:S(2)}) collective-permute-start(bf16[272,1280]{1,0:T(8,128)(2,1)} %collective-permute-done.9), channel_id=1, source_target_pairs={{0,8},{14,6},{1,9},{15,7},{16,24},{30,22},{17,25},{31,23},{32,40},... | collective-permute-start | bytes 2088968 | tf_op jit(solution)/shard_map/ppermute | solution.py:39
  81.3 1.7 copy-start.8
  81.3 1.8 copy-start.10
  83.0 55.8 %copy-start.2 = (bf16[16,80,640]{2,1,0:T(8,128)(2,1)}, bf16[16,80,640]{2,1,0:T(8,128)(2,1)S(1)}, u32[]{:S(2)}) copy-start(bf16[16,80,640]{2,1,0:T(8,128)(2,1)S(1)} %slice.97) | copy-start | bytes 4915204
  116.2 24.6 %collective-permute-start.7 = (bf16[640,512]{1,0:T(8,128)(2,1)}, bf16[640,512]{1,0:T(8,128)(2,1)}, u32[]{:S(2)}, u32[]{:S(2)}) collective-permute-start(bf16[640,512]{1,0:T(8,128)(2,1)} %convolution_convert_fusion.1), channel_id=1, source_target_pairs={{0,2},{2,4},{4,6},{1,3},{3,5},{5,7},{8,10},{10,12},{12,14},{9,11},... | collective-permute-start | bytes 1966088 | tf_op jit(solution)/shard_map/ppermute | solution.py:31
  117.5 23.3 %collective-permute-start.8 = (bf16[640,512]{1,0:T(8,128)(2,1)}, bf16[640,512]{1,0:T(8,128)(2,1)}, u32[]{:S(2)}, u32[]{:S(2)}) collective-permute-start(bf16[640,512]{1,0:T(8,128)(2,1)} %convolution_convert_fusion.1), channel_id=1, source_target_pairs={{2,0},{4,2},{6,4},{3,1},{5,3},{7,5},{10,8},{12,10},{14,12},{11,9},... | collective-permute-start | bytes 1966088 | tf_op jit(solution)/shard_map/ppermute | solution.py:31
  123.8 5.6 %collective-permute-start.13 = (f32[1,256]{1,0:T(1,128)S(1)}, f32[1,256]{1,0:T(1,128)S(1)}, u32[]{:S(2)}, u32[]{:S(2)}) collective-permute-start(f32[1,256]{1,0:T(1,128)S(1)} %slice_convert_fusion), channel_id=1, source_target_pairs={{0,1},{1,0},{2,3},{3,2},{4,5},{5,4},{6,7},{7,6},{8,9},{9,8},{10,11... | collective-permute-start | bytes 3080 | tf_op jit(solution)/shard_map/ppermute | solution.py:26
  126.9 1.6 copy-start.5
  129.4 7.8 %collective-permute-start.11 = (bf16[256,1280]{1,0:T(8,128)(2,1)}, bf16[256,1280]{1,0:T(8,128)(2,1)}, u32[]{:S(2)}, u32[]{:S(2)}) collective-permute-start(bf16[256,1280]{1,0:T(8,128)(2,1)} %fusion.10), channel_id=1, source_target_pairs={{0,1},{1,0},{2,3},{3,2},{4,5},{5,4},{6,7},{7,6},{8,9},{9,8},{10,11... | collective-permute-start | bytes 1966088 | tf_op jit(solution)/shard_map/ppermute | solution.py:26
  129.4 3.1 %collective-permute-start.4 = (bf16[8,80,320]{2,1,0:T(8,128)(2,1)S(1)}, bf16[8,80,320]{2,1,0:T(8,128)(2,1)S(1)}, u32[]{:S(2)}, u32[]{:S(2)}) collective-permute-start(bf16[8,80,320]{2,1,0:T(8,128)(2,1)S(1)} %get-tuple-element.41), channel_id=1, source_target_pairs={{0,1},{1,0},{2,3},{3,2},{4,5},{5,4},{6,7},{7,6},{8,9},{9,8},{10,11... | collective-permute-start | bytes 1228808 | tf_op jit(solution)/shard_map/ppermute | solution.py:26
  138.8 2.0 copy-start.12
  138.8 2.0 copy-start.14
  140.8 24.7 %copy-start.1 = (bf16[512,1280]{1,0:T(8,128)(2,1)S(1)}, bf16[512,1280]{1,0:T(8,128)(2,1)}, u32[]{:S(2)}) copy-start(bf16[512,1280]{1,0:T(8,128)(2,1)} %pad_maximum_fusion.3.cot_ref) | copy-start | bytes 3932164
  162.1 15.9 %collective-permute-start.16 = (bf16[2,320,512]{2,1,0:T(8,128)(2,1)}, bf16[2,320,512]{2,1,0:T(8,128)(2,1)}, u32[]{:S(2)}, u32[]{:S(2)}) collective-permute-start(bf16[2,320,512]{2,1,0:T(8,128)(2,1)} %get-tuple-element.21), channel_id=1, source_target_pairs={{2,0},{4,2},{6,4},{3,1},{5,3},{7,5},{10,8},{12,10},{14,12},{11,9},... | collective-permute-start | bytes 1966088 | tf_op jit(solution)/shard_map/ppermute | solution.py:31
  164.2 18.3 %collective-permute-start.17 = (bf16[2,320,512]{2,1,0:T(8,128)(2,1)}, bf16[2,320,512]{2,1,0:T(8,128)(2,1)}, u32[]{:S(2)}, u32[]{:S(2)}) collective-permute-start(bf16[2,320,512]{2,1,0:T(8,128)(2,1)} %get-tuple-element.22), channel_id=1, source_target_pairs={{0,2},{2,4},{4,6},{1,3},{3,5},{5,7},{8,10},{10,12},{12,14},{9,11},... | collective-permute-start | bytes 1966088 | tf_op jit(solution)/shard_map/ppermute | solution.py:31
  166.4 2.0 copy-start.13
  166.4 2.0 copy-start.15
  167.3 6.5 %collective-permute-start.15 = (bf16[320,512]{1,0:T(8,128)(2,1)S(1)}, bf16[320,512]{1,0:T(8,128)(2,1)S(1)}, u32[]{:S(2)}, u32[]{:S(2)}) collective-permute-start(bf16[320,512]{1,0:T(8,128)(2,1)S(1)} %copy-done.22), channel_id=1, source_target_pairs={{0,1},{1,0},{2,3},{3,2},{4,5},{5,4},{6,7},{7,6},{8,9},{9,8},{10,11... | collective-permute-start | bytes 983048 | tf_op jit(solution)/shard_map/ppermute | solution.py:26
  173.7 8.8 %copy-start.17 = (f32[2,320,512]{2,1,0:T(8,128)S(1)}, f32[2,320,512]{2,1,0:T(8,128)}, u32[]{:S(2)}) copy-start(f32[2,320,512]{2,1,0:T(8,128)} %get-tuple-element.20) | copy-start | bytes 3932164
  178.0 6.1 %copy-start.18 = (bf16[320,512]{1,0:T(8,128)(2,1)S(1)}, bf16[320,512]{1,0:T(8,128)(2,1)}, u32[]{:S(2)}) copy-start(bf16[320,512]{1,0:T(8,128)(2,1)} %get-tuple-element.24) | copy-start | bytes 983044
  178.0 6.1 %copy-start.19 = (bf16[2,320,512]{2,1,0:T(8,128)(2,1)S(1)}, bf16[2,320,512]{2,1,0:T(8,128)(2,1)}, u32[]{:S(2)}) copy-start(bf16[2,320,512]{2,1,0:T(8,128)(2,1)} %get-tuple-element.25) | copy-start | bytes 1966084
  184.1 1.7 copy-start.11
  184.3 2.7 copy-start.4
  184.3 7.0 %collective-permute-start.18 = (bf16[5,320,512]{2,1,0:T(8,128)(2,1)S(1)}, bf16[5,320,512]{2,1,0:T(8,128)(2,1)}, u32[]{:S(2)}, u32[]{:S(2)}) collective-permute-start(bf16[5,320,512]{2,1,0:T(8,128)(2,1)S(1)} %pad_maximum_fusion.1.own_ref), channel_id=1, source_target_pairs={{0,1},{1,0},{2,3},{3,2},{4,5},{5,4},{6,7},{7,6},{8,9},{9,8},{10,11... | collective-permute-start | bytes 4915208 | tf_op jit(solution)/shard_map/ppermute | solution.py:26
  199.8 7.4 %copy-start.20 = (bf16[2,320,512]{2,1,0:T(8,128)(2,1)S(1)}, bf16[2,320,512]{2,1,0:T(8,128)(2,1)}, u32[]{:S(2)}) copy-start(bf16[2,320,512]{2,1,0:T(8,128)(2,1)} %get-tuple-element.25) | copy-start | bytes 1966084
  199.8 9.3 %copy-start.6 = (bf16[16,80,320]{2,1,0:T(8,128)(2,1)S(1)}, bf16[16,80,320]{2,1,0:T(8,128)(2,1)}, u32[]{:S(2)}) copy-start(bf16[16,80,320]{2,1,0:T(8,128)(2,1)} %copy-done.5) | copy-start | bytes 2457604
  199.8 58.0 %all-to-all-start.1 = ((bf16[16,840,128]{2,1,0:T(8,128)(2,1)}), bf16[16,840,128]{2,1,0:T(8,128)(2,1)}, u32[]{:S(2)}, u32[]{:S(2)}) async-start(bf16[16,840,128]{2,1,0:T(8,128)(2,1)} %bitcast.74), calls=%async_computation.1 | async-start | bytes 6881280 | tf_op jit(solution)/shard_map/all_to_all | solution.py:393
  207.2 41.5 %collective-permute-start.19 = (bf16[2,320,512]{2,1,0:T(8,128)(2,1)S(1)}, bf16[2,320,512]{2,1,0:T(8,128)(2,1)}, u32[]{:S(2)}, u32[]{:S(2)}) collective-permute-start(bf16[2,320,512]{2,1,0:T(8,128)(2,1)S(1)} %copy-done.20), channel_id=1, source_target_pairs={{6,8},{8,6},{7,9},{9,7},{22,24},{24,22},{23,25},{25,23},{38,40},{4... | collective-permute-start | bytes 1966088 | tf_op jit(solution)/shard_map/ppermute | solution.py:43
  210.1 39.9 %copy-start.3 = (bf16[16,80,640]{2,1,0:T(8,128)(2,1)S(1)}, bf16[16,80,640]{2,1,0:T(8,128)(2,1)}, u32[]{:S(2)}) copy-start(bf16[16,80,640]{2,1,0:T(8,128)(2,1)} %copy-done.2) | copy-start | bytes 4915204
  251.3 5.1 %collective-permute-start.20 = (bf16[256,1280]{1,0:T(8,128)(2,1)S(1)}, bf16[256,1280]{1,0:T(8,128)(2,1)S(1)}, u32[]{:S(2)}, u32[]{:S(2)}) collective-permute-start(bf16[256,1280]{1,0:T(8,128)(2,1)S(1)} %fusion.20), channel_id=1, source_target_pairs={{0,1},{1,0},{2,3},{3,2},{4,5},{5,4},{6,7},{7,6},{8,9},{9,8},{10,11... | collective-permute-start | bytes 1966088 | tf_op jit(solution)/shard_map/ppermute | solution.py:26
  262.9 24.0 %all-to-all-start.2 = ((bf16[8,120,128]{2,1,0:T(8,128)(2,1)}), bf16[8,120,128]{2,1,0:T(8,128)(2,1)S(1)}, u32[]{:S(2)}, u32[]{:S(2)}) async-start(bf16[8,120,128]{2,1,0:T(8,128)(2,1)} %fusion.23), calls=%async_computation.2 | async-start | bytes 491520 | tf_op jit(solution)/shard_map/all_to_all | solution.py:412
  (5 other events, 4.6 us)

commit v3 on v2

--- a/solution.py
+++ b/solution.py
@@ -29,14 +29,6 @@
 def along_y(value, step):
     pairs = [(i, i + step) for i in range(Y) if 0 <= i + step < Y]
     return lax.ppermute(value, "y", pairs)
-
-
-def across_y(value):
-    return lax.ppermute(value, ("zh", "y"), [(Y - 1, 0), (Y, 2 * Y - 1)])
-
-
-def across_z(value):
-    return lax.ppermute(value, ("zh", "y"), [(0, Y), (2 * Y - 1, Y - 1)])
 
 
 def across(value):
@@ -84,13 +76,16 @@
                 chunks.append(chunk)
     grads_k, grads_v = ([None] * 6, [None] * 6)
     scale = 1.0 / math.sqrt(HEAD_DIM)
+    key_rows = jnp.concatenate(chunks_k, axis=1).T
+    value_rows = jnp.concatenate(chunks_v, axis=1).T
     for block in range(2):
+        span = slice(block * rows, (block + 5) * rows)
         cols = slice(block * rows, (block + 1) * rows)
         keys_t = jnp.concatenate(chunks_k[block:block + 5], axis=1)
         values_t = jnp.concatenate(chunks_v[block:block + 5], axis=1)
         query = (q_ref[:, cols].astype(F32) * scale).astype(BF)
         grad = g_ref[:, cols]
-        scores = dot(keys_t.T, query, 1, 0) + bias_ref[block]
+        scores = dot(key_rows[span], query, 1, 0) + bias_ref[block]
         peak = jnp.max(scores, axis=0, keepdims=True)
         exponent = jnp.exp(scores - peak)
         inverse = 1.0 / jnp.sum(exponent, axis=0, keepdims=True)
@@ -99,7 +94,7 @@
         attended = (dot(values_t, probs_b, 1, 0) * live_ref[:, cols]).astype(BF)
         att_ref[:, cols] = attended
         delta = jnp.sum(grad.astype(F32) * attended.astype(F32), axis=0, keepdims=True)
-        grad_probs = dot(values_t.T, grad, 1, 0)
+        grad_probs = dot(value_rows[span], grad, 1, 0)
         grad_scores = (probs * (grad_probs - delta)).astype(BF)
         dq_ref[:, cols] = (dot(keys_t, grad_scores, 1, 0) * scale).astype(BF)
         grad_k = dot(query, grad_scores, 1, 1)
@@ -222,10 +217,11 @@
     )(flags, own, other, cot)
 
 
-def weight_kernel(flag_ref, rows_ref, far_rows_ref, own_ref, other_ref, extra_ref, out_ref, near_ref, far_ref, sum_ref):
+def weight_kernel(flag_ref, rows_ref, far_rows_ref, own_q, other_q, own_kv, other_kv, own_far, other_far,
+                  extra_ref, out_ref, near_ref, far_ref, sum_ref):
     block = rows_ref.shape[2]
     count = rows_ref.shape[3]
-    half = own_ref.shape[1]
+    half = own_q.shape[0]
     cols = 3 * 2 * half // (ZH * Y * C)
 
     def assemble(core):
@@ -236,12 +232,13 @@
             while begin < end:
                 kind, which, row = begin // (2 * half), begin // half % 2, begin % half
                 size = min(end - begin, half - row)
-                ref = own_ref if which == core else other_ref
-                near.append(ref[kind].astype(F32)[row:row + size])
+                here = which == core
                 if kind == 0:
+                    near.append((own_q if here else other_q)[...].astype(F32)[row:row + size])
                     far.append(jnp.zeros((size, count), F32))
                 else:
-                    far.append(ref[kind + 2].astype(F32)[row:row + size])
+                    near.append((own_kv if here else other_kv)[kind - 1].astype(F32)[row:row + size])
+                    far.append((own_far if here else other_far)[kind - 1].astype(F32)[row:row + size])
                 begin += size
             pad = jnp.zeros((128 - cols, count), F32)
             near_ref[at * 128:(at + 1) * 128] = jnp.concatenate(near + [pad], axis=0).astype(BF)
@@ -272,17 +269,18 @@
     out_ref[0, :, ZL * ZH * block:] = extra_ref[0].astype(BF)
 
 
-def weight_terms(flags, rows_t, far_rows_t, own, other, extra):
+def weight_terms(flags, rows_t, far_rows_t, queries, pairs, far, extra):
     block = rows_t.shape[0] // (ZL * X)
     count = rows_t.shape[1]
     left = pl.BlockSpec((ZL, 1, block, count), lambda x: (0, x, 0, 0))
-    right = pl.BlockSpec(own.shape, lambda x: (0, 0, 0))
+    one = pl.BlockSpec(queries[0].shape, lambda x: (0, 0))
+    two = pl.BlockSpec(pairs[0].shape, lambda x: (0, 0, 0))
     lanes = ZH * Y * 128
     height = ZL * ZH * block + extra.shape[2]
     return pl.pallas_call(
         weight_kernel,
         grid=(X,),
-        in_specs=[SCALARS, left, left, right, right,
+        in_specs=[SCALARS, left, left, one, one, two, two, two, two,
                   pl.BlockSpec((1,) + extra.shape[1:], lambda x: (x, 0, 0, 0))],
         out_specs=pl.BlockSpec((1, Y, height, 128), lambda x: (x, 0, 0, 0)),
         out_shape=jax.ShapeDtypeStruct((X, Y, height, 128), BF),
@@ -292,7 +290,8 @@
             pltpu.VMEM((ZL * block, lanes), F32),
         ],
         name="weight_terms",
-    )(flags, rows_t.reshape(ZL, X, block, count), far_rows_t.reshape(ZL, X, block, count), own, other, extra)
+    )(flags, rows_t.reshape(ZL, X, block, count), far_rows_t.reshape(ZL, X, block, count),
+      *queries, *pairs, *far, extra)
 
 
 def body(frames, live, norm_gain, w_qkv, w_out, cotangent):
@@ -317,8 +316,7 @@
 
     live_own = live[0].astype(F32)[None]
     marks = jnp.pad(live_own.astype(BF), ((0, 15), (0, model - length)))
-    far = across_y(jnp.concatenate([frames[0], marks], axis=0))
-    far = across_z(far)
+    far = across(jnp.concatenate([frames[0], marks], axis=0))
     live_2 = both(core, live_own, swap_core(live_own), 1)
     unit_rows, inverse = norm_rows(frames[0].astype(F32))
     normed = (unit_rows * norm_gain).astype(BF)
@@ -380,15 +378,17 @@
     from_far = across(grad_far)
 
     attended_other = swap_core(attended)
+    grad_query_other = swap_core(grad_query)
+    grad_far_other = swap_core(grad_far)
     term_out = out_terms(flags, attended, attended_other, cot_mine)
     far_2, _ = lax.optimization_barrier((far_2, grad_own))
     far_t = turn(far_2)
     grad_own, term_out, far_t = lax.optimization_barrier((grad_own, term_out, far_t))
 
     grad_pairs = (grad_own + from_after.astype(F32) + from_before.astype(F32)).astype(BF)
-    grads = jnp.concatenate([grad_query[None], grad_pairs, grad_far], axis=0)
-    grads_other = swap_core(grads)
-    terms = weight_terms(flags, normed_t, far_t, grads, grads_other, term_out)
+    pairs_other = swap_core(grad_pairs)
+    terms = weight_terms(flags, normed_t, far_t, (grad_query, grad_query_other), (grad_pairs, pairs_other),
+                         (grad_far, grad_far_other), term_out)
     grad_pairs, terms = lax.optimization_barrier((grad_pairs, terms))
     got = lax.all_to_all(terms.reshape((X * Y,) + terms.shape[2:]), ("x", "y"), 0, 0, tiled=True)
 

time: 289 us -> 263 us (0.910)
  the two profiles are of different devices: /device:TPU:63 before, /device:TPU:46 now
where the time goes in v3:
time: 263 us; the launch traced here: 261 us
  waiting for transfers between devices  93.2 us (35%)
  starting transfers between devices  72.3 us (27%)
  Pallas kernels  44 us (17%)
  other arithmetic  25 us (10%)
  local copies, waits for them, and re-layouts  18 us (7%)
  matrix products  7.56 us (3%)
    all_to_all x1, waiting for transfers between devices, body(): lax.all_to_all(terms.reshape((X * Y,) + terms.shape[2:]), ('x', 'y'), 0,...  45.7 us
    all_to_all x1, waiting for transfers between devices, body(): weights = lax.all_to_all(spread, ('y', 'x'), 0, 0, tiled=True)  29.6 us
    ppermute x6, starting transfers between devices, along_y(): return lax.ppermute(value, 'y', pairs)  23.7 us
    pallas_call x1, Pallas kernels, attention(): pl.pallas_call(attention_kernel, grid=(heads,), in_specs=[SCALARS, one, o...  21.3 us
    all_to_all x1, starting transfers between devices, body(): sums = lax.all_to_all(sums, ('zl', 'zh'), 0, 0, tiled=True)  19.8 us
    all_to_all x1, starting transfers between devices, body(): lax.all_to_all(terms.reshape((X * Y,) + terms.shape[2:]), ('x', 'y'), 0,...  9.29 us
    pallas_call x2, Pallas kernels, turn(): pl.pallas_call(turn_kernel, grid=(cols // step,), in_specs=[pl.BlockSpec(...  8.45 us
    all_to_all x1, starting transfers between devices, body(): weights = lax.all_to_all(spread, ('y', 'x'), 0, 0, tiled=True)  7.95 us
  transfers between devices with their start and end apart: 25, of which 9 were waited for; matrix products, arithmetic and copies ran while one was open for 14% of the time, Pallas kernels for 6%

profile of v3, /device:TPU:46, one launch (start us, length us, event | category | flops | bytes accessed | tf_op | source)
XLA Modules:
  0.0 261.3 jit_solution(17897454307393201783)
XLA Ops:
  0.6 0.9 reshape.297
  1.8 1.4 reshape.296
  3.8 5.2 %collective-permute-start.2 = (bf16[80,1280]{1,0:T(8,128)(2,1)S(1)}, bf16[80,1280]{1,0:T(8,128)(2,1)S(1)}, u32[]{:S(2)}, u32[]{:S(2)}) collective-permute-start(bf16[80,1280]{1,0:T(8,128)(2,1)S(1)} %concatenate.57), channel_id=1, source_target_pairs={{0,128},{8,136},{66,194},{74,202},{132,12},{140,4},{198,78},{206,7... | collective-permute-start | bytes 614408 | tf_op jit(solution)/shard_map/ppermute | solution.py:47
  9.0 1.3 collective-permute-start.1
  10.3 1.3 collective-permute-start
  12.0 2.5 collective-permute-done.2
  14.6 3.1 %collective-permute-done = bf16[80,1280]{1,0:T(8,128)(2,1)S(1)} collective-permute-done((bf16[80,1280]{1,0:T(8,128)(2,1)S(1)}, bf16[80,1280]{1,0:T(8,128)(2,1)S(1)}, u32[]{:S(2)}, u32[]{:S(2)}) %collective-permute-start) | collective-permute-done | bytes 204832 | tf_op jit(solution)/shard_map/ppermute | solution.py:47
  17.8 2.0 broadcast_in_dim.12
  19.7 8.0 %all-to-all-start = ((bf16[16,80,1280]{2,1,0:T(8,128)(2,1)}), bf16[16,80,1280]{2,1,0:T(8,128)(2,1)}, u32[]{:S(2)}, u32[]{:S(2)}) async-start(bf16[16,80,1280]{2,1,0:T(8,128)(2,1)} %broadcast_in_dim.12), calls=%async_computation | async-start | bytes 6553600 | tf_op jit(solution)/shard_map/all_to_all | solution.py:339
  28.9 0.9 fusion.19
  31.2 2.5 collective-permute-start.13
  33.6 3.4 %collective-permute-start.11 = (f32[1,512]{1,0:T(1,128)S(1)}, f32[1,512]{1,0:T(1,128)S(1)}, u32[]{:S(2)}, u32[]{:S(2)}) collective-permute-start(f32[1,512]{1,0:T(1,128)S(1)} %pad_maximum_fusion.8.live_ref), channel_id=1, source_target_pairs={{0,2},{2,4},{4,6},{1,3},{3,5},{5,7},{8,10},{10,12},{12,14},{9,11},... | collective-permute-start | bytes 6152 | tf_op jit(solution)/shard_map/ppermute | solution.py:31
  37.0 2.6 broadcast_select_fusion.5
  39.7 1.2 pad_maximum_fusion.2.cot_ref
  40.9 29.6 %all-to-all-done = bf16[16,80,1280]{2,1,0:T(8,128)(2,1)} async-done(((bf16[16,80,1280]{2,1,0:T(8,128)(2,1)}), bf16[16,80,1280]{2,1,0:T(8,128)(2,1)}, u32[]{:S(2)}, u32[]{:S(2)}) %all-to-all-start) | async-done | bytes 3276832 | tf_op jit(solution)/shard_map/all_to_all | solution.py:339
  70.5 1.7 slice.97
  72.3 2.0 convolution_convert_fusion.1
  74.4 8.8 %collective-permute-start.8 = (bf16[640,512]{1,0:T(8,128)(2,1)}, bf16[640,512]{1,0:T(8,128)(2,1)}, u32[]{:S(2)}, u32[]{:S(2)}) collective-permute-start(bf16[640,512]{1,0:T(8,128)(2,1)} %convolution_convert_fusion.1), channel_id=1, source_target_pairs={{2,0},{4,2},{6,4},{3,1},{5,3},{7,5},{10,8},{12,10},{14,12},{11,9},... | collective-permute-start | bytes 1966088 | tf_op jit(solution)/shard_map/ppermute | solution.py:31
  83.3 1.9 collective-permute-start.7
  85.2 2.0 fusion.26
  87.2 1.5 convolution_convert_fusion.2.q_ref
  89.2 1.1 fusion.10
  92.6 1.8 pad_maximum_fusion.bias_ref
  95.2 3.9 %out_grads.1.g_ref = bf16[320,512]{1,0:T(8,128)(2,1)} custom-call(s32[3]{0:T(128)} %pad_add_fusion.flag_ref, bf16[8,80,320]{2,1,0:T(8,128)(2,1)} %get-tuple-element.42.own_ref, bf16[8,80,320]{2,1,0:T(8,128)(2,1)} %copy-done.22, bf16[512,1280]{1,0:T(8,128)(2,1)} %pad_maximum_fusion.2.cot_ref, f32[1,512]{1,0:T(1,128)} %copy-done.29), custom_call_target="tpu_custom_call" | custom-call | tf_op jit(solution)/shard_map/out_grads/pallas_call | solution.py:178
  99.1 1.5 broadcast_select_fusion.1
  100.7 1.9 convolution_convert_fusion
  102.7 21.3 %attention.1 = (bf16[320,512]{1,0:T(8,128)(2,1)}, bf16[320,512]{1,0:T(8,128)(2,1)}, f32[2,320,512]{2,1,0:T(8,128)}, bf16[2,320,512]{2,1,0:T(8,128)(2,1)}, bf16[2...) custom-call(s32[3]{0:T(128)} %pad_add_fusion.flag_ref, bf16[320,512]{1,0:T(8,128)(2,1)} %convolution_convert_fusion.2.q_ref, ...), custom_call_target="tpu_custom_call" | custom-call | tf_op jit(solution)/shard_map/attention/pallas_call | solution.py:125
  123.9 4.7 %collective-permute-start.15 = (bf16[2,320,512]{2,1,0:T(8,128)(2,1)}, bf16[2,320,512]{2,1,0:T(8,128)(2,1)}, u32[]{:S(2)}, u32[]{:S(2)}) collective-permute-start(bf16[2,320,512]{2,1,0:T(8,128)(2,1)} %get-tuple-element.21), channel_id=1, source_target_pairs={{2,0},{4,2},{6,4},{3,1},{5,3},{7,5},{10,8},{12,10},{14,12},{11,9},... | collective-permute-start | bytes 1966088 | tf_op jit(solution)/shard_map/ppermute | solution.py:31
  128.7 2.4 collective-permute-start.16
  132.9 1.0 pad_maximum_fusion.4.cot_ref
  133.9 1.1 pad_maximum_fusion.3.in_ref
  135.0 4.2 %turn.2 = bf16[1280,512]{1,0:T(8,128)(2,1)} custom-call(bf16[512,1280]{1,0:T(8,128)(2,1)} %pad_maximum_fusion.3.in_ref), custom_call_target="tpu_custom_call" | custom-call | tf_op jit(solution)/shard_map/turn/pallas_call | solution.py:151
  140.4 3.5 %out_terms.1.extra_ref = f32[4,4,200,128]{3,2,1,0:T(8,128)} custom-call(s32[3]{0:T(128)} %pad_add_fusion.flag_ref, bf16[320,512]{1,0:T(8,128)(2,1)} %get-tuple-element.18.own_ref, bf16[320,512]{1,0:T(8,128)(2,1)} %copy-done.25, bf16[512,640]{1,0:T(8,128)(2,1)} %pad_maximum_fusion.4.cot_ref), custom_call_target="tpu_custom_call" | custom-call | tf_op jit(solution)/shard_map/out_terms/pallas_call | solution.py:210
  144.7 2.9 %collective-permute-done.16 = bf16[2,320,512]{2,1,0:T(8,128)(2,1)} collective-permute-done((bf16[2,320,512]{2,1,0:T(8,128)(2,1)}, bf16[2,320,512]{2,1,0:T(8,128)(2,1)}, u32[]{:S(2)}, u32[]{:S(2)}) %collective-permute-start.16) | collective-permute-done | bytes 655392 | tf_op jit(solution)/shard_map/ppermute | solution.py:31
  147.6 1.6 add_convert_fusion.1.own_kv
  149.8 1.2 pad_maximum_fusion.1.in_ref
  151.1 4.2 %turn.3 = bf16[1280,512]{1,0:T(8,128)(2,1)} custom-call(bf16[512,1280]{1,0:T(8,128)(2,1)} %pad_maximum_fusion.1.in_ref), custom_call_target="tpu_custom_call" | custom-call | tf_op jit(solution)/shard_map/turn/pallas_call | solution.py:151
  156.2 6.8 %weight_terms.1 = bf16[4,4,840,128]{3,2,1,0:T(8,128)(2,1)} custom-call(s32[3]{0:T(128)} %pad_add_fusion.flag_ref, bf16[4,4,80,512]{3,2,1,0:T(8,128)(2,1)} %bitcast.81, bf16[4,4,80,512]{3,2,1,0:T(8,128)(2,1)} %bitcast.80, bf16[320,512]{1,0:T(8,128)(2,1)} %get-tuple-element.24.own_q, bf16[320,512]{1,0:T(8,128)(2,1)} %copy-done.23, ...), custom_call_target="tpu_custom_call" | custom-call | tf_op jit(solution)/shard_map/weight_terms/pallas_call | solution.py:280
  163.1 9.3 %all-to-all-start.1 = ((bf16[16,840,128]{2,1,0:T(8,128)(2,1)}), bf16[16,840,128]{2,1,0:T(8,128)(2,1)}, u32[]{:S(2)}, u32[]{:S(2)}) async-start(bf16[16,840,128]{2,1,0:T(8,128)(2,1)} %bitcast.73), calls=%async_computation.1 | async-start | bytes 6881280 | tf_op jit(solution)/shard_map/all_to_all | solution.py:393
  174.4 1.1 copy-done.3
  175.5 1.2 convolution_add_fusion
  176.9 2.1 collective-permute-done.21
  180.4 45.7 %all-to-all-done.1 = bf16[16,840,128]{2,1,0:T(8,128)(2,1)} async-done(((bf16[16,840,128]{2,1,0:T(8,128)(2,1)}), bf16[16,840,128]{2,1,0:T(8,128)(2,1)}, u32[]{:S(2)}, u32[]{:S(2)}) %all-to-all-start.1) | async-done | bytes 3440672 | tf_op jit(solution)/shard_map/all_to_all | solution.py:393
  226.1 2.5 reduce_sum.81
  229.5 1.7 fusion.23
  231.1 19.8 %all-to-all-start.2 = ((bf16[8,120,128]{2,1,0:T(8,128)(2,1)}), bf16[8,120,128]{2,1,0:T(8,128)(2,1)S(1)}, u32[]{:S(2)}, u32[]{:S(2)}) async-start(bf16[8,120,128]{2,1,0:T(8,128)(2,1)} %fusion.23), calls=%async_computation.2 | async-start | bytes 491520 | tf_op jit(solution)/shard_map/all_to_all | solution.py:412
  250.9 2.8 %fusion.21 = bf16[1,256,1280]{2,1,0:T(8,128)(2,1)} fusion(f32[256]{0:T(256)} %get-tuple-element.58, f32[256]{0:T(256)} %get-tuple-element.59, f32[256]{0:T(256)} %copy-done.28, f32[256]{0:T(256)} %copy-done.27, f32[1280]{0:T(1024)S(1)} %copy-done.26, bf16[256,1280]{1,0:T(8,128)(2,1)} %copy-done.17, f32[2,256,1280]{2,1,0:T(8,128)S(1)} %bitcast.76, ...), kind=kLoop, calls=%fused_computation.41 | loop fusion | flops 4259840 | bytes 3941380 | tf_op jit(solution)/shard_map/broadcast_in_dim | solution.py:421
  253.7 6.3 %all-to-all-done.2 = bf16[8,120,128]{2,1,0:T(8,128)(2,1)S(1)} async-done(((bf16[8,120,128]{2,1,0:T(8,128)(2,1)}), bf16[8,120,128]{2,1,0:T(8,128)(2,1)S(1)}, u32[]{:S(2)}, u32[]{:S(2)}) %all-to-all-start.2) | async-done | bytes 245792 | tf_op jit(solution)/shard_map/all_to_all | solution.py:412
  (145 shorter events, 18.6 us)
Async XLA Ops:
  1.8 9.9 %copy-start.30 = (s32[1,256]{1,0:T(1,128)S(1)}, s32[1,256]{1,0:T(1,128)}, u32[]{:S(2)}) copy-start(s32[1,256]{1,0:T(1,128)} %param.7) | copy-start | bytes 3076
  1.8 10.0 %copy-start = (bf16[1,256,1280]{2,1,0:T(8,128)(2,1)S(1)}, bf16[1,256,1280]{2,1,0:T(8,128)(2,1)}, u32[]{:S(2)}) copy-start(bf16[1,256,1280]{2,1,0:T(8,128)(2,1)} %param.6) | copy-start | bytes 1966084
  3.8 10.6 %collective-permute-start.2 = (bf16[80,1280]{1,0:T(8,128)(2,1)S(1)}, bf16[80,1280]{1,0:T(8,128)(2,1)S(1)}, u32[]{:S(2)}, u32[]{:S(2)}) collective-permute-start(bf16[80,1280]{1,0:T(8,128)(2,1)S(1)} %concatenate.57), channel_id=1, source_target_pairs={{0,128},{8,136},{66,194},{74,202},{132,12},{140,4},{198,78},{206,7... | collective-permute-start | bytes 614408 | tf_op jit(solution)/shard_map/ppermute | solution.py:47
  9.0 5.6 %collective-permute-start.1 = (bf16[80,1280]{1,0:T(8,128)(2,1)S(1)}, bf16[80,1280]{1,0:T(8,128)(2,1)S(1)}, u32[]{:S(2)}, u32[]{:S(2)}) collective-permute-start(bf16[80,1280]{1,0:T(8,128)(2,1)S(1)} %concatenate.57), channel_id=1, source_target_pairs={{0,200},{8,192},{66,2},{74,10},{132,68},{140,76},{198,134},{206,14... | collective-permute-start | bytes 614408 | tf_op jit(solution)/shard_map/ppermute | solution.py:47
  10.3 7.4 %collective-permute-start = (bf16[80,1280]{1,0:T(8,128)(2,1)S(1)}, bf16[80,1280]{1,0:T(8,128)(2,1)S(1)}, u32[]{:S(2)}, u32[]{:S(2)}) collective-permute-start(bf16[80,1280]{1,0:T(8,128)(2,1)S(1)} %concatenate.57), channel_id=1, source_target_pairs={{0,64},{8,72},{66,130},{74,138},{132,196},{140,204},{198,14},{206,... | collective-permute-start | bytes 614408 | tf_op jit(solution)/shard_map/ppermute | solution.py:47
  11.7 19.5 %collective-permute-start.6 = (f32[1,256]{1,0:T(1,128)S(1)}, f32[1,256]{1,0:T(1,128)S(1)}, u32[]{:S(2)}, u32[]{:S(2)}) collective-permute-start(f32[1,256]{1,0:T(1,128)S(1)} %get-tuple-element.57), channel_id=1, source_target_pairs={{0,1},{1,0},{2,3},{3,2},{4,5},{5,4},{6,7},{7,6},{8,9},{9,8},{10,11... | collective-permute-start | bytes 3080 | tf_op jit(solution)/shard_map/ppermute | solution.py:26
  12.0 167.0 %copy-start.27 = (f32[256]{0:T(256)}, f32[256]{0:T(256)S(1)}, u32[]{:S(2)}) copy-start(f32[256]{0:T(256)S(1)} %broadcast_multiply_fusion.4) | copy-start | bytes 3076
  19.7 8.3 %copy-start.26 = (f32[1280]{0:T(1024)S(1)}, f32[1280]{0:T(1024)}, u32[]{:S(2)}) copy-start(f32[1280]{0:T(1024)} %param.8) | copy-start | bytes 15364
  19.7 50.8 %all-to-all-start = ((bf16[16,80,1280]{2,1,0:T(8,128)(2,1)}), bf16[16,80,1280]{2,1,0:T(8,128)(2,1)}, u32[]{:S(2)}, u32[]{:S(2)}) async-start(bf16[16,80,1280]{2,1,0:T(8,128)(2,1)} %broadcast_in_dim.12), calls=%async_computation | async-start | bytes 6553600 | tf_op jit(solution)/shard_map/all_to_all | solution.py:339
  28.0 151.0 %copy-start.28 = (f32[256]{0:T(256)}, f32[256]{0:T(256)S(1)}, u32[]{:S(2)}) copy-start(f32[256]{0:T(256)S(1)} %add_rsqrt_fusion.1) | copy-start | bytes 3076
  28.3 8.7 %collective-permute-start.3 = (bf16[256,1280]{1,0:T(8,128)(2,1)S(1)}, bf16[256,1280]{1,0:T(8,128)(2,1)}, u32[]{:S(2)}, u32[]{:S(2)}) collective-permute-start(bf16[256,1280]{1,0:T(8,128)(2,1)S(1)} %fusion.11), channel_id=1, source_target_pairs={{0,1},{1,0},{2,3},{3,2},{4,5},{5,4},{6,7},{7,6},{8,9},{9,8},{10,11... | collective-permute-start | bytes 1966088 | tf_op jit(solution)/shard_map/ppermute | solution.py:26
  28.8 10.9 %collective-permute-start.5 = (bf16[256,1280]{1,0:T(8,128)(2,1)S(1)}, bf16[256,1280]{1,0:T(8,128)(2,1)S(1)}, u32[]{:S(2)}, u32[]{:S(2)}) collective-permute-start(bf16[256,1280]{1,0:T(8,128)(2,1)S(1)} %bitcast.86), channel_id=1, source_target_pairs={{0,1},{1,0},{2,3},{3,2},{4,5},{5,4},{6,7},{7,6},{8,9},{9,8},{10,11... | collective-permute-start | bytes 1966088 | tf_op jit(solution)/shard_map/ppermute | solution.py:26
  29.8 44.4 %collective-permute-start.9 = (bf16[272,1280]{1,0:T(8,128)(2,1)}, bf16[272,1280]{1,0:T(8,128)(2,1)S(1)}, u32[]{:S(2)}, u32[]{:S(2)}) collective-permute-start(bf16[272,1280]{1,0:T(8,128)(2,1)} %fusion.19), channel_id=1, source_target_pairs={{6,8},{8,6},{7,9},{9,7},{22,24},{24,22},{23,25},{25,23},{38,40},{4... | collective-permute-start | bytes 2088968 | tf_op jit(solution)/shard_map/ppermute | solution.py:35
  31.2 8.5 %copy-start.29 = (f32[1,512]{1,0:T(1,128)}, f32[1,512]{1,0:T(1,128)S(1)}, u32[]{:S(2)}) copy-start(f32[1,512]{1,0:T(1,128)S(1)} %pad_maximum_fusion.8.live_ref) | copy-start | bytes 6148
  31.2 60.5 %collective-permute-start.13 = (f32[1,512]{1,0:T(1,128)S(1)}, f32[1,512]{1,0:T(1,128)S(1)}, u32[]{:S(2)}, u32[]{:S(2)}) collective-permute-start(f32[1,512]{1,0:T(1,128)S(1)} %pad_maximum_fusion.8.live_ref), channel_id=1, source_target_pairs={{2,0},{4,2},{6,4},{3,1},{5,3},{7,5},{10,8},{12,10},{14,12},{11,9},... | collective-permute-start | bytes 6152 | tf_op jit(solution)/shard_map/ppermute | solution.py:31
  33.6 58.3 %collective-permute-start.11 = (f32[1,512]{1,0:T(1,128)S(1)}, f32[1,512]{1,0:T(1,128)S(1)}, u32[]{:S(2)}, u32[]{:S(2)}) collective-permute-start(f32[1,512]{1,0:T(1,128)S(1)} %pad_maximum_fusion.8.live_ref), channel_id=1, source_target_pairs={{0,2},{2,4},{4,6},{1,3},{3,5},{5,7},{8,10},{10,12},{12,14},{9,11},... | collective-permute-start | bytes 6152 | tf_op jit(solution)/shard_map/ppermute | solution.py:31
  70.5 1.7 copy-start.9
  70.5 1.8 copy-start.11
  72.2 28.5 %copy-start.2 = (bf16[16,80,640]{2,1,0:T(8,128)(2,1)}, bf16[16,80,640]{2,1,0:T(8,128)(2,1)S(1)}, u32[]{:S(2)}) copy-start(bf16[16,80,640]{2,1,0:T(8,128)(2,1)S(1)} %slice.97) | copy-start | bytes 4915204
  74.4 28.2 %collective-permute-start.8 = (bf16[640,512]{1,0:T(8,128)(2,1)}, bf16[640,512]{1,0:T(8,128)(2,1)}, u32[]{:S(2)}, u32[]{:S(2)}) collective-permute-start(bf16[640,512]{1,0:T(8,128)(2,1)} %convolution_convert_fusion.1), channel_id=1, source_target_pairs={{2,0},{4,2},{6,4},{3,1},{5,3},{7,5},{10,8},{12,10},{14,12},{11,9},... | collective-permute-start | bytes 1966088 | tf_op jit(solution)/shard_map/ppermute | solution.py:31
  83.3 19.4 %collective-permute-start.7 = (bf16[640,512]{1,0:T(8,128)(2,1)}, bf16[640,512]{1,0:T(8,128)(2,1)}, u32[]{:S(2)}, u32[]{:S(2)}) collective-permute-start(bf16[640,512]{1,0:T(8,128)(2,1)} %convolution_convert_fusion.1), channel_id=1, source_target_pairs={{0,2},{2,4},{4,6},{1,3},{3,5},{5,7},{8,10},{10,12},{12,14},{9,11},... | collective-permute-start | bytes 1966088 | tf_op jit(solution)/shard_map/ppermute | solution.py:31
  87.2 1.5 copy-start.6
  89.1 2.1 collective-permute-start.12
  91.2 3.2 %collective-permute-start.4 = (bf16[8,80,320]{2,1,0:T(8,128)(2,1)S(1)}, bf16[8,80,320]{2,1,0:T(8,128)(2,1)S(1)}, u32[]{:S(2)}, u32[]{:S(2)}) collective-permute-start(bf16[8,80,320]{2,1,0:T(8,128)(2,1)S(1)} %get-tuple-element.41), channel_id=1, source_target_pairs={{0,1},{1,0},{2,3},{3,2},{4,5},{5,4},{6,7},{7,6},{8,9},{9,8},{10,11... | collective-permute-start | bytes 1228808 | tf_op jit(solution)/shard_map/ppermute | solution.py:26
  91.7 7.4 %collective-permute-start.10 = (bf16[256,1280]{1,0:T(8,128)(2,1)}, bf16[256,1280]{1,0:T(8,128)(2,1)}, u32[]{:S(2)}, u32[]{:S(2)}) collective-permute-start(bf16[256,1280]{1,0:T(8,128)(2,1)} %fusion.10), channel_id=1, source_target_pairs={{0,1},{1,0},{2,3},{3,2},{4,5},{5,4},{6,7},{7,6},{8,9},{9,8},{10,11... | collective-permute-start | bytes 1966088 | tf_op jit(solution)/shard_map/ppermute | solution.py:26
  100.7 2.0 copy-start.13
  100.7 2.0 copy-start.15
  102.7 28.4 %copy-start.1 = (bf16[512,1280]{1,0:T(8,128)(2,1)S(1)}, bf16[512,1280]{1,0:T(8,128)(2,1)}, u32[]{:S(2)}) copy-start(bf16[512,1280]{1,0:T(8,128)(2,1)} %pad_maximum_fusion.2.cot_ref) | copy-start | bytes 3932164
  123.9 20.8 %collective-permute-start.15 = (bf16[2,320,512]{2,1,0:T(8,128)(2,1)}, bf16[2,320,512]{2,1,0:T(8,128)(2,1)}, u32[]{:S(2)}, u32[]{:S(2)}) collective-permute-start(bf16[2,320,512]{2,1,0:T(8,128)(2,1)} %get-tuple-element.21), channel_id=1, source_target_pairs={{2,0},{4,2},{6,4},{3,1},{5,3},{7,5},{10,8},{12,10},{14,12},{11,9},... | collective-permute-start | bytes 1966088 | tf_op jit(solution)/shard_map/ppermute | solution.py:31
  128.7 18.9 %collective-permute-start.16 = (bf16[2,320,512]{2,1,0:T(8,128)(2,1)}, bf16[2,320,512]{2,1,0:T(8,128)(2,1)}, u32[]{:S(2)}, u32[]{:S(2)}) collective-permute-start(bf16[2,320,512]{2,1,0:T(8,128)(2,1)} %get-tuple-element.22), channel_id=1, source_target_pairs={{0,2},{2,4},{4,6},{1,3},{3,5},{5,7},{8,10},{10,12},{12,14},{9,11},... | collective-permute-start | bytes 1966088 | tf_op jit(solution)/shard_map/ppermute | solution.py:31
  131.9 2.0 copy-start.14
  131.9 1.9 copy-start.16
  132.8 6.9 %collective-permute-start.14 = (bf16[320,512]{1,0:T(8,128)(2,1)S(1)}, bf16[320,512]{1,0:T(8,128)(2,1)S(1)}, u32[]{:S(2)}, u32[]{:S(2)}) collective-permute-start(bf16[320,512]{1,0:T(8,128)(2,1)S(1)} %copy-done.24), channel_id=1, source_target_pairs={{0,1},{1,0},{2,3},{3,2},{4,5},{5,4},{6,7},{7,6},{8,9},{9,8},{10,11... | collective-permute-start | bytes 983048 | tf_op jit(solution)/shard_map/ppermute | solution.py:26
  139.3 8.4 %copy-start.18 = (f32[2,320,512]{2,1,0:T(8,128)S(1)}, f32[2,320,512]{2,1,0:T(8,128)}, u32[]{:S(2)}) copy-start(f32[2,320,512]{2,1,0:T(8,128)} %get-tuple-element.20) | copy-start | bytes 3932164
  139.3 16.0 %collective-permute-start.19 = (bf16[2,320,512]{2,1,0:T(8,128)(2,1)}, bf16[2,320,512]{2,1,0:T(8,128)(2,1)}, u32[]{:S(2)}, u32[]{:S(2)}) collective-permute-start(bf16[2,320,512]{2,1,0:T(8,128)(2,1)} %get-tuple-element.25.own_far), channel_id=1, source_target_pairs={{0,1},{1,0},{2,3},{3,2},{4,5},{5,4},{6,7},{7,6},{8,9},{9,8},{10,11... | collective-permute-start | bytes 1966088 | tf_op jit(solution)/shard_map/ppermute | solution.py:26
  143.9 5.4 %copy-start.19 = (bf16[320,512]{1,0:T(8,128)(2,1)S(1)}, bf16[320,512]{1,0:T(8,128)(2,1)}, u32[]{:S(2)}) copy-start(bf16[320,512]{1,0:T(8,128)(2,1)} %get-tuple-element.24.own_q) | copy-start | bytes 983044
  143.9 5.9 %copy-start.10 = (bf16[256,1280]{1,0:T(8,128)(2,1)S(1)}, bf16[256,1280]{1,0:T(8,128)(2,1)}, u32[]{:S(2)}) copy-start(bf16[256,1280]{1,0:T(8,128)(2,1)} %get-tuple-element.39) | copy-start | bytes 1966084
  143.9 5.9 %copy-start.12 = (bf16[256,1280]{1,0:T(8,128)(2,1)S(1)}, bf16[256,1280]{1,0:T(8,128)(2,1)}, u32[]{:S(2)}) copy-start(bf16[256,1280]{1,0:T(8,128)(2,1)} %get-tuple-element.40) | copy-start | bytes 1966084
  149.2 1.9 copy-start.4
  149.2 6.1 %collective-permute-start.18 = (bf16[2,320,512]{2,1,0:T(8,128)(2,1)S(1)}, bf16[2,320,512]{2,1,0:T(8,128)(2,1)S(1)}, u32[]{:S(2)}, u32[]{:S(2)}) collective-permute-start(bf16[2,320,512]{2,1,0:T(8,128)(2,1)S(1)} %add_convert_fusion.1.own_kv), channel_id=1, source_target_pairs={{0,1},{1,0},{2,3},{3,2},{4,5},{5,4},{6,7},{7,6},{8,9},{9,8},{10,11... | collective-permute-start | bytes 1966088 | tf_op jit(solution)/shard_map/ppermute | solution.py:26
  149.3 6.0 %collective-permute-start.17 = (bf16[320,512]{1,0:T(8,128)(2,1)S(1)}, bf16[320,512]{1,0:T(8,128)(2,1)S(1)}, u32[]{:S(2)}, u32[]{:S(2)}) collective-permute-start(bf16[320,512]{1,0:T(8,128)(2,1)S(1)} %copy-done.19), channel_id=1, source_target_pairs={{0,1},{1,0},{2,3},{3,2},{4,5},{5,4},{6,7},{7,6},{8,9},{9,8},{10,11... | collective-permute-start | bytes 983048 | tf_op jit(solution)/shard_map/ppermute | solution.py:26
  163.1 10.0 %copy-start.7 = (bf16[16,80,320]{2,1,0:T(8,128)(2,1)S(1)}, bf16[16,80,320]{2,1,0:T(8,128)(2,1)}, u32[]{:S(2)}) copy-start(bf16[16,80,320]{2,1,0:T(8,128)(2,1)} %copy-done.6) | copy-start | bytes 2457604
  163.1 10.0 %copy-start.20 = (bf16[320,512]{1,0:T(8,128)(2,1)S(1)}, bf16[320,512]{1,0:T(8,128)(2,1)}, u32[]{:S(2)}) copy-start(bf16[320,512]{1,0:T(8,128)(2,1)} %get-tuple-element.24.own_q) | copy-start | bytes 983044
  163.1 63.0 %all-to-all-start.1 = ((bf16[16,840,128]{2,1,0:T(8,128)(2,1)}), bf16[16,840,128]{2,1,0:T(8,128)(2,1)}, u32[]{:S(2)}, u32[]{:S(2)}) async-start(bf16[16,840,128]{2,1,0:T(8,128)(2,1)} %bitcast.73), calls=%async_computation.1 | async-start | bytes 6881280 | tf_op jit(solution)/shard_map/all_to_all | solution.py:393
  172.4 1.6 collective-permute-start.20
  174.0 1.5 copy-start.3
  176.8 2.2 collective-permute-start.21
  231.1 28.9 %all-to-all-start.2 = ((bf16[8,120,128]{2,1,0:T(8,128)(2,1)}), bf16[8,120,128]{2,1,0:T(8,128)(2,1)S(1)}, u32[]{:S(2)}, u32[]{:S(2)}) async-start(bf16[8,120,128]{2,1,0:T(8,128)(2,1)} %fusion.23), calls=%async_computation.2 | async-start | bytes 491520 | tf_op jit(solution)/shard_map/all_to_all | solution.py:412
  (8 other events, 7.2 us)

commit v4 on v3

--- a/solution.py
+++ b/solution.py
@@ -305,10 +305,13 @@
     shard = w_qkv.shape[0]
     shards = ZL * X
 
-    mine = lax.dynamic_index_in_dim(w_qkv.reshape(shard, 3, 2, half), core, 2, keepdims=False)
-    out_cols = lax.dynamic_index_in_dim(w_out.reshape(shard // 2, 2, 2 * half), core, 1, keepdims=False)
+    def chosen(array, at, size):
+        return jnp.where(core == 0, array[:, at:at + size], array[:, at + size:at + 2 * size])
+
+    queries, keys, values = (chosen(w_qkv, kind * 2 * half, half) for kind in range(3))
+    out_cols = chosen(w_out, 0, 2 * half)
     out_cols = jnp.concatenate([out_cols[:, :half], out_cols[:, half:]], axis=0)
-    payload = jnp.concatenate([mine[:, 1], mine[:, 2], out_cols, mine[:, 0]], axis=1)
+    payload = jnp.concatenate([keys, values, out_cols, queries], axis=1)
     moved = []
     for step in (1, -1, 2):
         moved.append(spread_z(payload, step))

time: 263 us -> 262 us (level)
  the two profiles are of different devices: /device:TPU:46 before, /device:TPU:33 now
where the time goes in v4:
time: 262 us; the launch traced here: 261 us
  waiting for transfers between devices  103 us (39%)
  starting transfers between devices  62.1 us (24%)
  Pallas kernels  44 us (17%)
  other arithmetic  27.8 us (11%)
  local copies, waits for them, and re-layouts  14.7 us (6%)
  matrix products  7.54 us (3%)
    all_to_all x1, waiting for transfers between devices, body(): lax.all_to_all(terms.reshape((X * Y,) + terms.shape[2:]), ('x', 'y'), 0,...  48.9 us
    all_to_all x1, waiting for transfers between devices, body(): weights = lax.all_to_all(spread, ('y', 'x'), 0, 0, tiled=True)  34.9 us
    pallas_call x1, Pallas kernels, attention(): pl.pallas_call(attention_kernel, grid=(heads,), in_specs=[SCALARS, one, o...  21.3 us
    ppermute x6, starting transfers between devices, along_y(): return lax.ppermute(value, 'y', pairs)  19.7 us
    all_to_all x1, starting transfers between devices, body(): sums = lax.all_to_all(sums, ('zl', 'zh'), 0, 0, tiled=True)  15 us
    ppermute x3, waiting for transfers between devices, spread_z(): return lax.ppermute(value, ('zl', 'zh', 'y'), pairs)  10.1 us
    ppermute x11, starting transfers between devices, swap_core(): return lax.ppermute(value, 'c', [(0, 1), (1, 0)])  9.82 us
    pallas_call x2, Pallas kernels, turn(): pl.pallas_call(turn_kernel, grid=(cols // step,), in_specs=[pl.BlockSpec(...  8.48 us
  transfers between devices with their start and end apart: 25, of which 6 were waited for; matrix products, arithmetic and copies ran while one was open for 14% of the time, Pallas kernels for 6%

profile of v4, /device:TPU:33, one launch (start us, length us, event | category | flops | bytes accessed | tf_op | source)
XLA Modules:
  0.0 260.9 jit_solution(11309778663936984268)
XLA Ops:
  0.7 0.9 slice_select_fusion.3
  1.6 1.1 slice_select_fusion
  4.3 1.3 collective-permute-start
  6.6 10.1 %collective-permute-done = bf16[80,1280]{1,0:T(8,128)(2,1)S(1)} collective-permute-done((bf16[80,1280]{1,0:T(8,128)(2,1)S(1)}, bf16[80,1280]{1,0:T(8,128)(2,1)S(1)}, u32[]{:S(2)}, u32[]{:S(2)}) %collective-permute-start) | collective-permute-done | bytes 204832 | tf_op jit(solution)/shard_map/ppermute | solution.py:47
  16.8 2.0 broadcast_in_dim.12
  18.7 6.7 %all-to-all-start = ((bf16[16,80,1280]{2,1,0:T(8,128)(2,1)}), bf16[16,80,1280]{2,1,0:T(8,128)(2,1)}, u32[]{:S(2)}, u32[]{:S(2)}) async-start(bf16[16,80,1280]{2,1,0:T(8,128)(2,1)} %broadcast_in_dim.12), calls=%async_computation | async-start | bytes 6553600 | tf_op jit(solution)/shard_map/all_to_all | solution.py:342
  26.1 1.9 collective-permute-start.3
  28.3 0.9 fusion.19
  30.7 1.3 collective-permute-start.13
  32.0 4.1 %collective-permute-start.11 = (f32[1,512]{1,0:T(1,128)S(1)}, f32[1,512]{1,0:T(1,128)S(1)}, u32[]{:S(2)}, u32[]{:S(2)}) collective-permute-start(f32[1,512]{1,0:T(1,128)S(1)} %pad_maximum_fusion.8.live_ref), channel_id=1, source_target_pairs={{0,2},{2,4},{4,6},{1,3},{3,5},{5,7},{8,10},{10,12},{12,14},{9,11},... | collective-permute-start | bytes 6152 | tf_op jit(solution)/shard_map/ppermute | solution.py:31
  36.1 2.6 broadcast_select_fusion.5
  38.8 1.2 pad_maximum_fusion.2.cot_ref
  40.0 34.9 %all-to-all-done = bf16[16,80,1280]{2,1,0:T(8,128)(2,1)} async-done(((bf16[16,80,1280]{2,1,0:T(8,128)(2,1)}), bf16[16,80,1280]{2,1,0:T(8,128)(2,1)}, u32[]{:S(2)}, u32[]{:S(2)}) %all-to-all-start) | async-done | bytes 3276832 | tf_op jit(solution)/shard_map/all_to_all | solution.py:342
  74.9 1.7 slice.114
  76.7 2.0 convolution_convert_fusion.1
  78.8 1.3 collective-permute-start.8
  80.1 6.8 %collective-permute-start.7 = (bf16[640,512]{1,0:T(8,128)(2,1)}, bf16[640,512]{1,0:T(8,128)(2,1)}, u32[]{:S(2)}, u32[]{:S(2)}) collective-permute-start(bf16[640,512]{1,0:T(8,128)(2,1)} %convolution_convert_fusion.1), channel_id=1, source_target_pairs={{0,2},{2,4},{4,6},{1,3},{3,5},{5,7},{8,10},{10,12},{12,14},{9,11},... | collective-permute-start | bytes 1966088 | tf_op jit(solution)/shard_map/ppermute | solution.py:31
  87.0 2.0 fusion.26
  89.0 1.5 convolution_convert_fusion.2.q_ref
  90.9 3.3 %collective-permute-start.12 = (f32[1,256]{1,0:T(1,128)S(1)}, f32[1,256]{1,0:T(1,128)S(1)}, u32[]{:S(2)}, u32[]{:S(2)}) collective-permute-start(f32[1,256]{1,0:T(1,128)S(1)} %slice_convert_fusion), channel_id=1, source_target_pairs={{0,1},{1,0},{2,3},{3,2},{4,5},{5,4},{6,7},{7,6},{8,9},{9,8},{10,11... | collective-permute-start | bytes 3080 | tf_op jit(solution)/shard_map/ppermute | solution.py:26
  94.2 1.1 fusion.10
  97.5 1.8 pad_maximum_fusion.bias_ref
  100.1 3.9 %out_grads.1.g_ref = bf16[320,512]{1,0:T(8,128)(2,1)} custom-call(s32[3]{0:T(128)} %pad_add_fusion.flag_ref, bf16[8,80,320]{2,1,0:T(8,128)(2,1)} %get-tuple-element.42.own_ref, bf16[8,80,320]{2,1,0:T(8,128)(2,1)} %copy-done.22, bf16[512,1280]{1,0:T(8,128)(2,1)} %pad_maximum_fusion.2.cot_ref, f32[1,512]{1,0:T(1,128)} %copy-done.29), custom_call_target="tpu_custom_call" | custom-call | tf_op jit(solution)/shard_map/out_grads/pallas_call | solution.py:178
  104.0 1.5 broadcast_select_fusion.1
  105.6 1.9 convolution_convert_fusion
  107.5 21.3 %attention.1 = (bf16[320,512]{1,0:T(8,128)(2,1)}, bf16[320,512]{1,0:T(8,128)(2,1)}, f32[2,320,512]{2,1,0:T(8,128)}, bf16[2,320,512]{2,1,0:T(8,128)(2,1)}, bf16[2...) custom-call(s32[3]{0:T(128)} %pad_add_fusion.flag_ref, bf16[320,512]{1,0:T(8,128)(2,1)} %convolution_convert_fusion.2.q_ref, ...), custom_call_target="tpu_custom_call" | custom-call | tf_op jit(solution)/shard_map/attention/pallas_call | solution.py:125
  128.8 1.3 collective-permute-start.15
  130.1 4.8 %collective-permute-start.16 = (bf16[2,320,512]{2,1,0:T(8,128)(2,1)}, bf16[2,320,512]{2,1,0:T(8,128)(2,1)}, u32[]{:S(2)}, u32[]{:S(2)}) collective-permute-start(bf16[2,320,512]{2,1,0:T(8,128)(2,1)} %get-tuple-element.22), channel_id=1, source_target_pairs={{0,2},{2,4},{4,6},{1,3},{3,5},{5,7},{8,10},{10,12},{12,14},{9,11},... | collective-permute-start | bytes 1966088 | tf_op jit(solution)/shard_map/ppermute | solution.py:31
  137.4 1.0 pad_maximum_fusion.4.cot_ref
  138.3 1.2 pad_maximum_fusion.3.in_ref
  139.5 4.2 %turn.2 = bf16[1280,512]{1,0:T(8,128)(2,1)} custom-call(bf16[512,1280]{1,0:T(8,128)(2,1)} %pad_maximum_fusion.3.in_ref), custom_call_target="tpu_custom_call" | custom-call | tf_op jit(solution)/shard_map/turn/pallas_call | solution.py:151
  144.5 3.5 %out_terms.1.extra_ref = f32[4,4,200,128]{3,2,1,0:T(8,128)} custom-call(s32[3]{0:T(128)} %pad_add_fusion.flag_ref, bf16[320,512]{1,0:T(8,128)(2,1)} %get-tuple-element.18.own_ref, bf16[320,512]{1,0:T(8,128)(2,1)} %copy-done.25, bf16[512,640]{1,0:T(8,128)(2,1)} %pad_maximum_fusion.4.cot_ref), custom_call_target="tpu_custom_call" | custom-call | tf_op jit(solution)/shard_map/out_terms/pallas_call | solution.py:210
  148.1 1.7 add_convert_fusion.1.own_kv
  149.7 1.3 collective-permute-start.18
  151.3 1.3 pad_maximum_fusion.1.in_ref
  152.6 4.2 %turn.3 = bf16[1280,512]{1,0:T(8,128)(2,1)} custom-call(bf16[512,1280]{1,0:T(8,128)(2,1)} %pad_maximum_fusion.1.in_ref), custom_call_target="tpu_custom_call" | custom-call | tf_op jit(solution)/shard_map/turn/pallas_call | solution.py:151
  157.8 6.9 %weight_terms.1 = bf16[4,4,840,128]{3,2,1,0:T(8,128)(2,1)} custom-call(s32[3]{0:T(128)} %pad_add_fusion.flag_ref, bf16[4,4,80,512]{3,2,1,0:T(8,128)(2,1)} %bitcast.69, bf16[4,4,80,512]{3,2,1,0:T(8,128)(2,1)} %bitcast.68, bf16[320,512]{1,0:T(8,128)(2,1)} %get-tuple-element.24.own_q, bf16[320,512]{1,0:T(8,128)(2,1)} %copy-done.23, ...), custom_call_target="tpu_custom_call" | custom-call | tf_op jit(solution)/shard_map/weight_terms/pallas_call | solution.py:280
  164.6 6.8 %all-to-all-start.1 = ((bf16[16,840,128]{2,1,0:T(8,128)(2,1)}), bf16[16,840,128]{2,1,0:T(8,128)(2,1)}, u32[]{:S(2)}, u32[]{:S(2)}) async-start(bf16[16,840,128]{2,1,0:T(8,128)(2,1)} %bitcast.61), calls=%async_computation.1 | async-start | bytes 6881280 | tf_op jit(solution)/shard_map/all_to_all | solution.py:396
  172.2 0.9 fusion.28
  173.4 1.1 copy-done.3
  174.5 1.2 convolution_add_fusion
  176.4 1.7 collective-permute-done.21
  180.1 48.9 %all-to-all-done.1 = bf16[16,840,128]{2,1,0:T(8,128)(2,1)} async-done(((bf16[16,840,128]{2,1,0:T(8,128)(2,1)}), bf16[16,840,128]{2,1,0:T(8,128)(2,1)}, u32[]{:S(2)}, u32[]{:S(2)}) %all-to-all-start.1) | async-done | bytes 3440672 | tf_op jit(solution)/shard_map/all_to_all | solution.py:396
  229.0 2.5 reduce_sum.81
  232.4 1.6 fusion.23
  234.1 15.0 %all-to-all-start.2 = ((bf16[8,120,128]{2,1,0:T(8,128)(2,1)}), bf16[8,120,128]{2,1,0:T(8,128)(2,1)S(1)}, u32[]{:S(2)}, u32[]{:S(2)}) async-start(bf16[8,120,128]{2,1,0:T(8,128)(2,1)} %fusion.23), calls=%async_computation.2 | async-start | bytes 491520 | tf_op jit(solution)/shard_map/all_to_all | solution.py:415
  249.1 2.8 %fusion.21 = bf16[1,256,1280]{2,1,0:T(8,128)(2,1)} fusion(f32[256]{0:T(256)} %broadcast_multiply_fusion.1, f32[256]{0:T(256)} %broadcast_multiply_fusion.2, f32[256]{0:T(256)} %copy-done.28, f32[256]{0:T(256)} %copy-done.27, f32[1280]{0:T(1024)S(1)} %copy-done.26, bf16[256,1280]{1,0:T(8,128)(2,1)} %copy-done.17, f32[2,256,1280]{2,1,0:T(8,128)S(1)} %bitcast.64, ...), kind=kLoop, calls=%fused_computation.41 | loop fusion | flops 4259840 | bytes 3941380 | tf_op jit(solution)/shard_map/broadcast_in_dim | solution.py:424
  251.9 7.7 %all-to-all-done.2 = bf16[8,120,128]{2,1,0:T(8,128)(2,1)S(1)} async-done(((bf16[8,120,128]{2,1,0:T(8,128)(2,1)}), bf16[8,120,128]{2,1,0:T(8,128)(2,1)S(1)}, u32[]{:S(2)}, u32[]{:S(2)}) %all-to-all-start.2) | async-done | bytes 245792 | tf_op jit(solution)/shard_map/all_to_all | solution.py:415
  (140 shorter events, 18.8 us)
Async XLA Ops:
  0.6 5.0 %copy-start.30 = (s32[1,256]{1,0:T(1,128)S(1)}, s32[1,256]{1,0:T(1,128)}, u32[]{:S(2)}) copy-start(s32[1,256]{1,0:T(1,128)} %param.7) | copy-start | bytes 3076
  0.6 5.7 %copy-start = (bf16[1,256,1280]{2,1,0:T(8,128)(2,1)S(1)}, bf16[1,256,1280]{2,1,0:T(8,128)(2,1)}, u32[]{:S(2)}) copy-start(bf16[1,256,1280]{2,1,0:T(8,128)(2,1)} %param.6) | copy-start | bytes 1966084
  2.9 3.6 %collective-permute-start.2 = (bf16[80,1280]{1,0:T(8,128)(2,1)S(1)}, bf16[80,1280]{1,0:T(8,128)(2,1)S(1)}, u32[]{:S(2)}, u32[]{:S(2)}) collective-permute-start(bf16[80,1280]{1,0:T(8,128)(2,1)S(1)} %concatenate.57), channel_id=1, source_target_pairs={{0,128},{8,136},{66,194},{74,202},{132,12},{140,4},{198,78},{206,7... | collective-permute-start | bytes 614408 | tf_op jit(solution)/shard_map/ppermute | solution.py:47
  3.6 3.0 %collective-permute-start.1 = (bf16[80,1280]{1,0:T(8,128)(2,1)S(1)}, bf16[80,1280]{1,0:T(8,128)(2,1)S(1)}, u32[]{:S(2)}, u32[]{:S(2)}) collective-permute-start(bf16[80,1280]{1,0:T(8,128)(2,1)S(1)} %concatenate.57), channel_id=1, source_target_pairs={{0,200},{8,192},{66,2},{74,10},{132,68},{140,76},{198,134},{206,14... | collective-permute-start | bytes 614408 | tf_op jit(solution)/shard_map/ppermute | solution.py:47
  4.3 12.4 %collective-permute-start = (bf16[80,1280]{1,0:T(8,128)(2,1)S(1)}, bf16[80,1280]{1,0:T(8,128)(2,1)S(1)}, u32[]{:S(2)}, u32[]{:S(2)}) collective-permute-start(bf16[80,1280]{1,0:T(8,128)(2,1)S(1)} %concatenate.57), channel_id=1, source_target_pairs={{0,64},{8,72},{66,130},{74,138},{132,196},{140,204},{198,14},{206,... | collective-permute-start | bytes 614408 | tf_op jit(solution)/shard_map/ppermute | solution.py:47
  5.6 25.0 %collective-permute-start.6 = (f32[1,256]{1,0:T(1,128)S(1)}, f32[1,256]{1,0:T(1,128)S(1)}, u32[]{:S(2)}, u32[]{:S(2)}) collective-permute-start(f32[1,256]{1,0:T(1,128)S(1)} %get-tuple-element.57), channel_id=1, source_target_pairs={{0,1},{1,0},{2,3},{3,2},{4,5},{5,4},{6,7},{7,6},{8,9},{9,8},{10,11... | collective-permute-start | bytes 3080 | tf_op jit(solution)/shard_map/ppermute | solution.py:26
  6.6 171.6 %copy-start.27 = (f32[256]{0:T(256)}, f32[256]{0:T(256)S(1)}, u32[]{:S(2)}) copy-start(f32[256]{0:T(256)S(1)} %broadcast_multiply_fusion.4) | copy-start | bytes 3076
  18.7 7.0 %copy-start.26 = (f32[1280]{0:T(1024)S(1)}, f32[1280]{0:T(1024)}, u32[]{:S(2)}) copy-start(f32[1280]{0:T(1024)} %param.8) | copy-start | bytes 15364
  18.7 56.2 %all-to-all-start = ((bf16[16,80,1280]{2,1,0:T(8,128)(2,1)}), bf16[16,80,1280]{2,1,0:T(8,128)(2,1)}, u32[]{:S(2)}, u32[]{:S(2)}) async-start(bf16[16,80,1280]{2,1,0:T(8,128)(2,1)} %broadcast_in_dim.12), calls=%async_computation | async-start | bytes 6553600 | tf_op jit(solution)/shard_map/all_to_all | solution.py:342
  25.4 2.5 copy-start.8
  25.8 152.4 %copy-start.28 = (f32[256]{0:T(256)}, f32[256]{0:T(256)S(1)}, u32[]{:S(2)}) copy-start(f32[256]{0:T(256)S(1)} %add_rsqrt_fusion.1) | copy-start | bytes 3076
  26.1 10.0 %collective-permute-start.3 = (bf16[256,1280]{1,0:T(8,128)(2,1)S(1)}, bf16[256,1280]{1,0:T(8,128)(2,1)}, u32[]{:S(2)}, u32[]{:S(2)}) collective-permute-start(bf16[256,1280]{1,0:T(8,128)(2,1)S(1)} %fusion.11), channel_id=1, source_target_pairs={{0,1},{1,0},{2,3},{3,2},{4,5},{5,4},{6,7},{7,6},{8,9},{9,8},{10,11... | collective-permute-start | bytes 1966088 | tf_op jit(solution)/shard_map/ppermute | solution.py:26
  28.0 10.8 %collective-permute-start.5 = (bf16[256,1280]{1,0:T(8,128)(2,1)S(1)}, bf16[256,1280]{1,0:T(8,128)(2,1)S(1)}, u32[]{:S(2)}, u32[]{:S(2)}) collective-permute-start(bf16[256,1280]{1,0:T(8,128)(2,1)S(1)} %bitcast.74), channel_id=1, source_target_pairs={{0,1},{1,0},{2,3},{3,2},{4,5},{5,4},{6,7},{7,6},{8,9},{9,8},{10,11... | collective-permute-start | bytes 1966088 | tf_op jit(solution)/shard_map/ppermute | solution.py:26
  29.2 49.4 %collective-permute-start.9 = (bf16[272,1280]{1,0:T(8,128)(2,1)}, bf16[272,1280]{1,0:T(8,128)(2,1)S(1)}, u32[]{:S(2)}, u32[]{:S(2)}) collective-permute-start(bf16[272,1280]{1,0:T(8,128)(2,1)} %fusion.19), channel_id=1, source_target_pairs={{6,8},{8,6},{7,9},{9,7},{22,24},{24,22},{23,25},{25,23},{38,40},{4... | collective-permute-start | bytes 2088968 | tf_op jit(solution)/shard_map/ppermute | solution.py:35
  30.6 8.1 %copy-start.29 = (f32[1,512]{1,0:T(1,128)}, f32[1,512]{1,0:T(1,128)S(1)}, u32[]{:S(2)}) copy-start(f32[1,512]{1,0:T(1,128)S(1)} %pad_maximum_fusion.8.live_ref) | copy-start | bytes 6148
  30.7 65.5 %collective-permute-start.13 = (f32[1,512]{1,0:T(1,128)S(1)}, f32[1,512]{1,0:T(1,128)S(1)}, u32[]{:S(2)}, u32[]{:S(2)}) collective-permute-start(f32[1,512]{1,0:T(1,128)S(1)} %pad_maximum_fusion.8.live_ref), channel_id=1, source_target_pairs={{2,0},{4,2},{6,4},{3,1},{5,3},{7,5},{10,8},{12,10},{14,12},{11,9},... | collective-permute-start | bytes 6152 | tf_op jit(solution)/shard_map/ppermute | solution.py:31
  32.0 64.9 %collective-permute-start.11 = (f32[1,512]{1,0:T(1,128)S(1)}, f32[1,512]{1,0:T(1,128)S(1)}, u32[]{:S(2)}, u32[]{:S(2)}) collective-permute-start(f32[1,512]{1,0:T(1,128)S(1)} %pad_maximum_fusion.8.live_ref), channel_id=1, source_target_pairs={{0,2},{2,4},{4,6},{1,3},{3,5},{5,7},{8,10},{10,12},{12,14},{9,11},... | collective-permute-start | bytes 6152 | tf_op jit(solution)/shard_map/ppermute | solution.py:31
  74.9 1.7 copy-start.9
  74.9 1.8 copy-start.11
  76.6 29.0 %copy-start.2 = (bf16[16,80,640]{2,1,0:T(8,128)(2,1)}, bf16[16,80,640]{2,1,0:T(8,128)(2,1)S(1)}, u32[]{:S(2)}) copy-start(bf16[16,80,640]{2,1,0:T(8,128)(2,1)S(1)} %slice.114) | copy-start | bytes 4915204
  78.8 28.7 %collective-permute-start.8 = (bf16[640,512]{1,0:T(8,128)(2,1)}, bf16[640,512]{1,0:T(8,128)(2,1)}, u32[]{:S(2)}, u32[]{:S(2)}) collective-permute-start(bf16[640,512]{1,0:T(8,128)(2,1)} %convolution_convert_fusion.1), channel_id=1, source_target_pairs={{2,0},{4,2},{6,4},{3,1},{5,3},{7,5},{10,8},{12,10},{14,12},{11,9},... | collective-permute-start | bytes 1966088 | tf_op jit(solution)/shard_map/ppermute | solution.py:31
  80.1 27.4 %collective-permute-start.7 = (bf16[640,512]{1,0:T(8,128)(2,1)}, bf16[640,512]{1,0:T(8,128)(2,1)}, u32[]{:S(2)}, u32[]{:S(2)}) collective-permute-start(bf16[640,512]{1,0:T(8,128)(2,1)} %convolution_convert_fusion.1), channel_id=1, source_target_pairs={{0,2},{2,4},{4,6},{1,3},{3,5},{5,7},{8,10},{10,12},{12,14},{9,11},... | collective-permute-start | bytes 1966088 | tf_op jit(solution)/shard_map/ppermute | solution.py:31
  89.0 1.6 copy-start.6
  90.9 5.3 %collective-permute-start.12 = (f32[1,256]{1,0:T(1,128)S(1)}, f32[1,256]{1,0:T(1,128)S(1)}, u32[]{:S(2)}, u32[]{:S(2)}) collective-permute-start(f32[1,256]{1,0:T(1,128)S(1)} %slice_convert_fusion), channel_id=1, source_target_pairs={{0,1},{1,0},{2,3},{3,2},{4,5},{5,4},{6,7},{7,6},{8,9},{9,8},{10,11... | collective-permute-start | bytes 3080 | tf_op jit(solution)/shard_map/ppermute | solution.py:26
  96.2 3.1 %collective-permute-start.4 = (bf16[8,80,320]{2,1,0:T(8,128)(2,1)S(1)}, bf16[8,80,320]{2,1,0:T(8,128)(2,1)S(1)}, u32[]{:S(2)}, u32[]{:S(2)}) collective-permute-start(bf16[8,80,320]{2,1,0:T(8,128)(2,1)S(1)} %get-tuple-element.41), channel_id=1, source_target_pairs={{0,1},{1,0},{2,3},{3,2},{4,5},{5,4},{6,7},{7,6},{8,9},{9,8},{10,11... | collective-permute-start | bytes 1228808 | tf_op jit(solution)/shard_map/ppermute | solution.py:26
  96.2 7.8 %collective-permute-start.10 = (bf16[256,1280]{1,0:T(8,128)(2,1)}, bf16[256,1280]{1,0:T(8,128)(2,1)}, u32[]{:S(2)}, u32[]{:S(2)}) collective-permute-start(bf16[256,1280]{1,0:T(8,128)(2,1)} %fusion.10), channel_id=1, source_target_pairs={{0,1},{1,0},{2,3},{3,2},{4,5},{5,4},{6,7},{7,6},{8,9},{9,8},{10,11... | collective-permute-start | bytes 1966088 | tf_op jit(solution)/shard_map/ppermute | solution.py:26
  105.5 2.0 copy-start.13
  105.5 2.0 copy-start.15
  107.5 27.4 %copy-start.1 = (bf16[512,1280]{1,0:T(8,128)(2,1)S(1)}, bf16[512,1280]{1,0:T(8,128)(2,1)}, u32[]{:S(2)}) copy-start(bf16[512,1280]{1,0:T(8,128)(2,1)} %pad_maximum_fusion.2.cot_ref) | copy-start | bytes 3932164
  128.8 19.2 %collective-permute-start.15 = (bf16[2,320,512]{2,1,0:T(8,128)(2,1)}, bf16[2,320,512]{2,1,0:T(8,128)(2,1)}, u32[]{:S(2)}, u32[]{:S(2)}) collective-permute-start(bf16[2,320,512]{2,1,0:T(8,128)(2,1)} %get-tuple-element.21), channel_id=1, source_target_pairs={{2,0},{4,2},{6,4},{3,1},{5,3},{7,5},{10,8},{12,10},{14,12},{11,9},... | collective-permute-start | bytes 1966088 | tf_op jit(solution)/shard_map/ppermute | solution.py:31
  130.1 18.0 %collective-permute-start.16 = (bf16[2,320,512]{2,1,0:T(8,128)(2,1)}, bf16[2,320,512]{2,1,0:T(8,128)(2,1)}, u32[]{:S(2)}, u32[]{:S(2)}) collective-permute-start(bf16[2,320,512]{2,1,0:T(8,128)(2,1)} %get-tuple-element.22), channel_id=1, source_target_pairs={{0,2},{2,4},{4,6},{1,3},{3,5},{5,7},{8,10},{10,12},{12,14},{9,11},... | collective-permute-start | bytes 1966088 | tf_op jit(solution)/shard_map/ppermute | solution.py:31
  135.8 2.6 copy-start.14
  135.8 2.6 copy-start.16
  136.7 7.1 %collective-permute-start.14 = (bf16[320,512]{1,0:T(8,128)(2,1)S(1)}, bf16[320,512]{1,0:T(8,128)(2,1)S(1)}, u32[]{:S(2)}, u32[]{:S(2)}) collective-permute-start(bf16[320,512]{1,0:T(8,128)(2,1)S(1)} %copy-done.24), channel_id=1, source_target_pairs={{0,1},{1,0},{2,3},{3,2},{4,5},{5,4},{6,7},{7,6},{8,9},{9,8},{10,11... | collective-permute-start | bytes 983048 | tf_op jit(solution)/shard_map/ppermute | solution.py:26
  143.7 4.3 %copy-start.18 = (f32[2,320,512]{2,1,0:T(8,128)S(1)}, f32[2,320,512]{2,1,0:T(8,128)}, u32[]{:S(2)}) copy-start(f32[2,320,512]{2,1,0:T(8,128)} %get-tuple-element.20) | copy-start | bytes 3932164
  143.7 13.1 %collective-permute-start.19 = (bf16[2,320,512]{2,1,0:T(8,128)(2,1)}, bf16[2,320,512]{2,1,0:T(8,128)(2,1)}, u32[]{:S(2)}, u32[]{:S(2)}) collective-permute-start(bf16[2,320,512]{2,1,0:T(8,128)(2,1)} %get-tuple-element.25.own_far), channel_id=1, source_target_pairs={{0,1},{1,0},{2,3},{3,2},{4,5},{5,4},{6,7},{7,6},{8,9},{9,8},{10,11... | collective-permute-start | bytes 1966088 | tf_op jit(solution)/shard_map/ppermute | solution.py:26
  148.0 3.0 %copy-start.19 = (bf16[320,512]{1,0:T(8,128)(2,1)S(1)}, bf16[320,512]{1,0:T(8,128)(2,1)}, u32[]{:S(2)}) copy-start(bf16[320,512]{1,0:T(8,128)(2,1)} %get-tuple-element.24.own_q) | copy-start | bytes 983044
  148.0 3.3 %copy-start.10 = (bf16[256,1280]{1,0:T(8,128)(2,1)S(1)}, bf16[256,1280]{1,0:T(8,128)(2,1)}, u32[]{:S(2)}) copy-start(bf16[256,1280]{1,0:T(8,128)(2,1)} %get-tuple-element.39) | copy-start | bytes 1966084
  148.0 3.3 %copy-start.12 = (bf16[256,1280]{1,0:T(8,128)(2,1)S(1)}, bf16[256,1280]{1,0:T(8,128)(2,1)}, u32[]{:S(2)}) copy-start(bf16[256,1280]{1,0:T(8,128)(2,1)} %get-tuple-element.40) | copy-start | bytes 1966084
  149.7 2.9 %copy-start.4 = (bf16[2,320,512]{2,1,0:T(8,128)(2,1)}, bf16[2,320,512]{2,1,0:T(8,128)(2,1)S(1)}, u32[]{:S(2)}) copy-start(bf16[2,320,512]{2,1,0:T(8,128)(2,1)S(1)} %add_convert_fusion.1.own_kv) | copy-start | bytes 1966084
  149.7 7.1 %collective-permute-start.18 = (bf16[2,320,512]{2,1,0:T(8,128)(2,1)S(1)}, bf16[2,320,512]{2,1,0:T(8,128)(2,1)S(1)}, u32[]{:S(2)}, u32[]{:S(2)}) collective-permute-start(bf16[2,320,512]{2,1,0:T(8,128)(2,1)S(1)} %add_convert_fusion.1.own_kv), channel_id=1, source_target_pairs={{0,1},{1,0},{2,3},{3,2},{4,5},{5,4},{6,7},{7,6},{8,9},{9,8},{10,11... | collective-permute-start | bytes 1966088 | tf_op jit(solution)/shard_map/ppermute | solution.py:26
  151.0 5.8 %collective-permute-start.17 = (bf16[320,512]{1,0:T(8,128)(2,1)S(1)}, bf16[320,512]{1,0:T(8,128)(2,1)S(1)}, u32[]{:S(2)}, u32[]{:S(2)}) collective-permute-start(bf16[320,512]{1,0:T(8,128)(2,1)S(1)} %copy-done.19), channel_id=1, source_target_pairs={{0,1},{1,0},{2,3},{3,2},{4,5},{5,4},{6,7},{7,6},{8,9},{9,8},{10,11... | collective-permute-start | bytes 983048 | tf_op jit(solution)/shard_map/ppermute | solution.py:26
  164.6 7.5 %copy-start.7 = (bf16[16,80,320]{2,1,0:T(8,128)(2,1)S(1)}, bf16[16,80,320]{2,1,0:T(8,128)(2,1)}, u32[]{:S(2)}) copy-start(bf16[16,80,320]{2,1,0:T(8,128)(2,1)} %copy-done.6) | copy-start | bytes 2457604
  164.6 7.5 %copy-start.20 = (bf16[320,512]{1,0:T(8,128)(2,1)S(1)}, bf16[320,512]{1,0:T(8,128)(2,1)}, u32[]{:S(2)}) copy-start(bf16[320,512]{1,0:T(8,128)(2,1)} %get-tuple-element.24.own_q) | copy-start | bytes 983044
  164.6 64.4 %all-to-all-start.1 = ((bf16[16,840,128]{2,1,0:T(8,128)(2,1)}), bf16[16,840,128]{2,1,0:T(8,128)(2,1)}, u32[]{:S(2)}, u32[]{:S(2)}) async-start(bf16[16,840,128]{2,1,0:T(8,128)(2,1)} %bitcast.61), calls=%async_computation.1 | async-start | bytes 6881280 | tf_op jit(solution)/shard_map/all_to_all | solution.py:396
  171.4 1.6 collective-permute-start.20
  175.9 2.3 collective-permute-start.21
  234.1 25.5 %all-to-all-start.2 = ((bf16[8,120,128]{2,1,0:T(8,128)(2,1)}), bf16[8,120,128]{2,1,0:T(8,128)(2,1)S(1)}, u32[]{:S(2)}, u32[]{:S(2)}) async-start(bf16[8,120,128]{2,1,0:T(8,128)(2,1)} %fusion.23), calls=%async_computation.2 | async-start | bytes 491520 | tf_op jit(solution)/shard_map/all_to_all | solution.py:415
  (8 other events, 7.5 us)
